TPU v7x, 32 devices: a whole 2x2x4 slice. The times are simulated.
32 devices in a mesh: blk: 16 (over z, x, core), feat: 2 (over y).
Axes of the slice: x: 2, y: 2, z: 4, core: 2. Of those that a mesh axis runs over, the one named last changes fastest.
Arguments:
- inputs: bfloat16 [4096, 1024], P('blk'), may hold values from -6 to 6
- col_mask: int32 [2, 1024], replicated, may hold values 0 or 1
- row_mask: int32 [4096], P('blk'), may hold values from 0 to 1
- width_class: int32 [4096], P('blk'), may hold values from 0 to 1
- frequencies: bfloat16 [2048, 2048], P(None, 'feat'), may hold values from -0.375 to 0.375
- phases: float32 [2048], P('feat'), may hold values from -3.140625 to 3.140625
- targets: float32 [4096], P('blk'), may hold values from -6 to 6
- prior_draws: float32 [4096, 16], P('blk'), may hold values from -6 to 6
- hidden_weight: float32 [1024, 2048], P('blk', 'feat'), may hold values from -0.1875 to 0.1875
- hidden_moment: float32 [1024, 2048], P('blk', 'feat'), may hold values from -9.536743e-06 to 9.536743e-06
- hidden_second: float32 [1024, 2048], P('blk', 'feat'), may hold values from 4.2e-14 to 1.7e-13
- alpha_weight: float32 [4096, 16], P('blk'), may hold values from -1.5 to 1.5
- alpha_moment: float32 [4096, 16], P('blk'), may hold values from -2.2888184e-05 to 2.2888184e-05
- alpha_second: float32 [4096, 16], P('blk'), may hold values from 1.7578125e-13 to 7.080078e-13
Outputs:
- norm_before: float32 [], replicated
- resid_norm: float32 [], replicated
- hidden_out: float32 [1024, 2048], P('blk', 'feat')
- hidden_moment_out: float32 [1024, 2048], P('blk', 'feat')
- hidden_second_out: float32 [1024, 2048], P('blk', 'feat')
- hidden_copy: bfloat16 [1024, 2048], P('blk', 'feat')
- alpha_out: float32 [4096, 16], P('blk')
- alpha_moment_out: float32 [4096, 16], P('blk')
- alpha_second_out: float32 [4096, 16], P('blk')
- alpha_copy: bfloat16 [4096, 16], P('blk')
All inputs are finite; a program needn't handle non-finite values.
Results may differ from a plain program's by a relative error of at most 0.0034.
Values may be sent and summed in bfloat16 or wider, within the bound.
No kernel may reach another device: no remote copies, remote signals or barrier semaphores. Data moves between devices by JAX's collectives and lax.ppermute only.
A program may use at most 192 MiB of HBM per device.

v0:
```python
import jax
import jax.numpy as jnp
from jax import lax
from jax.sharding import PartitionSpec as P

F = 2048
S = 16
ADAM_STEP = 10


PRECISE = lax.Precision.HIGHEST
NOISE = 0.01
CLIP_AT = 0.01
BETA_ONE = 0.9
BETA_TWO = 0.999
ADAM_EPS = 1e-08
DECAY = 0.01


def adamw_update(weight, moment, second, gradient, step_rate):
    moment = BETA_ONE * moment + (1.0 - BETA_ONE) * gradient
    second = BETA_TWO * second + (1.0 - BETA_TWO) * gradient * gradient
    moment_hat = moment / (1.0 - BETA_ONE**ADAM_STEP)
    second_hat = second / (1.0 - BETA_TWO**ADAM_STEP)
    weight = weight - step_rate * (moment_hat / (jnp.sqrt(second_hat) + ADAM_EPS) + DECAY * weight)
    return (weight, moment, second)


def kernel_step(features, pieces):
    kernel = jnp.einsum("tf,pf->tp", features, pieces[0], preferred_element_type=jnp.float32)
    fitted = jnp.dot(kernel, pieces[1].astype(jnp.float32), precision=PRECISE)
    summed = jnp.einsum("pf,ps->fs", pieces[0], pieces[1], preferred_element_type=jnp.float32)
    return (fitted, summed)


def on_device(
    inputs,
    col_mask,
    row_mask,
    width_class,
    frequencies,
    phases,
    targets,
    prior_draws,
    hidden_weight,
    hidden_moment,
    hidden_second,
    alpha_weight,
    alpha_moment,
    alpha_second,
):
    classes = col_mask.shape[0]
    feat_scale = (2.0 / F) ** 0.5
    onehot = (width_class[:, None] == jnp.arange(classes, dtype=jnp.int32)[None, :]).astype(
        jnp.float32
    )
    keep_cols = jnp.dot(onehot, col_mask.astype(jnp.float32))
    masked = inputs * keep_cols.astype(jnp.bfloat16)
    keep_rows = row_mask.astype(jnp.float32)
    true_count = jnp.maximum(lax.psum(jnp.sum(keep_rows), "blk"), 1.0)
    columns = masked
    first_pre = jnp.dot(
        columns,
        lax.all_gather(hidden_weight.astype(jnp.bfloat16), "blk", axis=0, tiled=True),
        preferred_element_type=jnp.float32,
    )
    tanh_full = jnp.tanh(first_pre)
    hidden = tanh_full.astype(jnp.bfloat16)
    pre = jnp.dot(
        lax.all_gather(hidden, "feat", axis=1, tiled=True),
        frequencies,
        preferred_element_type=jnp.float32,
    )
    phase_arg = pre + phases[None, :]
    features = (feat_scale * jnp.cos(phase_arg)).astype(jnp.bfloat16)
    alpha_low = alpha_weight.astype(jnp.bfloat16)

    def fold_step(pieces):
        return kernel_step(features, pieces)

    fitted_part, moments = fold_step(
        (
            lax.all_gather(features, "blk", axis=0, tiled=True),
            lax.all_gather(alpha_low, "blk", axis=0, tiled=True),
        )
    )
    fitted = lax.psum(fitted_part, "feat") + NOISE * alpha_weight
    residual = fitted - targets[:, None] - prior_draws
    resid_grad = (2.0 * keep_rows[:, None] * residual / (true_count * S)).astype(jnp.bfloat16)
    pulled_part, back_moments = fold_step(
        (
            lax.all_gather(features, "blk", axis=0, tiled=True),
            lax.all_gather(resid_grad, "blk", axis=0, tiled=True),
        )
    )
    alpha_grad = lax.psum(pulled_part, "feat") + NOISE * resid_grad.astype(jnp.float32)
    feature_grad = jnp.dot(resid_grad.astype(jnp.float32), moments.T, precision=PRECISE)
    feature_grad = feature_grad + jnp.dot(
        alpha_low.astype(jnp.float32), back_moments.T, precision=PRECISE
    )
    pre_grad = (-feat_scale * jnp.sin(phase_arg) * feature_grad).astype(jnp.bfloat16)
    hidden_terms = jnp.einsum(
        "tf,hf->th", pre_grad, frequencies, preferred_element_type=jnp.float32
    )
    hidden_grad = lax.psum_scatter(hidden_terms, "feat", scatter_dimension=1, tiled=True)
    first_grad = ((1.0 - tanh_full * tanh_full) * hidden_grad).astype(jnp.bfloat16)
    columns = masked
    weight_grad = lax.psum_scatter(
        jnp.einsum("td,th->dh", columns, first_grad, preferred_element_type=jnp.float32),
        "blk",
        scatter_dimension=0,
        tiled=True,
    )
    first_feat = (lax.axis_index("feat") == 0).astype(jnp.float32)
    grad_part = jnp.sum(weight_grad * weight_grad) + first_feat * jnp.sum(alpha_grad * alpha_grad)
    resid_part = first_feat * jnp.sum(keep_rows[:, None] * residual * residual)
    grad_total, resid_total = lax.psum((grad_part, resid_part), ("blk", "feat"))
    norm_before = jnp.sqrt(grad_total)
    resid_norm = jnp.sqrt(resid_total)
    clip = jnp.minimum(1.0, CLIP_AT / (norm_before + 1e-06))
    hidden_out, moment_out, second_out = adamw_update(
        hidden_weight, hidden_moment, hidden_second, weight_grad * clip, 0.02
    )
    alpha_out, alpha_moment_out, alpha_second_out = adamw_update(
        alpha_weight, alpha_moment, alpha_second, alpha_grad * clip, 0.05
    )
    return (
        norm_before,
        resid_norm,
        hidden_out,
        moment_out,
        second_out,
        hidden_out.astype(jnp.bfloat16),
        alpha_out,
        alpha_moment_out,
        alpha_second_out,
        alpha_out.astype(jnp.bfloat16),
    )


def solution(mesh):
    in_specs = (
        P("blk", None),
        P(),
        P("blk"),
        P("blk"),
        P(None, "feat"),
        P("feat"),
        P("blk"),
        P("blk", None),
        P("blk", "feat"),
        P("blk", "feat"),
        P("blk", "feat"),
        P("blk", None),
        P("blk", None),
        P("blk", None),
    )
    out_specs = (
        P(),
        P(),
        P("blk", "feat"),
        P("blk", "feat"),
        P("blk", "feat"),
        P("blk", "feat"),
        P("blk", None),
        P("blk", None),
        P("blk", None),
        P("blk", None),
    )
    return jax.shard_map(
        on_device, mesh=mesh, in_specs=in_specs, out_specs=out_specs, check_vma=False
    )
```

profile of v0, /device:TPU:0, one launch (start us, length us, event | category | flops | bytes accessed | tf_op | source)
XLA Modules:
  0.0 378.5 jit_solution(18336091625798306020)
XLA Ops:
  7.2 0.0 copy-start.11
  7.2 0.0 all-gather.4.cloned.1.call-start
  7.2 1.6 convert_element_type.47
  8.9 0.0 all-gather.4.cloned.1.call-update
  8.9 0.0 all-gather.6.cloned.1.call-start
  8.9 1.4 fusion.3
  10.3 44.6 %all-gather.4.cloned.1.call-done = bf16[1024,1024]{1,0:T(8,128)(2,1)} async-done(((bf16[64,1024]{1,0:T(8,128)(2,1)}), bf16[1024,1024]{1,0:T(8,128)(2,1)}) %all-gather.4.cloned.1.call-update) | async-done | bytes 2097168 | tf_op jit(solution)/shard_map/all_gather | solution.py:64
  54.9 3.1 fusion.16
  58.1 0.0 all-gather.6.cloned.1.call-update
  58.1 0.0 copy-start.8
  58.1 0.0 copy-start.4
  58.1 0.0 all-gather.8.cloned.1.call-start
  58.2 20.1 %all-gather.6.cloned.1.call-done = bf16[256,2048]{1,0:T(8,128)(2,1)} async-done(((bf16[256,1024]{1,0:T(8,128)(2,1)}), bf16[256,2048]{1,0:T(8,128)(2,1)}) %all-gather.6.cloned.1.call-update) | async-done | bytes 1048592 | tf_op jit(solution)/shard_map/all_gather | solution.py:70
  78.3 0.0 copy-done.11
  78.3 7.3 %multiply_convert_fusion.1 = (bf16[256,1024]{1,0:T(8,128)(2,1)}, f32[256,1024]{1,0:T(8,128)S(1)}) fusion(f32[1024]{0:T(1024)S(1)} %copy-done.11, bf16[256,2048]{1,0:T(8,128)(2,1)} %all-gather.6.cloned.1.call-done, bf16[2048,1024]{1,0:T(8,128)(2,1)} %param.18), kind=kOutput, calls=%fused_computation.9 | convolution fusion | flops 1074528256 | bytes 6819840 | tf_op jit(solution)/shard_map/dot_general | solution.py:69
  85.6 0.0 all-gather.8.cloned.1.call-update
  85.6 0.0 reduce-scatter.3.cloned.1.call-start
  85.6 0.0 copy-done.8
  85.6 0.6 broadcast_multiply_fusion
  86.2 34.6 %psum.36 = f32[]{:T(128)} all-reduce(f32[]{:T(128)} %get-tuple-element.23), channel_id=1, replica_groups=mesh['blk'=16,'feat'=2] {'blk'}, use_global_device_ids=true, to_apply=%region_2.0 | all-reduce | flops 1 | bytes 8 | tf_op jit(solution)/shard_map/psum | solution.py:60
  121.5 18.8 %all_gather.19 = bf16[4096,16]{0,1:T(8,128)(2,1)S(1)} all-gather(bf16[256,16]{0,1:T(8,128)(2,1)S(1)} %convert_element_type.51), channel_id=1, replica_groups=mesh['blk'=16,'feat'=2] {'blk'}, dimensions={0}, use_global_device_ids=true | all-gather | bytes 139264 | tf_op jit(solution)/shard_map/all_gather | solution.py:84
  140.2 20.7 %all-gather.8.cloned.1.call-done = bf16[4096,1024]{1,0:T(8,128)(2,1)} async-done(((bf16[256,1024]{1,0:T(8,128)(2,1)}), bf16[4096,1024]{1,0:T(8,128)(2,1)}) %all-gather.8.cloned.1.call-update) | async-done | bytes 8388624 | tf_op jit(solution)/shard_map/all_gather | solution.py:83
  160.9 5.9 %fusion.17 = f32[256,4096]{1,0:T(8,128)S(1)} fusion(bf16[256,1024]{1,0:T(8,128)(2,1)} %get-tuple-element.26, bf16[4096,1024]{1,0:T(8,128)(2,1)} %all-gather.8.cloned.1.call-done), kind=kOutput, calls=%fused_computation.36 | convolution fusion | flops 2147483648 | bytes 13107200 | tf_op jit(solution)/shard_map/tf,pf->tp/dot_general | solution.py:30
  166.9 1.9 copy-done
  168.8 2.0 fusion.18
  170.8 8.3 %psum.35 = f32[256,16]{0,1:T(8,128)S(1)} all-reduce(f32[256,16]{0,1:T(8,128)S(1)} %fusion.18), channel_id=1, replica_groups=mesh['blk'=16,'feat'=2] {'feat'}, use_global_device_ids=true, to_apply=%region_0.0 | all-reduce | flops 4096 | bytes 32768 | tf_op jit(solution)/shard_map/psum | solution.py:87
  179.2 0.6 fusion.8
  179.8 19.3 %all_gather.20 = bf16[4096,16]{0,1:T(8,128)(2,1)S(1)} all-gather(bf16[256,16]{0,1:T(8,128)(2,1)S(1)} %divide_convert_fusion), channel_id=1, replica_groups=mesh['blk'=16,'feat'=2] {'blk'}, dimensions={0}, use_global_device_ids=true | all-gather | bytes 139264 | tf_op jit(solution)/shard_map/all_gather | solution.py:93
  199.1 5.8 %fusion.19 = f32[1024,16]{1,0:T(8,128)S(1)} fusion(bf16[4096,1024]{1,0:T(8,128)(2,1)} %all-gather.8.cloned.1.call-done, bf16[4096,16]{0,1:T(8,128)(2,1)S(1)} %all_gather.19), kind=kOutput, calls=%fused_computation.38 | convolution fusion | flops 134217728 | bytes 8585216 | tf_op jit(solution)/shard_map/pf,ps->fs/dot_general | solution.py:32
  204.8 0.6 fusion.20
  205.5 0.0 copy-start.10
  205.5 5.9 %fusion.21 = f32[1024,16]{1,0:T(8,128)S(1)} fusion(bf16[4096,1024]{1,0:T(8,128)(2,1)} %all-gather.8.cloned.1.call-done, bf16[4096,16]{0,1:T(8,128)(2,1)S(1)} %all_gather.20), kind=kOutput, calls=%fused_computation.40 | convolution fusion | flops 134217728 | bytes 8585216 | tf_op jit(solution)/shard_map/pf,ps->fs/dot_general | solution.py:32
  211.4 4.3 %fusion.2 = bf16[256,1024]{1,0:T(8,128)(2,1)S(1)} fusion(f32[256,1024]{1,0:T(8,128)S(1)} %fusion.20, f32[1024,16]{1,0:T(8,128)S(1)} %fusion.21, bf16[256,16]{0,1:T(8,128)(2,1)S(1)} %convert_element_type.51, f32[256,1024]{1,0:T(8,128)S(1)} %get-tuple-element.27), kind=kOutput, calls=%fused_computation.5 | convolution fusion | flops 51380224 | bytes 2695168 | tf_op jit(solution)/shard_map/dot_general | solution.py:98
  215.7 2.6 fusion.22
  218.3 0.0 reduce-scatter.3.cloned.1.call-update
  218.3 0.0 reduce-scatter.5.cloned.1.call-start
  218.4 28.4 %reduce-scatter.3.cloned.1.call-done = f32[256,1024]{1,0:T(8,128)} async-done(((f32[256,2048]{1,0:T(8,128)}), f32[256,1024]{1,0:T(8,128)}) %reduce-scatter.3.cloned.1.call-update) | async-done | bytes 1048592 | tf_op jit(solution)/shard_map/reduce_scatter | solution.py:105
  246.8 3.9 %fusion.4 = f32[1024,1024]{1,0:T(8,128)} fusion(bf16[256,1024]{1,0:T(8,128)(2,1)S(1)} %fusion.3, f32[256,1024]{1,0:T(8,128)} %reduce-scatter.3.cloned.1.call-done, f32[256,1024]{1,0:T(8,128)S(1)} %get-tuple-element.25), kind=kOutput, calls=%fused_computation.10 | convolution fusion | flops 537919488 | bytes 6815744 | tf_op jit(solution)/shard_map/td,th->dh/dot_general | solution.py:109
  250.8 0.0 copy-start.3
  250.8 0.0 reduce-scatter.5.cloned.1.call-update
  251.5 4.2 %fusion.23 = f32[256,16]{0,1:T(8,128)S(1)} fusion(f32[256,4096]{1,0:T(8,128)} %copy-done, bf16[4096,16]{0,1:T(8,128)(2,1)S(1)} %all_gather.20), kind=kOutput, calls=%fused_computation.42 | convolution fusion | flops 201326592 | bytes 4341760 | tf_op jit(solution)/shard_map/dot_general | solution.py:31
  255.7 7.0 %psum.37 = f32[256,16]{0,1:T(8,128)S(1)} all-reduce(f32[256,16]{0,1:T(8,128)S(1)} %fusion.23), channel_id=1, replica_groups=mesh['blk'=16,'feat'=2] {'feat'}, use_global_device_ids=true, to_apply=%region_6.0 | all-reduce | flops 4096 | bytes 32768 | tf_op jit(solution)/shard_map/psum | solution.py:96
  262.7 0.6 multiply_reduce_fusion.1
  264.0 59.8 %reduce-scatter.5.cloned.1.call-done = f32[64,1024]{1,0:T(8,128)} async-done(((f32[1024,1024]{1,0:T(8,128)}), f32[64,1024]{1,0:T(8,128)}) %reduce-scatter.5.cloned.1.call-update) | async-done | bytes 262160 | tf_op jit(solution)/shard_map/reduce_scatter | solution.py:108
  323.7 1.6 multiply_reduce_fusion
  326.0 39.6 %all-reduce = (f32[]{:T(128)}, f32[]{:T(128)}) all-reduce(f32[]{:T(128)S(6)} %add.72, f32[]{:T(128)S(6)} %mul.177), channel_id=1, replica_groups=mesh['blk'=16,'feat'=2] {'blk','feat'}, use_global_device_ids=true, to_apply=%region_8.0 | all-reduce | flops 2 | bytes 16 | tf_op jit(solution)/shard_map/psum | solution.py:117
  367.0 0.6 fusion.12
  367.7 2.0 fusion.14
  (19 shorter events, 0.0 us)
Async XLA Ops:
  7.2 71.1 %copy-start.11 = (f32[1024]{0:T(1024)S(1)}, f32[1024]{0:T(1024)}, u32[]{:S(2)}) copy-start(f32[1024]{0:T(1024)} %param.19) | copy-start | bytes 12292
  7.2 47.8 %all-gather.4.cloned.1.call-start = ((), (), s32[]{:S(2)}) async-start(), calls=%async_computation.2 | async-start | bytes 2228224 | tf_op jit(solution)/shard_map/all_gather | solution.py:64
  8.9 69.4 %all-gather.6.cloned.1.call-start = ((), (), s32[]{:S(2)}) async-start(), calls=%async_computation.3 | async-start | bytes 1572864 | tf_op jit(solution)/shard_map/all_gather | solution.py:70
  58.1 27.5 %copy-start.8 = (s32[256]{0:T(256)S(1)}, s32[256]{0:T(256)}, u32[]{:S(2)}) copy-start(s32[256]{0:T(256)} %param.16) | copy-start | bytes 3076
  58.1 62.7 %copy-start.4 = (f32[256,16]{0,1:T(8,128)S(1)}, f32[256,16]{0,1:T(8,128)}, u32[]{:S(2)}) copy-start(f32[256,16]{0,1:T(8,128)} %param.25) | copy-start | bytes 49156
  58.1 102.8 %all-gather.8.cloned.1.call-start = ((), (), s32[]{:S(2)}) async-start(), calls=%async_computation.4 | async-start | bytes 8912896 | tf_op jit(solution)/shard_map/all_gather | solution.py:83
  85.6 161.2 %reduce-scatter.3.cloned.1.call-start = ((), (), s32[]{:S(2)}) async-start(), calls=%async_computation.5 | async-start | bytes 3145728 | tf_op jit(solution)/shard_map/reduce_scatter | solution.py:105
  166.9 1.9 copy-start
  168.8 10.3 %copy-start.7 = (f32[256,16]{0,1:T(8,128)S(1)}, f32[256,16]{0,1:T(8,128)}, u32[]{:S(2)}) copy-start(f32[256,16]{0,1:T(8,128)} %param.21) | copy-start | bytes 49156
  168.8 10.3 %copy-start.9 = (f32[256]{0:T(256)S(1)}, f32[256]{0:T(256)}, u32[]{:S(2)}) copy-start(f32[256]{0:T(256)} %param.20) | copy-start | bytes 3076
  205.5 10.2 %copy-start.10 = (bf16[2048,1024]{1,0:T(8,128)(2,1)S(1)}, bf16[2048,1024]{1,0:T(8,128)(2,1)}, u32[]{:S(2)}) copy-start(bf16[2048,1024]{1,0:T(8,128)(2,1)} %param.18) | copy-start | bytes 12582916
  218.3 105.4 %reduce-scatter.5.cloned.1.call-start = ((), (), s32[]{:S(2)}) async-start(), calls=%async_computation.6 | async-start | bytes 4456448 | tf_op jit(solution)/shard_map/reduce_scatter | solution.py:108
  250.8 116.3 %copy-start.5 = (f32[256,16]{0,1:T(8,128)S(1)}, f32[256,16]{0,1:T(8,128)}, u32[]{:S(2)}) copy-start(f32[256,16]{0,1:T(8,128)} %param.26) | copy-start | bytes 49156
  250.8 116.3 %copy-start.6 = (f32[256,16]{0,1:T(8,128)S(1)}, f32[256,16]{0,1:T(8,128)}, u32[]{:S(2)}) copy-start(f32[256,16]{0,1:T(8,128)} %param.27) | copy-start | bytes 49156
  250.8 116.9 %copy-start.1 = (f32[64,1024]{1,0:T(8,128)S(1)}, f32[64,1024]{1,0:T(8,128)}, u32[]{:S(2)}) copy-start(f32[64,1024]{1,0:T(8,128)} %param.22) | copy-start | bytes 786436
  250.8 116.9 %copy-start.2 = (f32[64,1024]{1,0:T(8,128)S(1)}, f32[64,1024]{1,0:T(8,128)}, u32[]{:S(2)}) copy-start(f32[64,1024]{1,0:T(8,128)} %param.23) | copy-start | bytes 786436
  250.8 116.9 %copy-start.3 = (f32[64,1024]{1,0:T(8,128)S(1)}, f32[64,1024]{1,0:T(8,128)}, u32[]{:S(2)}) copy-start(f32[64,1024]{1,0:T(8,128)} %param.24) | copy-start | bytes 786436
Sparse Core Ops, SparseCore 0:
  10.7 44.1 all-gather.3
  58.2 19.9 all-gather.5
  85.7 75.1 all-gather.7
  218.4 28.3 reduce-scatter.2
  250.9 72.7 reduce-scatter.4
where the time goes:
time: 379 us; the launch traced here: 378 us
  waiting for transfers between devices  174 us (46%)
  blocking collectives  128 us (34%)
  matrix products  47.1 us (12%)
  between operations  20.3 us (5%)
  other arithmetic  7.74 us (2%)
    reduce_scatter x1, waiting for transfers between devices, on_device(): lax.psum_scatter(jnp.einsum('td,th->dh', columns, first_grad, preferred_e...  59.8 us
    all_gather x1, waiting for transfers between devices, on_device(): lax.all_gather(hidden_weight.astype(jnp.bfloat16), 'blk', axis=0, tiled=T...  44.6 us
    psum x1, blocking collectives, on_device(): grad_total, resid_total = lax.psum((grad_part, resid_part), ('blk', 'feat'))  39.6 us
    psum x1, blocking collectives, on_device(): true_count = jnp.maximum(lax.psum(jnp.sum(keep_rows), 'blk'), 1.0)  34.6 us
    reduce_scatter x1, waiting for transfers between devices, on_device(): lax.psum_scatter(hidden_terms, 'feat', scatter_dimension=1, tiled=True)  28.4 us
    all_gather x1, waiting for transfers between devices, on_device(): lax.all_gather(features, 'blk', axis=0, tiled=True)  20.7 us
    all_gather x1, waiting for transfers between devices, on_device(): lax.all_gather(hidden, 'feat', axis=1, tiled=True)  20.1 us
    all_gather x1, blocking collectives, on_device(): lax.all_gather(resid_grad, 'blk', axis=0, tiled=True)  19.3 us
  transfers between devices with their start and end apart: 5, of which 5 were waited for; matrix products, arithmetic and copies ran while one was open for 2% of the time, Pallas kernels for 0%

commit v1 on v0

v1 whole, which is shorter than its diff:
```python
import jax
import jax.numpy as jnp
from jax import lax
from jax.sharding import PartitionSpec as P

ADAM_STEP = 10
NOISE = 0.01
CLIP_AT = 0.01
BETA_ONE = 0.9
BETA_TWO = 0.999
ADAM_EPS = 1e-08
DECAY = 0.01
CHUNKS = 2
LANES = 128
BF = jnp.bfloat16
F32 = jnp.float32


def adamw_update(weight, moment, second, gradient, step_rate):
    moment = BETA_ONE * moment + (1.0 - BETA_ONE) * gradient
    second = BETA_TWO * second + (1.0 - BETA_TWO) * gradient * gradient
    moment_hat = moment / (1.0 - BETA_ONE**ADAM_STEP)
    second_hat = second / (1.0 - BETA_TWO**ADAM_STEP)
    weight = weight - step_rate * (moment_hat / (jnp.sqrt(second_hat) + ADAM_EPS) + DECAY * weight)
    return (weight, moment, second)


def swap(x, axis, size, mask):
    return lax.ppermute(x, axis, [(i, i ^ mask) for i in range(size)])


def dot(a, b, dims):
    return lax.dot_general(a, b, (dims, ((), ())), preferred_element_type=F32)


def split_low(x):
    high = x.astype(BF)
    return high, (x - high.astype(F32)).astype(BF)


def reduce_angle(x):
    turns = jnp.round(x * 0.6366197723675814)
    rest = x - turns * 1.5703125
    rest = rest - turns * 0.00048351287841796875
    rest = rest - turns * 3.1385570764541626e-07
    rest = rest - turns * 6.077100628276711e-11
    return turns.astype(jnp.int32), rest


def sin_poly(r):
    s = r * r
    return r + r * s * (-1.6666654611e-1 + s * (8.3321608736e-3 + s * (-1.9515295891e-4)))


def cos_poly(r):
    s = r * r
    return 1.0 - 0.5 * s + s * s * (4.166664568298827e-2 + s * (-1.388731625493765e-3 + s * 2.443315711809948e-5))


def cosine(x):
    turns, rest = reduce_angle(x)
    value = jnp.where((turns & 1) == 0, cos_poly(rest), sin_poly(rest))
    return jnp.where(((turns + 1) & 2) == 0, value, -value)


def sine(x):
    turns, rest = reduce_angle(x)
    value = jnp.where((turns & 1) == 0, sin_poly(rest), cos_poly(rest))
    return jnp.where((turns & 2) == 0, value, -value)


def groups_of(size):
    bits = [1 << k for k in range(size.bit_length() - 1)]
    groups = [bits[:1]]
    if len(bits) > 2:
        groups.append([bits[1], bits[2], bits[1] | bits[2]])
    groups += [[b] for b in bits[3:]]
    if len(bits) == 2:
        groups.append([bits[1]])
    return [g for g in groups if g]


def sum_over_blk(x, size):
    for group in groups_of(size):
        x = x + sum(swap(x, "blk", size, m) for m in group)
    return x


def build(n_blk, n_feat):
    masks = [1 << k for k in range(n_blk.bit_length() - 1)]
    order = [0]
    for m in reversed(masks):
        order = order + [p ^ m for p in order]

    def on_device(
        inputs,
        col_mask,
        row_mask,
        width_class,
        frequencies,
        phases,
        targets,
        prior_draws,
        hidden_weight,
        hidden_moment,
        hidden_second,
        alpha_weight,
        alpha_moment,
        alpha_second,
    ):
        classes, d_in = col_mask.shape
        rows = d_in // n_blk
        n_low = frequencies.shape[1]
        feat_scale = (2.0 / (n_low * n_feat)) ** 0.5
        samples = alpha_weight.shape[1]
        h_own = hidden_weight.shape[1]
        width = h_own // CHUNKS
        me = lax.axis_index("blk")
        half = lax.axis_index("feat")

        low = hidden_weight.astype(BF)
        gathered = []
        for c in range(CHUNKS):
            held = low[:, c * width : (c + 1) * width]
            for m in reversed(masks):
                held = jnp.concatenate([held, swap(held, "blk", n_blk, m)], axis=0)
            gathered.append(held)

        onehot = (width_class[:, None] == jnp.arange(classes, dtype=jnp.int32)[None, :]).astype(F32)
        keep_cols = jnp.dot(onehot, col_mask.astype(F32))
        masked = inputs * keep_cols.astype(BF)
        column = jnp.arange(d_in, dtype=jnp.int32)
        source = (jnp.asarray(order, jnp.int32) ^ me)[column // rows] * rows + column % rows
        select = (column[:, None] == source[None, :]).astype(BF)
        masked = jnp.dot(masked, select, preferred_element_type=F32).astype(BF)
        keep_rows = row_mask.astype(F32)
        own_freq = lax.dynamic_slice_in_dim(frequencies, half * h_own, h_own, 0)
        far_freq = lax.dynamic_slice_in_dim(frequencies, (1 - half) * h_own, h_own, 0)

        tanhs = []
        pre = None
        for c in range(CHUNKS):
            first_pre = dot(masked, gathered[c], ((1,), (0,)))
            tanh_full = jnp.tanh(first_pre)
            hidden = tanh_full.astype(BF)
            far = swap(hidden, "feat", n_feat, 1)
            part = slice(c * width, (c + 1) * width)
            term = dot(hidden, own_freq[part], ((1,), (0,))) + dot(far, far_freq[part], ((1,), (0,)))
            pre = term if pre is None else pre + term
            tanhs.append(tanh_full)
        phase_arg = pre + phases[None, :]
        features = (feat_scale * cosine(phase_arg)).astype(BF)
        slope = -feat_scale * sine(phase_arg)

        alpha = alpha_weight.T
        alpha_low = alpha.astype(BF)
        count_here = jnp.sum(keep_rows)
        moments = dot(alpha_low, features, ((1,), (0,)))
        moments = jnp.concatenate([moments, jnp.full((samples, LANES), count_here, F32)], axis=1)
        moments = sum_over_blk(moments, n_blk)
        true_count = jnp.maximum(moments[0, n_low], 1.0)
        moments_hl = split_low(moments[:, :n_low])
        both = dot(jnp.concatenate(moments_hl, axis=0), features, ((1,), (1,)))
        fitted = both[:samples] + both[samples:]
        fitted = fitted + swap(fitted, "feat", n_feat, 1)
        residual = fitted + NOISE * alpha - targets[None, :] - prior_draws.T
        resid_grad = (2.0 * keep_rows[None, :] * residual / (true_count * samples)).astype(BF)
        squares_here = jnp.sum(keep_rows[None, :] * residual * residual)
        back = dot(resid_grad, features, ((1,), (0,)))
        back = jnp.concatenate([back, jnp.full((samples, LANES), squares_here, F32)], axis=1)
        back = sum_over_blk(back, n_blk)
        resid_norm = jnp.sqrt(back[0, n_low])
        back_hl = split_low(back[:, :n_low])

        left = jnp.concatenate([resid_grad, resid_grad, alpha_low, alpha_low], axis=0)
        right = jnp.concatenate([*moments_hl, *back_hl], axis=0)
        feature_grad = dot(left, right, ((0,), (0,)))
        pre_grad = (slope * feature_grad).astype(BF)

        both = dot(jnp.concatenate(back_hl, axis=0), features, ((1,), (1,)))
        pulled = both[:samples] + both[samples:]

        weight_grad = []
        arrived = []
        for c in range(CHUNKS):
            part = slice(c * width, (c + 1) * width)
            away = dot(pre_grad, far_freq[part], ((1,), (1,))).astype(BF)
            arrived.append(swap(away, "feat", n_feat, 1))
        pulled = pulled + swap(pulled, "feat", n_feat, 1)
        alpha_grad = pulled + NOISE * resid_grad.astype(F32)
        for c in range(CHUNKS):
            part = slice(c * width, (c + 1) * width)
            hidden_grad = dot(pre_grad, own_freq[part], ((1,), (1,))) + arrived[c].astype(F32)
            first_grad = ((1.0 - tanhs[c] * tanhs[c]) * hidden_grad).astype(BF)
            mid = d_in // 2
            send = dot(masked[:, mid:], first_grad, ((0,), (0,))).astype(BF)
            keep = dot(masked[:, :mid], first_grad, ((0,), (0,)))
            for m in masks:
                keep = keep + swap(send, "blk", n_blk, m).astype(F32)
                mid = mid // 2
                send = keep[mid:].astype(BF)
                keep = keep[:mid] if m != masks[-1] else keep
            weight_grad.append(keep)
        weight_grad = jnp.concatenate(weight_grad, axis=1)

        first_feat = (half == 0).astype(F32)
        grad_part = jnp.sum(weight_grad * weight_grad) + first_feat * jnp.sum(alpha_grad * alpha_grad)
        spread = jnp.broadcast_to(grad_part, (n_blk * n_feat, LANES))
        spread = lax.all_to_all(spread, ("blk", "feat"), 0, 0, tiled=True)
        norm_before = jnp.sqrt(jnp.sum(spread[:, 0]))
        clip = jnp.minimum(1.0, CLIP_AT / (norm_before + 1e-06))
        hidden_out, moment_out, second_out = adamw_update(
            hidden_weight, hidden_moment, hidden_second, weight_grad * clip, 0.02
        )
        alpha_out, alpha_moment_out, alpha_second_out = adamw_update(
            alpha_weight, alpha_moment, alpha_second, alpha_grad.T * clip, 0.05
        )
        return (
            norm_before,
            resid_norm,
            hidden_out,
            moment_out,
            second_out,
            hidden_out.astype(BF),
            alpha_out,
            alpha_moment_out,
            alpha_second_out,
            alpha_out.astype(BF),
        )

    return on_device


def solution(mesh):
    in_specs = (
        P("blk", None),
        P(),
        P("blk"),
        P("blk"),
        P(None, "feat"),
        P("feat"),
        P("blk"),
        P("blk", None),
        P("blk", "feat"),
        P("blk", "feat"),
        P("blk", "feat"),
        P("blk", None),
        P("blk", None),
        P("blk", None),
    )
    out_specs = (
        P(),
        P(),
        P("blk", "feat"),
        P("blk", "feat"),
        P("blk", "feat"),
        P("blk", "feat"),
        P("blk", None),
        P("blk", None),
        P("blk", None),
        P("blk", None),
    )
    on_device = build(mesh.shape["blk"], mesh.shape["feat"])
    return jax.shard_map(
        on_device, mesh=mesh, in_specs=in_specs, out_specs=out_specs, check_vma=False
    )
```

time: 379 us -> 158 us (0.42)
  blocking collectives: 128 us -> 0 us
  waiting for transfers between devices: 174 us -> 67.3 us
  starting transfers between devices: 0.21 us -> 40.5 us
  matrix products: 47.1 us -> 15.7 us
  between operations: 20.3 us -> 6.9 us
  other arithmetic: 7.74 us -> 20.6 us
  local copies, waits for them, and re-layouts: 1.99 us -> 6.03 us
    psum x4 -> x0, blocking collectives: 89.5 us -> none  [the longest x1 39.6 us: on_device(): grad_total, resid_total = lax.psum((grad_part, resid_part), ('blk', 'feat'))]
    reduce_scatter x2 -> x0, waiting for transfers between devices: 88.2 us -> none  [the longest x1 59.8 us: on_device(): lax.psum_scatter(jnp.einsum('td,th->dh', columns, first_grad, preferred_e...]
    all_gather x3 -> x0, waiting for transfers between devices: 85.4 us -> none  [the longest x1 44.6 us: on_device(): lax.all_gather(hidden_weight.astype(jnp.bfloat16), 'blk', axis=0, tiled=T...]
    ppermute x0 -> x32, waiting for transfers between devices: none -> 61.3 us  [swap(): return lax.ppermute(x, axis, [(i, i ^ mask) for i in range(size)])]
    all_gather x2 -> x0, blocking collectives: 38.1 us -> none  [the longest x1 19.3 us: on_device(): lax.all_gather(resid_grad, 'blk', axis=0, tiled=True)]
    ppermute x0 -> x32, starting transfers between devices: none -> 37.1 us  [swap(): return lax.ppermute(x, axis, [(i, i ^ mask) for i in range(size)])]
    dot_general x12 -> x20, matrix products: 47.1 us -> 15.7 us  [the longest x19 13.4 us: dot(): return lax.dot_general(a, b, (dims, ((), ())), preferred_element_type=F32)]
    add x0 -> x15, other arithmetic: none -> 9.33 us  [the longest x1 5.79 us: on_device(): (jnp.asarray(order, jnp.int32) ^ me)[column // rows] * rows + column % rows]
  transfers between devices with their start and end apart: 5 -> 33, of which waited for: 5 -> 23; matrix products, arithmetic and copies ran while one was open for 2% -> 19% of each run, Pallas kernels for 0% -> 0%
where the time goes in v1:
time: 158 us; the launch traced here: 157 us
  waiting for transfers between devices  67.3 us (43%)
  starting transfers between devices  40.5 us (26%)
  other arithmetic  20.6 us (13%)
  matrix products  15.7 us (10%)
  between operations  6.9 us (4%)
  local copies, waits for them, and re-layouts  6.03 us (4%)
    ppermute x32, waiting for transfers between devices, swap(): return lax.ppermute(x, axis, [(i, i ^ mask) for i in range(size)])  61.3 us
    ppermute x32, starting transfers between devices, swap(): return lax.ppermute(x, axis, [(i, i ^ mask) for i in range(size)])  37.1 us
    dot_general x19, matrix products, dot(): return lax.dot_general(a, b, (dims, ((), ())), preferred_element_type=F32)  13.4 us
    all_to_all x1, waiting for transfers between devices, on_device(): spread = lax.all_to_all(spread, ('blk', 'feat'), 0, 0, tiled=True)  5.94 us
    add x1, other arithmetic, on_device(): (jnp.asarray(order, jnp.int32) ^ me)[column // rows] * rows + column % rows  5.79 us
    gather x10, other arithmetic, on_device(): (jnp.asarray(order, jnp.int32) ^ me)[column // rows] * rows + column % rows  4.74 us
    all_to_all x1, starting transfers between devices, on_device(): spread = lax.all_to_all(spread, ('blk', 'feat'), 0, 0, tiled=True)  3.36 us
  transfers between devices with their start and end apart: 33, of which 23 were waited for; matrix products, arithmetic and copies ran while one was open for 19% of the time, Pallas kernels for 0%

profile of v1, /device:TPU:0, one launch (start us, length us, event | category | flops | bytes accessed | tf_op | source)
XLA Modules:
  0.0 157.1 jit_solution(9027467370137820094)
XLA Ops:
  1.7 4.1 %collective-permute-start = (bf16[64,512]{1,0:T(8,128)(2,1)S(1)}, bf16[64,512]{1,0:T(8,128)(2,1)S(1)}, u32[]{:S(2)}, u32[]{:S(2)}) collective-permute-start(bf16[64,512]{1,0:T(8,128)(2,1)S(1)} %get-tuple-element.29), channel_id=1, source_target_pairs={{0,16},{2,18},{4,20},{6,22},{8,24},{10,26},{12,28},{14,30},{16,0},... | collective-permute-start | bytes 196616 | tf_op jit(solution)/shard_map/ppermute | solution.py:29
  7.5 4.4 %compare_select_fusion.1 = s32[1024,1]{0,1:T(1,128)S(1)} fusion(s32[]{:T(128)} %bitcast.9, s32[]{:T(128)} %bitcast.10, s32[]{:T(128)} %bitcast.11, s32[]{:T(128)} %bitcast.12, s32[]{:T(128)} %bitcast.13, s32[]{:T(128)} %bitcast.15, s32[]{:T(128)} %bitcast.14), kind=kLoop, calls=%fused_computation.155 | loop fusion | flops 23552 | bytes 4124 | tf_op jit(solution)/shard_map/gather | solution.py:133
  12.0 5.8 %fusion.66 = s32[1024]{0:T(1024)S(1)} fusion(pred[1024]{0:T(1024)(128)(4,1)S(1)} %compare_reduce_fusion, pred[1024]{0:T(1024)(128)(4,1)S(1)} %compare_reduce_fusion.1, pred[1024]{0:T(1024)(128)(4,1)S(1)} %compare_reduce_fusion.2, pred[1024]{0:T(1024)(128)(4,1)S(1)} %compare_reduce_fusion.3, pred[1024]{0:T(1024)(128)(4,1)S(1)} %compare_reduce_fusion.4, ...), kind=kLoop, calls=%fused_computation.167 | loop fusion | flops 17408 | bytes 17444 | tf_op jit(solution)/shard_map/add | solution.py:133
  17.8 2.3 %fusion.5 = bf16[256,1024]{1,0:T(8,128)(2,1)S(1)} fusion(s32[1024]{0:T(1024)S(1)} %fusion.66, bf16[256,1024]{1,0:T(8,128)(2,1)} %param.15, s32[256]{0:T(256)} %param.18, s32[2,1024]{1,0:T(2,128)} %param.16), kind=kOutput, calls=%fused_computation.13 | convolution fusion | flops 539757056 | bytes 1061888 | tf_op jit(solution)/shard_map/dot_general | solution.py:135
  20.2 1.9 %collective-permute-start.1 = (bf16[128,512]{1,0:T(8,128)(2,1)S(1)}, bf16[128,512]{1,0:T(8,128)(2,1)S(1)}, u32[]{:S(2)}, u32[]{:S(2)}) collective-permute-start(bf16[128,512]{1,0:T(8,128)(2,1)S(1)} %pad_maximum_fusion.5), channel_id=1, source_target_pairs={{0,8},{2,10},{4,12},{6,14},{8,0},{10,2},{12,4},{14,6},{16,24},{18,... | collective-permute-start | bytes 393224 | tf_op jit(solution)/shard_map/ppermute | solution.py:29
  22.9 3.1 %collective-permute-done.1 = bf16[128,512]{1,0:T(8,128)(2,1)S(1)} collective-permute-done((bf16[128,512]{1,0:T(8,128)(2,1)S(1)}, bf16[128,512]{1,0:T(8,128)(2,1)S(1)}, u32[]{:S(2)}, u32[]{:S(2)}) %collective-permute-start.1) | collective-permute-done | bytes 131104 | tf_op jit(solution)/shard_map/ppermute | solution.py:29
  26.0 2.1 %collective-permute-start.2 = (bf16[256,512]{1,0:T(8,128)(2,1)S(1)}, bf16[256,512]{1,0:T(8,128)(2,1)S(1)}, u32[]{:S(2)}, u32[]{:S(2)}) collective-permute-start(bf16[256,512]{1,0:T(8,128)(2,1)S(1)} %pad_maximum_fusion.2), channel_id=1, source_target_pairs={{0,4},{2,6},{4,0},{6,2},{8,12},{10,14},{12,8},{14,10},{16,20},{18,... | collective-permute-start | bytes 786440 | tf_op jit(solution)/shard_map/ppermute | solution.py:29
  28.2 1.7 %collective-permute-start.7 = (bf16[256,512]{1,0:T(8,128)(2,1)S(1)}, bf16[256,512]{1,0:T(8,128)(2,1)S(1)}, u32[]{:S(2)}, u32[]{:S(2)}) collective-permute-start(bf16[256,512]{1,0:T(8,128)(2,1)S(1)} %pad_maximum_fusion.3), channel_id=1, source_target_pairs={{0,4},{2,6},{4,0},{6,2},{8,12},{10,14},{12,8},{14,10},{16,20},{18,... | collective-permute-start | bytes 786440 | tf_op jit(solution)/shard_map/ppermute | solution.py:29
  29.8 5.4 %collective-permute-done.2 = bf16[256,512]{1,0:T(8,128)(2,1)S(1)} collective-permute-done((bf16[256,512]{1,0:T(8,128)(2,1)S(1)}, bf16[256,512]{1,0:T(8,128)(2,1)S(1)}, u32[]{:S(2)}, u32[]{:S(2)}) %collective-permute-start.2) | collective-permute-done | bytes 262176 | tf_op jit(solution)/shard_map/ppermute | solution.py:29
  35.4 2.7 %collective-permute-done.7 = bf16[256,512]{1,0:T(8,128)(2,1)S(1)} collective-permute-done((bf16[256,512]{1,0:T(8,128)(2,1)S(1)}, bf16[256,512]{1,0:T(8,128)(2,1)S(1)}, u32[]{:S(2)}, u32[]{:S(2)}) %collective-permute-start.7) | collective-permute-done | bytes 262176 | tf_op jit(solution)/shard_map/ppermute | solution.py:29
  38.8 1.9 %collective-permute-start.4 = (bf16[256,512]{1,0:T(8,128)(2,1)S(1)}, bf16[256,512]{1,0:T(8,128)(2,1)S(1)}, u32[]{:S(2)}, u32[]{:S(2)}) collective-permute-start(bf16[256,512]{1,0:T(8,128)(2,1)S(1)} %get-tuple-element.48), channel_id=1, source_target_pairs={{0,1},{1,0},{2,3},{3,2},{4,5},{5,4},{6,7},{7,6},{8,9},{9,8},{10,11... | collective-permute-start | bytes 786440 | tf_op jit(solution)/shard_map/ppermute | solution.py:29
  41.6 1.3 collective-permute-start.9
  43.4 4.6 %collective-permute-done.4 = bf16[256,512]{1,0:T(8,128)(2,1)S(1)} collective-permute-done((bf16[256,512]{1,0:T(8,128)(2,1)S(1)}, bf16[256,512]{1,0:T(8,128)(2,1)S(1)}, u32[]{:S(2)}, u32[]{:S(2)}) %collective-permute-start.4) | collective-permute-done | bytes 262176 | tf_op jit(solution)/shard_map/ppermute | solution.py:29
  48.5 4.7 %collective-permute-done.9 = bf16[256,512]{1,0:T(8,128)(2,1)S(1)} collective-permute-done((bf16[256,512]{1,0:T(8,128)(2,1)S(1)}, bf16[256,512]{1,0:T(8,128)(2,1)S(1)}, u32[]{:S(2)}, u32[]{:S(2)}) %collective-permute-start.9) | collective-permute-done | bytes 262176 | tf_op jit(solution)/shard_map/ppermute | solution.py:29
  53.3 1.9 %fusion.18 = (bf16[256,1024]{1,0:T(8,128)(2,1)S(1)}, f32[256,1024]{1,0:T(8,128)S(1)}) fusion(f32[1024]{0:T(1024)S(1)} %copy-done.12, f32[256,1024]{1,0:T(8,128)S(1)} %convolution_add_fusion.3, f32[256,1024]{1,0:T(8,128)S(1)} %fusion.23, bf16[256,512]{1,0:T(8,128)(2,1)S(1)} %collective-permute-done.9, bf16[2048,1024]{1,0:T(8,128)(2,1)S(1)} %copy-done, ...), kind=kOutput, calls=%fused_computation.41 | convolution fusion | flops 279183360 | bytes 4984836 | tf_op jit(solution)/shard_map/dot_general | solution.py:33
  56.1 1.3 collective-permute-done.10
  58.0 1.9 %collective-permute-start.13 = (f32[16,1152]{1,0:T(8,128)S(1)}, f32[16,1152]{1,0:T(8,128)S(1)}, u32[]{:S(2)}, u32[]{:S(2)}) collective-permute-start(f32[16,1152]{1,0:T(8,128)S(1)} %pad_add_fusion.1), channel_id=1, source_target_pairs={{0,12},{2,14},{4,8},{6,10},{8,4},{10,6},{12,0},{14,2},{16,28},{18,... | collective-permute-start | bytes 221192 | tf_op jit(solution)/shard_map/ppermute | solution.py:29
  60.5 1.1 collective-permute-start.12
  61.5 1.8 %collective-permute-done.13 = f32[16,1152]{1,0:T(8,128)S(1)} collective-permute-done((f32[16,1152]{1,0:T(8,128)S(1)}, f32[16,1152]{1,0:T(8,128)S(1)}, u32[]{:S(2)}, u32[]{:S(2)}) %collective-permute-start.13) | collective-permute-done | bytes 73760 | tf_op jit(solution)/shard_map/ppermute | solution.py:29
  63.4 1.5 collective-permute-done.11
  65.1 2.6 %collective-permute-start.14 = (f32[16,1152]{1,0:T(8,128)S(1)}, f32[16,1152]{1,0:T(8,128)S(1)}, u32[]{:S(2)}, u32[]{:S(2)}) collective-permute-start(f32[16,1152]{1,0:T(8,128)S(1)} %add_add_fusion.1), channel_id=1, source_target_pairs={{0,16},{2,18},{4,20},{6,22},{8,24},{10,26},{12,28},{14,30},{16,0},... | collective-permute-start | bytes 221192 | tf_op jit(solution)/shard_map/ppermute | solution.py:29
  67.8 3.8 %collective-permute-done.14 = f32[16,1152]{1,0:T(8,128)S(1)} collective-permute-done((f32[16,1152]{1,0:T(8,128)S(1)}, f32[16,1152]{1,0:T(8,128)S(1)}, u32[]{:S(2)}, u32[]{:S(2)}) %collective-permute-start.14) | collective-permute-done | bytes 73760 | tf_op jit(solution)/shard_map/ppermute | solution.py:29
  71.9 1.6 %collective-permute-start.15 = (f32[16,256]{1,0:T(8,128)S(1)}, f32[16,256]{1,0:T(8,128)S(1)}, u32[]{:S(2)}, u32[]{:S(2)}) collective-permute-start(f32[16,256]{1,0:T(8,128)S(1)} %slice_add_fusion.7), channel_id=1, source_target_pairs={{0,1},{1,0},{2,3},{3,2},{4,5},{5,4},{6,7},{7,6},{8,9},{9,8},{10,11... | collective-permute-start | bytes 49160 | tf_op jit(solution)/shard_map/ppermute | solution.py:29
  74.7 1.0 collective-permute-done.15
  77.3 1.3 collective-permute-done.16
  80.8 1.9 %collective-permute-start.18 = (f32[16,1152]{1,0:T(8,128)S(1)}, f32[16,1152]{1,0:T(8,128)S(1)}, u32[]{:S(2)}, u32[]{:S(2)}) collective-permute-start(f32[16,1152]{1,0:T(8,128)S(1)} %pad_add_fusion), channel_id=1, source_target_pairs={{0,8},{2,10},{4,12},{6,14},{8,0},{10,2},{12,4},{14,6},{16,24},{18,... | collective-permute-start | bytes 221192 | tf_op jit(solution)/shard_map/ppermute | solution.py:29
  82.7 2.5 %collective-permute-done.19 = f32[16,1152]{1,0:T(8,128)S(1)} collective-permute-done((f32[16,1152]{1,0:T(8,128)S(1)}, f32[16,1152]{1,0:T(8,128)S(1)}, u32[]{:S(2)}, u32[]{:S(2)}) %collective-permute-start.19) | collective-permute-done | bytes 73760 | tf_op jit(solution)/shard_map/ppermute | solution.py:29
  85.8 2.8 %collective-permute-start.20 = (f32[16,1152]{1,0:T(8,128)S(1)}, f32[16,1152]{1,0:T(8,128)S(1)}, u32[]{:S(2)}, u32[]{:S(2)}) collective-permute-start(f32[16,1152]{1,0:T(8,128)S(1)} %add_add_fusion), channel_id=1, source_target_pairs={{0,16},{2,18},{4,20},{6,22},{8,24},{10,26},{12,28},{14,30},{16,0},... | collective-permute-start | bytes 221192 | tf_op jit(solution)/shard_map/ppermute | solution.py:29
  88.6 3.5 %collective-permute-done.20 = f32[16,1152]{1,0:T(8,128)S(1)} collective-permute-done((f32[16,1152]{1,0:T(8,128)S(1)}, f32[16,1152]{1,0:T(8,128)S(1)}, u32[]{:S(2)}, u32[]{:S(2)}) %collective-permute-start.20) | collective-permute-done | bytes 73760 | tf_op jit(solution)/shard_map/ppermute | solution.py:29
  92.8 1.4 fusion.4
  95.2 1.7 %convolution_convert_fusion.4 = bf16[256,512]{1,0:T(8,128)(2,1)S(1)} fusion(bf16[256,1024]{1,0:T(8,128)(2,1)S(1)} %fusion.4, bf16[2048,1024]{1,0:T(8,128)(2,1)} %param.19, s32[]{:T(128)S(6)} %select_n.56), kind=kOutput, calls=%fused_computation.21 | convolution fusion | flops 268566528 | bytes 1835012 | tf_op jit(solution)/shard_map/dot_general | solution.py:33
  96.9 1.6 %collective-permute-start.21 = (bf16[256,512]{1,0:T(8,128)(2,1)S(1)}, bf16[256,512]{1,0:T(8,128)(2,1)S(1)}, u32[]{:S(2)}, u32[]{:S(2)}) collective-permute-start(bf16[256,512]{1,0:T(8,128)(2,1)S(1)} %convolution_convert_fusion.4), channel_id=1, source_target_pairs={{0,1},{1,0},{2,3},{3,2},{4,5},{5,4},{6,7},{7,6},{8,9},{9,8},{10,11... | collective-permute-start | bytes 786440 | tf_op jit(solution)/shard_map/ppermute | solution.py:29
  98.5 5.4 %collective-permute-done.26 = bf16[256,512]{1,0:T(8,128)(2,1)S(1)} collective-permute-done((bf16[256,512]{1,0:T(8,128)(2,1)S(1)}, bf16[256,512]{1,0:T(8,128)(2,1)S(1)}, u32[]{:S(2)}, u32[]{:S(2)}) %collective-permute-start.26) | collective-permute-done | bytes 262176 | tf_op jit(solution)/shard_map/ppermute | solution.py:29
  103.9 1.7 %multiply_convert_fusion = bf16[256,512]{1,0:T(8,128)(2,1)S(1)} fusion(bf16[256,512]{1,0:T(8,128)(2,1)S(1)} %collective-permute-done.26, f32[256,512]{1,0:T(8,128)S(1)} %get-tuple-element.51, bf16[256,1024]{1,0:T(8,128)(2,1)S(1)} %fusion.4, bf16[2048,1024]{1,0:T(8,128)(2,1)} %param.19, s32[]{:T(128)S(6)} %add.271), kind=kOutput, calls=%fused_computation.65 | convolution fusion | flops 269221888 | bytes 2621444 | tf_op jit(solution)/shard_map/dot_general | solution.py:33
  106.1 1.2 collective-permute-done.21
  107.3 1.7 %multiply_convert_fusion.1 = bf16[256,512]{1,0:T(8,128)(2,1)S(1)} fusion(bf16[256,512]{1,0:T(8,128)(2,1)S(1)} %collective-permute-done.21, f32[256,512]{1,0:T(8,128)S(1)} %get-tuple-element.49, bf16[256,1024]{1,0:T(8,128)(2,1)S(1)} %fusion.4, bf16[2048,1024]{1,0:T(8,128)(2,1)} %param.19, s32[]{:T(128)S(6)} %select_n.55), kind=kOutput, calls=%fused_computation.66 | convolution fusion | flops 269221888 | bytes 2621444 | tf_op jit(solution)/shard_map/dot_general | solution.py:33
  109.8 1.2 collective-permute-start.31
  113.6 1.6 collective-permute-start.23
  116.4 5.1 %collective-permute-done.28 = bf16[256,512]{1,0:T(8,128)(2,1)} collective-permute-done((bf16[256,512]{1,0:T(8,128)(2,1)}, bf16[256,512]{1,0:T(8,128)(2,1)}, u32[]{:S(2)}, u32[]{:S(2)}) %collective-permute-start.28) | collective-permute-done | bytes 262176 | tf_op jit(solution)/shard_map/ppermute | solution.py:29
  121.5 1.0 slice_add_fusion
  122.7 3.7 %collective-permute-done.23 = bf16[256,512]{1,0:T(8,128)(2,1)} collective-permute-done((bf16[256,512]{1,0:T(8,128)(2,1)}, bf16[256,512]{1,0:T(8,128)(2,1)}, u32[]{:S(2)}, u32[]{:S(2)}) %collective-permute-start.23) | collective-permute-done | bytes 262176 | tf_op jit(solution)/shard_map/ppermute | solution.py:29
  126.4 1.0 slice_add_fusion.1
  127.7 3.0 %collective-permute-start.30 = (bf16[64,512]{1,0:T(8,128)(2,1)S(1)}, bf16[64,512]{1,0:T(8,128)(2,1)S(1)}, u32[]{:S(2)}, u32[]{:S(2)}) collective-permute-start(bf16[64,512]{1,0:T(8,128)(2,1)S(1)} %slice.205), channel_id=1, source_target_pairs={{0,16},{2,18},{4,20},{6,22},{8,24},{10,26},{12,28},{14,30},{16,0},... | collective-permute-start | bytes 196616 | tf_op jit(solution)/shard_map/ppermute | solution.py:29
  130.7 2.9 %collective-permute-done.24 = bf16[128,512]{1,0:T(8,128)(2,1)S(1)} collective-permute-done((bf16[128,512]{1,0:T(8,128)(2,1)S(1)}, bf16[128,512]{1,0:T(8,128)(2,1)S(1)}, u32[]{:S(2)}, u32[]{:S(2)}) %collective-permute-start.24) | collective-permute-done | bytes 131104 | tf_op jit(solution)/shard_map/ppermute | solution.py:29
  134.5 4.8 %collective-permute-done.25 = bf16[64,512]{1,0:T(8,128)(2,1)S(1)} collective-permute-done((bf16[64,512]{1,0:T(8,128)(2,1)S(1)}, bf16[64,512]{1,0:T(8,128)(2,1)S(1)}, u32[]{:S(2)}, u32[]{:S(2)}) %collective-permute-start.25) | collective-permute-done | bytes 65568 | tf_op jit(solution)/shard_map/ppermute | solution.py:29
  141.2 3.4 %all-to-all-start = ((f32[32,1,128]{2,1,0:T(1,128)}), f32[32,1,128]{2,1,0:T(1,128)S(1)}, u32[]{:S(2)}, u32[]{:S(2)}) async-start(f32[32,1,128]{2,1,0:T(1,128)} %broadcast_in_dim.2), calls=%async_computation | async-start | bytes 32768 | tf_op jit(solution)/shard_map/all_to_all | solution.py:209
  145.8 5.9 %all-to-all-done = f32[32,1,128]{2,1,0:T(1,128)S(1)} async-done(((f32[32,1,128]{2,1,0:T(1,128)}), f32[32,1,128]{2,1,0:T(1,128)S(1)}, u32[]{:S(2)}, u32[]{:S(2)}) %all-to-all-start) | async-done | bytes 16416 | tf_op jit(solution)/shard_map/all_to_all | solution.py:209
  153.1 1.1 fusion.89
  (130 shorter events, 24.1 us)
Async XLA Ops:
  0.6 21.4 %copy-start.10 = (s32[256]{0:T(256)S(1)}, s32[256]{0:T(256)}, u32[]{:S(2)}) copy-start(s32[256]{0:T(256)} %param.17) | copy-start | bytes 3076
  1.7 18.5 %collective-permute-start = (bf16[64,512]{1,0:T(8,128)(2,1)S(1)}, bf16[64,512]{1,0:T(8,128)(2,1)S(1)}, u32[]{:S(2)}, u32[]{:S(2)}) collective-permute-start(bf16[64,512]{1,0:T(8,128)(2,1)S(1)} %get-tuple-element.29), channel_id=1, source_target_pairs={{0,16},{2,18},{4,20},{6,22},{8,24},{10,26},{12,28},{14,30},{16,0},... | collective-permute-start | bytes 196616 | tf_op jit(solution)/shard_map/ppermute | solution.py:29
  5.8 16.9 %collective-permute-start.5 = (bf16[64,512]{1,0:T(8,128)(2,1)S(1)}, bf16[64,512]{1,0:T(8,128)(2,1)S(1)}, u32[]{:S(2)}, u32[]{:S(2)}) collective-permute-start(bf16[64,512]{1,0:T(8,128)(2,1)S(1)} %get-tuple-element.26), channel_id=1, source_target_pairs={{0,16},{2,18},{4,20},{6,22},{8,24},{10,26},{12,28},{14,30},{16,0},... | collective-permute-start | bytes 196616 | tf_op jit(solution)/shard_map/ppermute | solution.py:29
  20.2 5.9 %collective-permute-start.1 = (bf16[128,512]{1,0:T(8,128)(2,1)S(1)}, bf16[128,512]{1,0:T(8,128)(2,1)S(1)}, u32[]{:S(2)}, u32[]{:S(2)}) collective-permute-start(bf16[128,512]{1,0:T(8,128)(2,1)S(1)} %pad_maximum_fusion.5), channel_id=1, source_target_pairs={{0,8},{2,10},{4,12},{6,14},{8,0},{10,2},{12,4},{14,6},{16,24},{18,... | collective-permute-start | bytes 393224 | tf_op jit(solution)/shard_map/ppermute | solution.py:29
  22.7 5.5 %collective-permute-start.6 = (bf16[128,512]{1,0:T(8,128)(2,1)S(1)}, bf16[128,512]{1,0:T(8,128)(2,1)S(1)}, u32[]{:S(2)}, u32[]{:S(2)}) collective-permute-start(bf16[128,512]{1,0:T(8,128)(2,1)S(1)} %pad_maximum_fusion.6), channel_id=1, source_target_pairs={{0,8},{2,10},{4,12},{6,14},{8,0},{10,2},{12,4},{14,6},{16,24},{18,... | collective-permute-start | bytes 393224 | tf_op jit(solution)/shard_map/ppermute | solution.py:29
  26.0 9.2 %collective-permute-start.2 = (bf16[256,512]{1,0:T(8,128)(2,1)S(1)}, bf16[256,512]{1,0:T(8,128)(2,1)S(1)}, u32[]{:S(2)}, u32[]{:S(2)}) collective-permute-start(bf16[256,512]{1,0:T(8,128)(2,1)S(1)} %pad_maximum_fusion.2), channel_id=1, source_target_pairs={{0,4},{2,6},{4,0},{6,2},{8,12},{10,14},{12,8},{14,10},{16,20},{18,... | collective-permute-start | bytes 786440 | tf_op jit(solution)/shard_map/ppermute | solution.py:29
  28.2 9.9 %collective-permute-start.7 = (bf16[256,512]{1,0:T(8,128)(2,1)S(1)}, bf16[256,512]{1,0:T(8,128)(2,1)S(1)}, u32[]{:S(2)}, u32[]{:S(2)}) collective-permute-start(bf16[256,512]{1,0:T(8,128)(2,1)S(1)} %pad_maximum_fusion.3), channel_id=1, source_target_pairs={{0,4},{2,6},{4,0},{6,2},{8,12},{10,14},{12,8},{14,10},{16,20},{18,... | collective-permute-start | bytes 786440 | tf_op jit(solution)/shard_map/ppermute | solution.py:29
  35.3 3.0 %collective-permute-start.3 = (bf16[512,512]{1,0:T(8,128)(2,1)S(1)}, bf16[512,512]{1,0:T(8,128)(2,1)S(1)}, u32[]{:S(2)}, u32[]{:S(2)}) collective-permute-start(bf16[512,512]{1,0:T(8,128)(2,1)S(1)} %pad_maximum_fusion), channel_id=1, source_target_pairs={{0,2},{2,0},{4,6},{6,4},{8,10},{10,8},{12,14},{14,12},{16,18},{18,... | collective-permute-start | bytes 1572872 | tf_op jit(solution)/shard_map/ppermute | solution.py:29
  38.1 3.0 %copy-start = (bf16[2048,1024]{1,0:T(8,128)(2,1)S(1)}, bf16[2048,1024]{1,0:T(8,128)(2,1)}, u32[]{:S(2)}) copy-start(bf16[2048,1024]{1,0:T(8,128)(2,1)} %param.19) | copy-start | bytes 12582916
  38.2 2.5 %collective-permute-start.8 = (bf16[512,512]{1,0:T(8,128)(2,1)S(1)}, bf16[512,512]{1,0:T(8,128)(2,1)S(1)}, u32[]{:S(2)}, u32[]{:S(2)}) collective-permute-start(bf16[512,512]{1,0:T(8,128)(2,1)S(1)} %pad_maximum_fusion.1), channel_id=1, source_target_pairs={{0,2},{2,0},{4,6},{6,4},{8,10},{10,8},{12,14},{14,12},{16,18},{18,... | collective-permute-start | bytes 1572872 | tf_op jit(solution)/shard_map/ppermute | solution.py:29
  38.8 9.2 %collective-permute-start.4 = (bf16[256,512]{1,0:T(8,128)(2,1)S(1)}, bf16[256,512]{1,0:T(8,128)(2,1)S(1)}, u32[]{:S(2)}, u32[]{:S(2)}) collective-permute-start(bf16[256,512]{1,0:T(8,128)(2,1)S(1)} %get-tuple-element.48), channel_id=1, source_target_pairs={{0,1},{1,0},{2,3},{3,2},{4,5},{5,4},{6,7},{7,6},{8,9},{9,8},{10,11... | collective-permute-start | bytes 786440 | tf_op jit(solution)/shard_map/ppermute | solution.py:29
  41.2 12.1 %copy-start.12 = (f32[1024]{0:T(1024)S(1)}, f32[1024]{0:T(1024)}, u32[]{:S(2)}) copy-start(f32[1024]{0:T(1024)} %param.20) | copy-start | bytes 12292
  41.6 11.6 %collective-permute-start.9 = (bf16[256,512]{1,0:T(8,128)(2,1)S(1)}, bf16[256,512]{1,0:T(8,128)(2,1)S(1)}, u32[]{:S(2)}, u32[]{:S(2)}) collective-permute-start(bf16[256,512]{1,0:T(8,128)(2,1)S(1)} %get-tuple-element.50), channel_id=1, source_target_pairs={{0,1},{1,0},{2,3},{3,2},{4,5},{5,4},{6,7},{7,6},{8,9},{9,8},{10,11... | collective-permute-start | bytes 786440 | tf_op jit(solution)/shard_map/ppermute | solution.py:29
  48.5 6.6 %copy-start.4 = (f32[256,16]{0,1:T(8,128)S(1)}, f32[256,16]{0,1:T(8,128)}, u32[]{:S(2)}) copy-start(f32[256,16]{0,1:T(8,128)} %param.26) | copy-start | bytes 49156
  48.5 27.2 %copy-start.7 = (f32[256,16]{0,1:T(8,128)S(1)}, f32[256,16]{0,1:T(8,128)}, u32[]{:S(2)}) copy-start(f32[256,16]{0,1:T(8,128)} %param.22) | copy-start | bytes 49156
  48.5 27.2 %copy-start.11 = (f32[256]{0:T(256)S(1)}, f32[256]{0:T(256)}, u32[]{:S(2)}) copy-start(f32[256]{0:T(256)} %param.21) | copy-start | bytes 3076
  56.0 1.3 collective-permute-start.10
  58.0 5.4 %collective-permute-start.13 = (f32[16,1152]{1,0:T(8,128)S(1)}, f32[16,1152]{1,0:T(8,128)S(1)}, u32[]{:S(2)}, u32[]{:S(2)}) collective-permute-start(f32[16,1152]{1,0:T(8,128)S(1)} %pad_add_fusion.1), channel_id=1, source_target_pairs={{0,12},{2,14},{4,8},{6,10},{8,4},{10,6},{12,0},{14,2},{16,28},{18,... | collective-permute-start | bytes 221192 | tf_op jit(solution)/shard_map/ppermute | solution.py:29
  59.9 4.9 %collective-permute-start.11 = (f32[16,1152]{1,0:T(8,128)S(1)}, f32[16,1152]{1,0:T(8,128)S(1)}, u32[]{:S(2)}, u32[]{:S(2)}) collective-permute-start(f32[16,1152]{1,0:T(8,128)S(1)} %pad_add_fusion.1), channel_id=1, source_target_pairs={{0,4},{2,6},{4,0},{6,2},{8,12},{10,14},{12,8},{14,10},{16,20},{18,... | collective-permute-start | bytes 221192 | tf_op jit(solution)/shard_map/ppermute | solution.py:29
  60.5 4.6 %collective-permute-start.12 = (f32[16,1152]{1,0:T(8,128)S(1)}, f32[16,1152]{1,0:T(8,128)S(1)}, u32[]{:S(2)}, u32[]{:S(2)}) collective-permute-start(f32[16,1152]{1,0:T(8,128)S(1)} %pad_add_fusion.1), channel_id=1, source_target_pairs={{0,8},{2,10},{4,12},{6,14},{8,0},{10,2},{12,4},{14,6},{16,24},{18,... | collective-permute-start | bytes 221192 | tf_op jit(solution)/shard_map/ppermute | solution.py:29
  65.1 6.5 %collective-permute-start.14 = (f32[16,1152]{1,0:T(8,128)S(1)}, f32[16,1152]{1,0:T(8,128)S(1)}, u32[]{:S(2)}, u32[]{:S(2)}) collective-permute-start(f32[16,1152]{1,0:T(8,128)S(1)} %add_add_fusion.1), channel_id=1, source_target_pairs={{0,16},{2,18},{4,20},{6,22},{8,24},{10,26},{12,28},{14,30},{16,0},... | collective-permute-start | bytes 221192 | tf_op jit(solution)/shard_map/ppermute | solution.py:29
  71.9 3.8 %collective-permute-start.15 = (f32[16,256]{1,0:T(8,128)S(1)}, f32[16,256]{1,0:T(8,128)S(1)}, u32[]{:S(2)}, u32[]{:S(2)}) collective-permute-start(f32[16,256]{1,0:T(8,128)S(1)} %slice_add_fusion.7), channel_id=1, source_target_pairs={{0,1},{1,0},{2,3},{3,2},{4,5},{5,4},{6,7},{7,6},{8,9},{9,8},{10,11... | collective-permute-start | bytes 49160 | tf_op jit(solution)/shard_map/ppermute | solution.py:29
  77.2 1.3 collective-permute-start.16
  79.2 6.0 %collective-permute-start.19 = (f32[16,1152]{1,0:T(8,128)S(1)}, f32[16,1152]{1,0:T(8,128)S(1)}, u32[]{:S(2)}, u32[]{:S(2)}) collective-permute-start(f32[16,1152]{1,0:T(8,128)S(1)} %pad_add_fusion), channel_id=1, source_target_pairs={{0,12},{2,14},{4,8},{6,10},{8,4},{10,6},{12,0},{14,2},{16,28},{18,... | collective-permute-start | bytes 221192 | tf_op jit(solution)/shard_map/ppermute | solution.py:29
  80.1 5.6 %collective-permute-start.17 = (f32[16,1152]{1,0:T(8,128)S(1)}, f32[16,1152]{1,0:T(8,128)S(1)}, u32[]{:S(2)}, u32[]{:S(2)}) collective-permute-start(f32[16,1152]{1,0:T(8,128)S(1)} %pad_add_fusion), channel_id=1, source_target_pairs={{0,4},{2,6},{4,0},{6,2},{8,12},{10,14},{12,8},{14,10},{16,20},{18,... | collective-permute-start | bytes 221192 | tf_op jit(solution)/shard_map/ppermute | solution.py:29
  80.8 4.9 %collective-permute-start.18 = (f32[16,1152]{1,0:T(8,128)S(1)}, f32[16,1152]{1,0:T(8,128)S(1)}, u32[]{:S(2)}, u32[]{:S(2)}) collective-permute-start(f32[16,1152]{1,0:T(8,128)S(1)} %pad_add_fusion), channel_id=1, source_target_pairs={{0,8},{2,10},{4,12},{6,14},{8,0},{10,2},{12,4},{14,6},{16,24},{18,... | collective-permute-start | bytes 221192 | tf_op jit(solution)/shard_map/ppermute | solution.py:29
  85.8 6.3 %collective-permute-start.20 = (f32[16,1152]{1,0:T(8,128)S(1)}, f32[16,1152]{1,0:T(8,128)S(1)}, u32[]{:S(2)}, u32[]{:S(2)}) collective-permute-start(f32[16,1152]{1,0:T(8,128)S(1)} %add_add_fusion), channel_id=1, source_target_pairs={{0,16},{2,18},{4,20},{6,22},{8,24},{10,26},{12,28},{14,30},{16,0},... | collective-permute-start | bytes 221192 | tf_op jit(solution)/shard_map/ppermute | solution.py:29
  92.2 0.6 copy-start.5
  94.6 9.2 %collective-permute-start.26 = (bf16[256,512]{1,0:T(8,128)(2,1)S(1)}, bf16[256,512]{1,0:T(8,128)(2,1)S(1)}, u32[]{:S(2)}, u32[]{:S(2)}) collective-permute-start(bf16[256,512]{1,0:T(8,128)(2,1)S(1)} %convolution_convert_fusion.3), channel_id=1, source_target_pairs={{0,1},{1,0},{2,3},{3,2},{4,5},{5,4},{6,7},{7,6},{8,9},{9,8},{10,11... | collective-permute-start | bytes 786440 | tf_op jit(solution)/shard_map/ppermute | solution.py:29
  95.2 14.3 %copy-start.6 = (bf16[16,1024]{1,0:T(8,128)(2,1)S(1)}, bf16[16,1024]{1,0:T(8,128)(2,1)}, u32[]{:S(2)}) copy-start(bf16[16,1024]{1,0:T(8,128)(2,1)} %copy-done.5) | copy-start | bytes 98308
  96.9 10.4 %collective-permute-start.21 = (bf16[256,512]{1,0:T(8,128)(2,1)S(1)}, bf16[256,512]{1,0:T(8,128)(2,1)S(1)}, u32[]{:S(2)}, u32[]{:S(2)}) collective-permute-start(bf16[256,512]{1,0:T(8,128)(2,1)S(1)} %convolution_convert_fusion.4), channel_id=1, source_target_pairs={{0,1},{1,0},{2,3},{3,2},{4,5},{5,4},{6,7},{7,6},{8,9},{9,8},{10,11... | collective-permute-start | bytes 786440 | tf_op jit(solution)/shard_map/ppermute | solution.py:29
  106.0 5.0 %collective-permute-start.27 = (bf16[512,512]{1,0:T(8,128)(2,1)S(1)}, bf16[512,512]{1,0:T(8,128)(2,1)S(1)}, u32[]{:S(2)}, u32[]{:S(2)}) collective-permute-start(bf16[512,512]{1,0:T(8,128)(2,1)S(1)} %convolution_convert_fusion), channel_id=1, source_target_pairs={{0,2},{2,0},{4,6},{6,4},{8,10},{10,8},{12,14},{14,12},{16,18},{18,... | collective-permute-start | bytes 1572872 | tf_op jit(solution)/shard_map/ppermute | solution.py:29
  109.4 3.1 %collective-permute-start.22 = (bf16[512,512]{1,0:T(8,128)(2,1)S(1)}, bf16[512,512]{1,0:T(8,128)(2,1)S(1)}, u32[]{:S(2)}, u32[]{:S(2)}) collective-permute-start(bf16[512,512]{1,0:T(8,128)(2,1)S(1)} %convolution_convert_fusion.1), channel_id=1, source_target_pairs={{0,2},{2,0},{4,6},{6,4},{8,10},{10,8},{12,14},{14,12},{16,18},{18,... | collective-permute-start | bytes 1572872 | tf_op jit(solution)/shard_map/ppermute | solution.py:29
  109.8 5.4 %collective-permute-start.31 = (f32[16,256]{1,0:T(8,128)S(1)}, f32[16,256]{1,0:T(8,128)S(1)}, u32[]{:S(2)}, u32[]{:S(2)}) collective-permute-start(f32[16,256]{1,0:T(8,128)S(1)} %slice_add_fusion.6), channel_id=1, source_target_pairs={{0,1},{1,0},{2,3},{3,2},{4,5},{5,4},{6,7},{7,6},{8,9},{9,8},{10,11... | collective-permute-start | bytes 49160 | tf_op jit(solution)/shard_map/ppermute | solution.py:29
  112.0 41.0 %copy-start.1 = (f32[64,1024]{1,0:T(8,128)S(1)}, f32[64,1024]{1,0:T(8,128)}, u32[]{:S(2)}) copy-start(f32[64,1024]{1,0:T(8,128)} %param.23) | copy-start | bytes 786436
  112.0 41.1 %copy-start.2 = (f32[64,1024]{1,0:T(8,128)S(1)}, f32[64,1024]{1,0:T(8,128)}, u32[]{:S(2)}) copy-start(f32[64,1024]{1,0:T(8,128)} %param.24) | copy-start | bytes 786436
  112.0 41.1 %copy-start.3 = (f32[64,1024]{1,0:T(8,128)S(1)}, f32[64,1024]{1,0:T(8,128)}, u32[]{:S(2)}) copy-start(f32[64,1024]{1,0:T(8,128)} %param.25) | copy-start | bytes 786436
  112.0 9.5 %collective-permute-start.28 = (bf16[256,512]{1,0:T(8,128)(2,1)}, bf16[256,512]{1,0:T(8,128)(2,1)}, u32[]{:S(2)}, u32[]{:S(2)}) collective-permute-start(bf16[256,512]{1,0:T(8,128)(2,1)} %slice.201), channel_id=1, source_target_pairs={{0,4},{2,6},{4,0},{6,2},{8,12},{10,14},{12,8},{14,10},{16,20},{18,... | collective-permute-start | bytes 786440 | tf_op jit(solution)/shard_map/ppermute | solution.py:29
  112.9 41.3 %copy-start.8 = (f32[256,16]{0,1:T(8,128)S(1)}, f32[256,16]{0,1:T(8,128)}, u32[]{:S(2)}) copy-start(f32[256,16]{0,1:T(8,128)} %param.27) | copy-start | bytes 49156
  112.9 41.3 %copy-start.9 = (f32[256,16]{0,1:T(8,128)S(1)}, f32[256,16]{0,1:T(8,128)}, u32[]{:S(2)}) copy-start(f32[256,16]{0,1:T(8,128)} %param.28) | copy-start | bytes 49156
  113.6 12.8 %collective-permute-start.23 = (bf16[256,512]{1,0:T(8,128)(2,1)}, bf16[256,512]{1,0:T(8,128)(2,1)}, u32[]{:S(2)}, u32[]{:S(2)}) collective-permute-start(bf16[256,512]{1,0:T(8,128)(2,1)} %slice.202), channel_id=1, source_target_pairs={{0,4},{2,6},{4,0},{6,2},{8,12},{10,14},{12,8},{14,10},{16,20},{18,... | collective-permute-start | bytes 786440 | tf_op jit(solution)/shard_map/ppermute | solution.py:29
  122.6 5.0 %collective-permute-start.29 = (bf16[128,512]{1,0:T(8,128)(2,1)S(1)}, bf16[128,512]{1,0:T(8,128)(2,1)S(1)}, u32[]{:S(2)}, u32[]{:S(2)}) collective-permute-start(bf16[128,512]{1,0:T(8,128)(2,1)S(1)} %slice.203), channel_id=1, source_target_pairs={{0,8},{2,10},{4,12},{6,14},{8,0},{10,2},{12,4},{14,6},{16,24},{18,... | collective-permute-start | bytes 393224 | tf_op jit(solution)/shard_map/ppermute | solution.py:29
  127.4 6.2 %collective-permute-start.24 = (bf16[128,512]{1,0:T(8,128)(2,1)S(1)}, bf16[128,512]{1,0:T(8,128)(2,1)S(1)}, u32[]{:S(2)}, u32[]{:S(2)}) collective-permute-start(bf16[128,512]{1,0:T(8,128)(2,1)S(1)} %slice.204), channel_id=1, source_target_pairs={{0,8},{2,10},{4,12},{6,14},{8,0},{10,2},{12,4},{14,6},{16,24},{18,... | collective-permute-start | bytes 393224 | tf_op jit(solution)/shard_map/ppermute | solution.py:29
  127.7 6.8 %collective-permute-start.30 = (bf16[64,512]{1,0:T(8,128)(2,1)S(1)}, bf16[64,512]{1,0:T(8,128)(2,1)S(1)}, u32[]{:S(2)}, u32[]{:S(2)}) collective-permute-start(bf16[64,512]{1,0:T(8,128)(2,1)S(1)} %slice.205), channel_id=1, source_target_pairs={{0,16},{2,18},{4,20},{6,22},{8,24},{10,26},{12,28},{14,30},{16,0},... | collective-permute-start | bytes 196616 | tf_op jit(solution)/shard_map/ppermute | solution.py:29
  133.7 5.5 %collective-permute-start.25 = (bf16[64,512]{1,0:T(8,128)(2,1)S(1)}, bf16[64,512]{1,0:T(8,128)(2,1)S(1)}, u32[]{:S(2)}, u32[]{:S(2)}) collective-permute-start(bf16[64,512]{1,0:T(8,128)(2,1)S(1)} %slice.206), channel_id=1, source_target_pairs={{0,16},{2,18},{4,20},{6,22},{8,24},{10,26},{12,28},{14,30},{16,0},... | collective-permute-start | bytes 196616 | tf_op jit(solution)/shard_map/ppermute | solution.py:29
  141.2 10.5 %all-to-all-start = ((f32[32,1,128]{2,1,0:T(1,128)}), f32[32,1,128]{2,1,0:T(1,128)S(1)}, u32[]{:S(2)}, u32[]{:S(2)}) async-start(f32[32,1,128]{2,1,0:T(1,128)} %broadcast_in_dim.2), calls=%async_computation | async-start | bytes 32768 | tf_op jit(solution)/shard_map/all_to_all | solution.py:209

commit v2 on v1

v2 whole, which is shorter than its diff:
```python
import jax
import jax.numpy as jnp
from jax import lax
from jax.experimental import pallas as pl
from jax.experimental.pallas import tpu as pltpu
from jax.sharding import Mesh
from jax.sharding import PartitionSpec as P

ADAM_STEP = 10
NOISE = 0.01
CLIP_AT = 0.01
BETA_ONE = 0.9
BETA_TWO = 0.999
ADAM_EPS = 1e-08
DECAY = 0.01
CHUNKS = 2
LANES = 128
SCRATCH = 16 << 20
BIAS_A = 1
BIAS_C = 1
BF = jnp.bfloat16
F32 = jnp.float32
BLK = ("hi", "core")


def adamw_update(weight, moment, second, gradient, step_rate):
    moment = BETA_ONE * moment + (1.0 - BETA_ONE) * gradient
    second = BETA_TWO * second + (1.0 - BETA_TWO) * gradient * gradient
    moment_hat = moment / (1.0 - BETA_ONE**ADAM_STEP)
    second_hat = second / (1.0 - BETA_TWO**ADAM_STEP)
    weight = weight - step_rate * (moment_hat / (jnp.sqrt(second_hat) + ADAM_EPS) + DECAY * weight)
    return (weight, moment, second)


def swap(x, axis, size, mask):
    return lax.ppermute(x, axis, [(i, i ^ mask) for i in range(size)])


def dot(a, b, dims=((1,), (0,))):
    return lax.dot_general(a, b, (dims, ((), ())), preferred_element_type=F32)


def split_low(x):
    high = x.astype(BF)
    return high, (x - high.astype(F32)).astype(BF)


def sine_cosine(x):
    turns = jnp.round(x * 0.6366197723675814)
    rest = x - turns * 1.5703125
    rest = rest - turns * 0.00048351287841796875
    rest = rest - turns * 3.1385570764541626e-07
    rest = rest - turns * 6.077100628276711e-11
    turns = turns.astype(jnp.int32)
    s = rest * rest
    sin_part = rest + rest * s * (-1.6666654611e-1 + s * (8.3321608736e-3 + s * (-1.9515295891e-4)))
    cos_part = 1.0 - 0.5 * s + s * s * (
        4.166664568298827e-2 + s * (-1.388731625493765e-3 + s * 2.443315711809948e-5)
    )
    even = (turns & 1) == 0
    sine = jnp.where(even, sin_part, cos_part)
    cosine = jnp.where(even, cos_part, sin_part)
    sine = jnp.where((turns & 2) == 0, sine, -sine)
    cosine = jnp.where(((turns + 1) & 2) == 0, cosine, -cosine)
    return sine, cosine


def groups_of(size):
    bits = [1 << k for k in range(1, size.bit_length() - 1)]
    if len(bits) < 2:
        return [bits]
    return [[bits[0], bits[1], bits[0] | bits[1]]] + [[b] for b in bits[2:]]


def call(name, body, outs, *args, last=False, weight=1):
    shapes = jax.ShapeDtypeStruct if last else pltpu.VMEM
    return pl.pallas_call(
        body,
        out_shape=[shapes(shape, dtype) for shape, dtype in outs],
        cost_estimate=pl.CostEstimate(flops=weight, transcendentals=0, bytes_accessed=1),
        compiler_params=pltpu.CompilerParams(vmem_limit_bytes=SCRATCH),
        name=name,
    )(*[pltpu.with_memory_space_constraint(x, pltpu.VMEM) for x in args])


def my_half():
    return lax.axis_index("feat")


def turned(x):
    own = x.shape[0] // 2
    core = lax.axis_index("core")
    low, high = x[:own], x[own:]
    return jnp.concatenate(
        [jnp.where(core == 0, low, high), jnp.where(core == 0, high, low)], axis=0
    )


def freq_rows(freq_ref, half, start, count):
    total = freq_ref.shape[0] // 2
    return freq_ref[pl.ds(pl.multiple_of(half * total + start, count), count), :]


def prepare(inputs, width_class, col_mask, masked):
    d_in = inputs.shape[1]
    n_blk = lax.axis_size("hi") * 2
    rows = d_in // n_blk
    classes = col_mask.shape[0]
    me = lax.axis_index("hi") * 2 + lax.axis_index("core")
    chosen = width_class[...] == lax.broadcasted_iota(jnp.int32, (classes, inputs.shape[0]), 0)
    keep_cols = dot(chosen.astype(F32), col_mask[...].astype(F32), ((0,), (0,)))
    plain = inputs[...] * keep_cols.astype(BF)
    tile = min(256, d_in)
    n_bits, shift = n_blk.bit_length() - 1, rows.bit_length() - 1
    for t in range(d_in // tile):
        column = lax.broadcasted_iota(jnp.int32, (1, tile), 1) + t * tile
        place = column >> shift
        source = jnp.zeros_like(place)
        for k in range(n_bits):
            source = source | (((place >> k) & 1) << (n_bits - 1 - k))
        source = ((source ^ me) << shift) | (column & (rows - 1))
        select = lax.broadcasted_iota(jnp.int32, (d_in, tile), 0) == source
        select = jnp.where(select, 1.0, 0.0).astype(BF)
        masked[:, t * tile : (t + 1) * tile] = dot(plain, select).astype(BF)


def hidden_units(masked, held, hidden, damp):
    value = jnp.tanh(dot(masked[...], held[...]))
    hidden[...] = value.astype(BF)
    damp[...] = 1.0 - value * value


def own_pre(first, second, freq, phases, pre):
    width = first.shape[1]
    half = my_half()
    value = dot(first[...], freq_rows(freq, half, 0, width))
    value = value + dot(second[...], freq_rows(freq, half, width, width))
    pre[...] = value + phases[...]


def far_pre(pre, far, freq, out):
    out[...] = pre[...] + dot(far[...], freq_rows(freq, 1 - my_half(), 0, far.shape[1]))


def payload(keep, send, value, scalar):
    own = keep.shape[0]
    n_low = value.shape[1]
    keep[:, :n_low] = value[:own]
    keep[:, n_low:] = jnp.full((own, LANES), scalar, F32)
    send[:, :n_low] = value[own:]
    send[:, n_low:] = jnp.full((own, LANES), scalar, F32)


def make_features(pre, far, freq, alpha, row_mask, features, slope, keep, send):
    width = far.shape[1]
    scale = (2.0 / (pre.shape[1] * lax.axis_size("feat"))) ** 0.5
    angle = pre[...] + dot(far[...], freq_rows(freq, 1 - my_half(), width, width))
    sine, cosine = sine_cosine(angle)
    value = (scale * cosine).astype(BF)
    features[...] = value
    slope[...] = -scale * sine
    moments = dot(turned(alpha[...]).astype(BF), value)
    payload(keep, send, moments, jnp.sum(row_mask[...].astype(F32)))


def fit(mine, other, features, moments, fitted):
    n_low = features.shape[1]
    value = jnp.concatenate([mine[:, :n_low], other[:, :n_low]], axis=0)
    parts = jnp.concatenate(split_low(value), axis=0)
    moments[...] = parts
    both = dot(parts, features[...], ((1,), (1,)))
    samples = value.shape[0]
    fitted[...] = both[:samples] + both[samples:]


def residuals(near, far, mine, alpha, targets, prior, row_mask, features, resid_grad, keep, send):
    samples = alpha.shape[0]
    n_low = features.shape[1]
    true_count = jnp.maximum(mine[0:1, n_low : n_low + 1], 1.0)
    residual = near[...] + far[...] + NOISE * turned(alpha[...]) - targets[...] - turned(prior[...])
    keep_rows = row_mask[...].astype(F32)
    value = (2.0 * keep_rows * residual / (true_count * samples)).astype(BF)
    resid_grad[...] = value
    payload(keep, send, dot(value, features[...]), jnp.sum(keep_rows * residual * residual))


def pre_gradient(mine, other, moments, resid_grad, alpha, slope, freq, back, pre_grad, away):
    n_low = slope.shape[1]
    value = jnp.concatenate([mine[:, :n_low], other[:, :n_low]], axis=0)
    parts = jnp.concatenate(split_low(value), axis=0)
    back[...] = parts
    low = turned(alpha[...]).astype(BF)
    resid = resid_grad[...]
    left = jnp.concatenate([resid, resid, low, low], axis=0)
    right = jnp.concatenate([moments[...], parts], axis=0)
    grad = (slope[...] * dot(left, right, ((0,), (0,)))).astype(BF)
    pre_grad[...] = grad
    away[...] = dot(grad, freq_rows(freq, 1 - my_half(), 0, away.shape[1]), ((1,), (1,))).astype(BF)


def second_away(pre_grad, freq, away):
    width = away.shape[1]
    away[...] = dot(
        pre_grad[...], freq_rows(freq, 1 - my_half(), width, width), ((1,), (1,))
    ).astype(BF)


def own_gradient(pre_grad, freq, back, features, near, pulled):
    near[...] = dot(pre_grad[...], freq_rows(freq, my_half(), 0, near.shape[1]), ((1,), (1,)))
    both = dot(back[...], features[...], ((1,), (1,)))
    samples = pulled.shape[0]
    pulled[...] = both[:samples] + both[samples:]


def weight_terms(part):
    def body(near, got, damp, masked, *refs):
        *pulls, send, keep = refs if len(refs) == 2 else refs[:-1]
        hidden_grad = near[:, part] + got[...].astype(F32)
        first_grad = (damp[...] * hidden_grad).astype(BF)
        mid = send.shape[0]
        send[...] = dot(masked[:, mid:], first_grad, ((0,), (0,))).astype(BF)
        keep[...] = dot(masked[:, :mid], first_grad, ((0,), (0,)))
        if pulls:
            pulled, pulled_far, resid_grad = pulls
            refs[-1][...] = pulled[...] + pulled_far[...] + NOISE * resid_grad[...].astype(F32)

    return body


def add_halves(keep, got, send, rest):
    mid = rest.shape[0]
    send[...] = (keep[mid:] + got[mid:].astype(F32)).astype(BF)
    rest[...] = keep[:mid] + got[:mid].astype(F32)


def finish_gradients(keep, got, *refs):
    *earlier, weight_grad, total = refs
    value = keep[...] + got[...].astype(F32)
    weight_grad[...] = value
    whole = jnp.sum(value * value)
    if earlier:
        alpha_grad, before = earlier
        own = alpha_grad[...]
        whole = whole + before[0, 0] + jnp.where(my_half() == 0, jnp.sum(own * own), 0.0)
    total[...] = jnp.full(total.shape, whole, F32)


def update(*refs):
    spread, squares, *grads = refs[: 2 + CHUNKS]
    alpha_grad, *refs = refs[2 + CHUNKS :]
    weight, moment, second, alpha, alpha_moment, alpha_second = refs[:6]
    norm_out, resid_out = refs[6:8]
    norm = jnp.sqrt(jnp.sum(spread[:, :, 0:1], axis=0))
    norm_out[...] = norm
    last = squares.shape[1] - 1
    resid_out[...] = jnp.sqrt(squares[0:1, last:])
    clip = jnp.minimum(1.0, CLIP_AT / (norm + 1e-06))
    width = weight.shape[1] // CHUNKS
    work = [
        (slice(c * width, (c + 1) * width), (weight, moment, second), grad[...], 0.02, refs[8:12])
        for c, grad in enumerate(grads)
    ]
    held = (alpha, alpha_moment, alpha_second)
    work.append((slice(None), held, turned(alpha_grad[...]), 0.05, refs[12:16]))
    for part, values, grad, rate, outs in work:
        new = adamw_update(*[v[:, part] for v in values], grad * clip, rate)
        for out, value in zip(outs, (*new, new[0].astype(BF))):
            out[:, part] = value


def build(n_blk, n_feat):
    masks = [1 << k for k in range(n_blk.bit_length() - 1)]
    size = n_blk * n_feat

    def sum_over_blk(keep, send):
        keep = keep + swap(send, BLK, n_blk, 1)
        for group in groups_of(n_blk):
            keep = keep + sum(swap(keep, BLK, n_blk, m) for m in group)
        return keep, swap(keep, BLK, n_blk, 1)

    def on_device(
        inputs,
        col_mask,
        row_mask,
        width_class,
        frequencies,
        phases,
        targets,
        prior_draws,
        hidden_weight,
        hidden_moment,
        hidden_second,
        alpha_weight,
        alpha_moment,
        alpha_second,
    ):
        d_in = col_mask.shape[1]
        points, samples = alpha_weight.shape
        n_low = frequencies.shape[1]
        h_own = hidden_weight.shape[1]
        width = h_own // CHUNKS
        row_mask, width_class, phases, targets = (
            x.reshape(1, -1) for x in (row_mask, width_class, phases, targets)
        )
        alpha, prior = alpha_weight.T, prior_draws.T

        low = hidden_weight.astype(BF)
        (masked,) = call(
            "prepare", prepare, [((points, d_in), BF)], inputs, width_class, col_mask
        )
        units = [((points, width), BF), ((points, width), F32)]
        hidden, damps = [], []
        for c in range(CHUNKS):
            held = low[:, c * width : (c + 1) * width]
            for m in reversed(masks):
                held = jnp.concatenate([held, swap(held, BLK, n_blk, m)], axis=0)
            unit, damp = call("hidden", hidden_units, units, masked, held)
            hidden.append(unit)
            damps.append(damp)
        fars = [swap(h, "feat", n_feat, 1) for h in hidden]
        wide = ((points, n_low), F32)
        (pre,) = call("own_pre", own_pre, [wide], *hidden, frequencies, phases)
        (pre,) = call("far_pre", far_pre, [wide], pre, fars[0], frequencies, weight=BIAS_A)
        pair = [((samples // 2, n_low + LANES), F32)] * 2
        features, slope, keep, send = call(
            "features",
            make_features,
            [((points, n_low), BF), wide, *pair],
            pre,
            fars[1],
            frequencies,
            alpha,
            row_mask,
        )
        mine, other = sum_over_blk(keep, send)
        parts = ((2 * samples, n_low), BF)
        thin = ((samples, points), F32)
        moments, fitted = call("fit", fit, [parts, thin], mine, other, features)
        fitted_far = swap(fitted, "feat", n_feat, 1)
        resid_grad, keep, send = call(
            "residuals",
            residuals,
            [((samples, points), BF), *pair],
            fitted,
            fitted_far,
            mine,
            alpha,
            targets,
            prior,
            row_mask,
            features,
        )
        mine, other = sum_over_blk(keep, send)
        away = ((points, width), BF)
        back, pre_grad, first = call(
            "pre_gradient",
            pre_gradient,
            [parts, ((points, n_low), BF), away],
            mine,
            other,
            moments,
            resid_grad,
            alpha,
            slope,
            frequencies,
        )
        gots = [swap(first, "feat", n_feat, 1)]
        (second,) = call("second_away", second_away, [away], pre_grad, frequencies)
        gots.append(swap(second, "feat", n_feat, 1))
        near, pulled = call(
            "own_gradient",
            own_gradient,
            [((points, h_own), F32), thin],
            pre_grad,
            frequencies,
            back,
            features,
        )
        pulled_far = swap(pulled, "feat", n_feat, 1)

        grads, totals = [], []
        for c in range(CHUNKS):
            mid = d_in // 2
            shapes = [((mid, width), BF), ((mid, width), F32)]
            part = slice(c * width, (c + 1) * width)
            operands = [near, gots[c], damps[c], masked]
            if c == CHUNKS - 1:
                operands += [pulled, pulled_far, resid_grad]
                shapes = shapes + [thin]
            send, keep, *alpha_grad = call("weight_terms", weight_terms(part), shapes, *operands)
            for m in masks[:-1]:
                got = swap(send, BLK, n_blk, m)
                mid = mid // 2
                shapes = [((mid, width), BF), ((mid, width), F32)]
                send, keep = call("add_halves", add_halves, shapes, keep, got)
            got = swap(send, BLK, n_blk, masks[-1])
            last = c == CHUNKS - 1
            outs = [((mid, width), F32), ((size, 1, LANES) if last else (1, LANES), F32)]
            grad, total = call(
                "finish",
                finish_gradients,
                outs,
                keep,
                got,
                *alpha_grad,
                *totals,
                weight=1 if last else BIAS_C,
            )
            grads.append(grad)
            totals = [total]
        (spread,) = totals
        spread = lax.all_to_all(spread, (*BLK, "feat"), 0, 0, tiled=True)
        scalar = ((1, 1), F32)
        big, small = hidden_weight.shape, (samples, points)
        outs = call(
            "update",
            update,
            [scalar, scalar]
            + [(big, F32)] * 3
            + [(big, BF)]
            + [(small, F32)] * 3
            + [(small, BF)],
            spread,
            mine,
            *grads,
            *alpha_grad,
            hidden_weight,
            hidden_moment,
            hidden_second,
            alpha,
            alpha_moment.T,
            alpha_second.T,
            last=True,
        )
        norm, resid = outs[:2]
        return (norm[0, 0], resid[0, 0], *outs[2:6], *[x.T for x in outs[6:]])

    return on_device


def solution(mesh):
    in_specs = (
        P(BLK, None),
        P(),
        P(BLK),
        P(BLK),
        P(None, "feat"),
        P("feat"),
        P(BLK),
        P(BLK, None),
        P(BLK, "feat"),
        P(BLK, "feat"),
        P(BLK, "feat"),
        P(BLK, None),
        P(BLK, None),
        P(BLK, None),
    )
    out_specs = (
        P(),
        P(),
        P(BLK, "feat"),
        P(BLK, "feat"),
        P(BLK, "feat"),
        P(BLK, "feat"),
        P(BLK, None),
        P(BLK, None),
        P(BLK, None),
        P(BLK, None),
    )
    n_blk, n_feat = mesh.shape["blk"], mesh.shape["feat"]
    inner = Mesh(mesh.devices.reshape(n_blk // 2, 2, n_feat), (*BLK, "feat"))
    on_device = build(n_blk, n_feat)
    return jax.shard_map(
        on_device, mesh=inner, in_specs=in_specs, out_specs=out_specs, check_vma=False
    )
```

time: 158 us -> 136 us (0.86)
  other arithmetic: 20.6 us -> 1.14 us
  matrix products: 15.7 us -> 0 us
  blocking collectives: 0 us -> 13.9 us
  Pallas kernels: 0 us -> 10.4 us
  between operations: 6.9 us -> 1.05 us
  waiting for transfers between devices: 67.3 us -> 62.8 us
  local copies, waits for them, and re-layouts: 6.03 us -> 2.64 us
  starting transfers between devices: 40.5 us -> 43.8 us
    dot_general x20 -> x0, matrix products: 15.7 us -> none  [the longest x19 13.4 us: dot(): return lax.dot_general(a, b, (dims, ((), ())), preferred_element_type=F32)]
    all_to_all x0 -> x1, blocking collectives: none -> 13.9 us  [on_device(): spread = lax.all_to_all(spread, (*BLK, 'feat'), 0, 0, tiled=True)]
    pallas_call x0 -> x22, Pallas kernels: none -> 10.4 us  [call(): pl.pallas_call(body, out_shape=[shapes(shape, dtype) for shape, dtype in...]
    add x15 -> x6, other arithmetic: 9.33 us -> 0.05 us  [the longest x4 0.04 us: sum_over_blk(): keep = keep + sum((swap(keep, BLK, n_blk, m) for m in group))]
    ppermute x32 -> x34, starting transfers between devices: 37.1 us -> 43.8 us  [swap(): return lax.ppermute(x, axis, [(i, i ^ mask) for i in range(size)])]
    all_to_all x1 -> x0, waiting for transfers between devices: 5.94 us -> none  [on_device(): spread = lax.all_to_all(spread, ('blk', 'feat'), 0, 0, tiled=True)]
    gather x10 -> x0, other arithmetic: 4.74 us -> none  [on_device(): (jnp.asarray(order, jnp.int32) ^ me)[column // rows] * rows + column % rows]
    all_to_all x1 -> x0, starting transfers between devices: 3.36 us -> none  [on_device(): spread = lax.all_to_all(spread, ('blk', 'feat'), 0, 0, tiled=True)]
  transfers between devices with their start and end apart: 33 -> 34, of which waited for: 23 -> 28; matrix products, arithmetic and copies ran while one was open for 19% -> 0% of each run, Pallas kernels for 0% -> 4%
where the time goes in v2:
time: 136 us
  waiting for transfers between devices  62.8 us (46%)
  starting transfers between devices  43.8 us (32%)
  blocking collectives  13.9 us (10%)
  Pallas kernels  10.4 us (8%)
  local copies, waits for them, and re-layouts  2.64 us (2%)
    ppermute x34, waiting for transfers between devices, swap(): return lax.ppermute(x, axis, [(i, i ^ mask) for i in range(size)])  62.8 us
    ppermute x34, starting transfers between devices, swap(): return lax.ppermute(x, axis, [(i, i ^ mask) for i in range(size)])  43.8 us
    all_to_all x1, blocking collectives, on_device(): spread = lax.all_to_all(spread, (*BLK, 'feat'), 0, 0, tiled=True)  13.9 us
    pallas_call x22, Pallas kernels, call(): pl.pallas_call(body, out_shape=[shapes(shape, dtype) for shape, dtype in...  10.4 us
  transfers between devices with their start and end apart: 34, of which 28 were waited for; matrix products, arithmetic and copies ran while one was open for 0% of the time, Pallas kernels for 4%

profile of v2, /device:TPU:0, one launch (start us, length us, event | category | flops | bytes accessed | tf_op | source)
XLA Modules:
  0.0 135.8 jit_solution(2212788405176227651)
XLA Ops:
  0.6 1.0 convert_element_type.3
  1.6 4.1 %collective-permute-start = (bf16[64,512]{1,0:T(8,128)(2,1)S(1)}, bf16[64,512]{1,0:T(8,128)(2,1)S(1)}, u32[]{:S(2)}, u32[]{:S(2)}) collective-permute-start(bf16[64,512]{1,0:T(8,128)(2,1)S(1)} %get-tuple-element.111), channel_id=1, source_target_pairs={{0,16},{2,18},{4,20},{6,22},{8,24},{10,26},{12,28},{14,30},{16,0},... | collective-permute-start | bytes 196616 | tf_op jit(solution)/shard_map/ppermute | solution.py:36
  5.8 3.6 %collective-permute-done = bf16[64,512]{1,0:T(8,128)(2,1)S(1)} collective-permute-done((bf16[64,512]{1,0:T(8,128)(2,1)S(1)}, bf16[64,512]{1,0:T(8,128)(2,1)S(1)}, u32[]{:S(2)}, u32[]{:S(2)}) %collective-permute-start) | collective-permute-done | bytes 65568 | tf_op jit(solution)/shard_map/ppermute | solution.py:36
  9.5 2.1 %collective-permute-start.1 = (bf16[128,512]{1,0:T(8,128)(2,1)S(1)}, bf16[128,512]{1,0:T(8,128)(2,1)S(1)}, u32[]{:S(2)}, u32[]{:S(2)}) collective-permute-start(bf16[128,512]{1,0:T(8,128)(2,1)S(1)} %pad_maximum_fusion.4), channel_id=1, source_target_pairs={{0,8},{2,10},{4,12},{6,14},{8,0},{10,2},{12,4},{14,6},{16,24},{18,... | collective-permute-start | bytes 393224 | tf_op jit(solution)/shard_map/ppermute | solution.py:36
  12.9 3.1 %collective-permute-done.1 = bf16[128,512]{1,0:T(8,128)(2,1)S(1)} collective-permute-done((bf16[128,512]{1,0:T(8,128)(2,1)S(1)}, bf16[128,512]{1,0:T(8,128)(2,1)S(1)}, u32[]{:S(2)}, u32[]{:S(2)}) %collective-permute-start.1) | collective-permute-done | bytes 131104 | tf_op jit(solution)/shard_map/ppermute | solution.py:36
  16.0 1.2 collective-permute-start.2
  17.1 1.0 copy-done.2
  19.6 1.0 prepare.1.masked
  20.6 1.0 collective-permute-start.6
  21.6 2.2 %collective-permute-done.2 = bf16[256,512]{1,0:T(8,128)(2,1)S(1)} collective-permute-done((bf16[256,512]{1,0:T(8,128)(2,1)S(1)}, bf16[256,512]{1,0:T(8,128)(2,1)S(1)}, u32[]{:S(2)}, u32[]{:S(2)}) %collective-permute-start.2) | collective-permute-done | bytes 262176 | tf_op jit(solution)/shard_map/ppermute | solution.py:36
  24.0 4.4 %collective-permute-done.6 = bf16[256,512]{1,0:T(8,128)(2,1)S(1)} collective-permute-done((bf16[256,512]{1,0:T(8,128)(2,1)S(1)}, bf16[256,512]{1,0:T(8,128)(2,1)S(1)}, u32[]{:S(2)}, u32[]{:S(2)}) %collective-permute-start.6) | collective-permute-done | bytes 262176 | tf_op jit(solution)/shard_map/ppermute | solution.py:36
  29.1 1.3 collective-permute-done.7
  30.5 1.3 collective-permute-start.8
  33.8 5.9 %collective-permute-done.8.far = bf16[256,512]{1,0:T(8,128)(2,1)S(1)} collective-permute-done((bf16[256,512]{1,0:T(8,128)(2,1)S(1)}, bf16[256,512]{1,0:T(8,128)(2,1)S(1)}, u32[]{:S(2)}, u32[]{:S(2)}) %collective-permute-start.8) | collective-permute-done | bytes 262176 | tf_op jit(solution)/shard_map/ppermute | solution.py:36
  40.2 4.3 %collective-permute-done.9.far = bf16[256,512]{1,0:T(8,128)(2,1)S(1)} collective-permute-done((bf16[256,512]{1,0:T(8,128)(2,1)S(1)}, bf16[256,512]{1,0:T(8,128)(2,1)S(1)}, u32[]{:S(2)}, u32[]{:S(2)}) %collective-permute-start.9) | collective-permute-done | bytes 262176 | tf_op jit(solution)/shard_map/ppermute | solution.py:36
  44.5 2.0 %features.1 = (bf16[256,1024]{1,0:T(8,128)(2,1)S(1)}, f32[256,1024]{1,0:T(8,128)S(1)}, f32[8,1152]{1,0:T(8,128)S(1)}, f32[8,1152]{1,0:T(8,128)S(1)}) custom-call(f32[256,1024]{1,0:T(8,128)S(1)} %far_pre.1.pre, bf16[256,512]{1,0:T(8,128)(2,1)S(1)} %collective-permute-done.9.far, bf16[2048,1024]{1,0:T(8,128)(2,1)S(1)} %copy-done, f32[16,256]{1,0:T(8,128)S(1)} %bitcast.14, ...), custom_call_target="tpu_custom_call" | custom-call | flops 1 | bytes 1 | tf_op jit(solution)/shard_map/features/pallas_call | solution.py:77
  46.5 1.2 collective-permute-done.10
  47.7 2.6 %collective-permute-start.13 = (f32[8,1152]{1,0:T(8,128)S(1)}, f32[8,1152]{1,0:T(8,128)S(1)}, u32[]{:S(2)}, u32[]{:S(2)}) collective-permute-start(f32[8,1152]{1,0:T(8,128)S(1)} %add.30), channel_id=1, source_target_pairs={{0,12},{2,14},{4,8},{6,10},{8,4},{10,6},{12,0},{14,2},{16,28},{18,... | collective-permute-start | bytes 110600 | tf_op jit(solution)/shard_map/ppermute | solution.py:36
  51.2 1.4 %collective-permute-done.13 = f32[8,1152]{1,0:T(8,128)S(1)} collective-permute-done((f32[8,1152]{1,0:T(8,128)S(1)}, f32[8,1152]{1,0:T(8,128)S(1)}, u32[]{:S(2)}, u32[]{:S(2)}) %collective-permute-start.13) | collective-permute-done | bytes 36896 | tf_op jit(solution)/shard_map/ppermute | solution.py:36
  52.6 1.7 %collective-permute-done.11 = f32[8,1152]{1,0:T(8,128)S(1)} collective-permute-done((f32[8,1152]{1,0:T(8,128)S(1)}, f32[8,1152]{1,0:T(8,128)S(1)}, u32[]{:S(2)}, u32[]{:S(2)}) %collective-permute-start.11) | collective-permute-done | bytes 36896 | tf_op jit(solution)/shard_map/ppermute | solution.py:36
  54.8 3.4 %collective-permute-start.14 = (f32[8,1152]{1,0:T(8,128)S(1)}, f32[8,1152]{1,0:T(8,128)S(1)}, u32[]{:S(2)}, u32[]{:S(2)}) collective-permute-start(f32[8,1152]{1,0:T(8,128)S(1)} %add_add_fusion.1), channel_id=1, source_target_pairs={{0,16},{2,18},{4,20},{6,22},{8,24},{10,26},{12,28},{14,30},{16,0},... | collective-permute-start | bytes 110600 | tf_op jit(solution)/shard_map/ppermute | solution.py:36
  58.2 2.2 %collective-permute-done.14 = f32[8,1152]{1,0:T(8,128)S(1)} collective-permute-done((f32[8,1152]{1,0:T(8,128)S(1)}, f32[8,1152]{1,0:T(8,128)S(1)}, u32[]{:S(2)}, u32[]{:S(2)}) %collective-permute-start.14) | collective-permute-done | bytes 36896 | tf_op jit(solution)/shard_map/ppermute | solution.py:36
  60.4 1.2 collective-permute-done.15.other
  61.9 1.6 %collective-permute-start.16 = (f32[16,256]{1,0:T(8,128)S(1)}, f32[16,256]{1,0:T(8,128)S(1)}, u32[]{:S(2)}, u32[]{:S(2)}) collective-permute-start(f32[16,256]{1,0:T(8,128)S(1)} %get-tuple-element.64.near), channel_id=1, source_target_pairs={{0,1},{1,0},{2,3},{3,2},{4,5},{5,4},{6,7},{7,6},{8,9},{9,8},{10,11... | collective-permute-start | bytes 49160 | tf_op jit(solution)/shard_map/ppermute | solution.py:36
  63.4 2.2 %collective-permute-done.16.far = f32[16,256]{1,0:T(8,128)S(1)} collective-permute-done((f32[16,256]{1,0:T(8,128)S(1)}, f32[16,256]{1,0:T(8,128)S(1)}, u32[]{:S(2)}, u32[]{:S(2)}) %collective-permute-start.16) | collective-permute-done | bytes 16416 | tf_op jit(solution)/shard_map/ppermute | solution.py:36
  65.9 1.2 collective-permute-done.17
  67.1 1.1 collective-permute-start.20
  68.8 1.8 %collective-permute-start.19 = (f32[8,1152]{1,0:T(8,128)S(1)}, f32[8,1152]{1,0:T(8,128)S(1)}, u32[]{:S(2)}, u32[]{:S(2)}) collective-permute-start(f32[8,1152]{1,0:T(8,128)S(1)} %add.35), channel_id=1, source_target_pairs={{0,8},{2,10},{4,12},{6,14},{8,0},{10,2},{12,4},{14,6},{16,24},{18,... | collective-permute-start | bytes 110600 | tf_op jit(solution)/shard_map/ppermute | solution.py:36
  70.6 1.4 %collective-permute-done.20 = f32[8,1152]{1,0:T(8,128)S(1)} collective-permute-done((f32[8,1152]{1,0:T(8,128)S(1)}, f32[8,1152]{1,0:T(8,128)S(1)}, u32[]{:S(2)}, u32[]{:S(2)}) %collective-permute-start.20) | collective-permute-done | bytes 36896 | tf_op jit(solution)/shard_map/ppermute | solution.py:36
  72.8 3.0 %collective-permute-start.21 = (f32[8,1152]{1,0:T(8,128)S(1)}, f32[8,1152]{1,0:T(8,128)S(1)}, u32[]{:S(2)}, u32[]{:S(2)}) collective-permute-start(f32[8,1152]{1,0:T(8,128)S(1)} %add_add_fusion), channel_id=1, source_target_pairs={{0,16},{2,18},{4,20},{6,22},{8,24},{10,26},{12,28},{14,30},{16,0},... | collective-permute-start | bytes 110600 | tf_op jit(solution)/shard_map/ppermute | solution.py:36
  75.7 2.0 %collective-permute-done.21 = f32[8,1152]{1,0:T(8,128)S(1)} collective-permute-done((f32[8,1152]{1,0:T(8,128)S(1)}, f32[8,1152]{1,0:T(8,128)S(1)}, u32[]{:S(2)}, u32[]{:S(2)}) %collective-permute-start.21) | collective-permute-done | bytes 36896 | tf_op jit(solution)/shard_map/ppermute | solution.py:36
  77.7 1.2 collective-permute-done.22.other
  79.5 1.6 %collective-permute-start.29 = (bf16[256,512]{1,0:T(8,128)(2,1)S(1)}, bf16[256,512]{1,0:T(8,128)(2,1)S(1)}, u32[]{:S(2)}, u32[]{:S(2)}) collective-permute-start(bf16[256,512]{1,0:T(8,128)(2,1)S(1)} %get-tuple-element.84), channel_id=1, source_target_pairs={{0,1},{1,0},{2,3},{3,2},{4,5},{5,4},{6,7},{7,6},{8,9},{9,8},{10,11... | collective-permute-start | bytes 786440 | tf_op jit(solution)/shard_map/ppermute | solution.py:36
  82.2 0.8 own_gradient.1
  83.0 1.6 %collective-permute-start.24 = (f32[16,256]{1,0:T(8,128)S(1)}, f32[16,256]{1,0:T(8,128)S(1)}, u32[]{:S(2)}, u32[]{:S(2)}) collective-permute-start(f32[16,256]{1,0:T(8,128)S(1)} %get-tuple-element.74.refs_0_), channel_id=1, source_target_pairs={{0,1},{1,0},{2,3},{3,2},{4,5},{5,4},{6,7},{7,6},{8,9},{9,8},{10,11... | collective-permute-start | bytes 49160 | tf_op jit(solution)/shard_map/ppermute | solution.py:36
  84.6 4.2 %collective-permute-done.29.got = bf16[256,512]{1,0:T(8,128)(2,1)S(1)} collective-permute-done((bf16[256,512]{1,0:T(8,128)(2,1)S(1)}, bf16[256,512]{1,0:T(8,128)(2,1)S(1)}, u32[]{:S(2)}, u32[]{:S(2)}) %collective-permute-start.29) | collective-permute-done | bytes 262176 | tf_op jit(solution)/shard_map/ppermute | solution.py:36
  89.4 4.6 %collective-permute-done.24.refs_1_ = f32[16,256]{1,0:T(8,128)S(1)} collective-permute-done((f32[16,256]{1,0:T(8,128)S(1)}, f32[16,256]{1,0:T(8,128)S(1)}, u32[]{:S(2)}, u32[]{:S(2)}) %collective-permute-start.24) | collective-permute-done | bytes 16416 | tf_op jit(solution)/shard_map/ppermute | solution.py:36
  94.7 1.5 %collective-permute-start.31 = (bf16[256,512]{1,0:T(8,128)(2,1)S(1)}, bf16[256,512]{1,0:T(8,128)(2,1)S(1)}, u32[]{:S(2)}, u32[]{:S(2)}) collective-permute-start(bf16[256,512]{1,0:T(8,128)(2,1)S(1)} %get-tuple-element.89), channel_id=1, source_target_pairs={{0,4},{2,6},{4,0},{6,2},{8,12},{10,14},{12,8},{14,10},{16,20},{18,... | collective-permute-start | bytes 786440 | tf_op jit(solution)/shard_map/ppermute | solution.py:36
  96.6 1.5 %collective-permute-start.26 = (bf16[256,512]{1,0:T(8,128)(2,1)S(1)}, bf16[256,512]{1,0:T(8,128)(2,1)S(1)}, u32[]{:S(2)}, u32[]{:S(2)}) collective-permute-start(bf16[256,512]{1,0:T(8,128)(2,1)S(1)} %get-tuple-element.78), channel_id=1, source_target_pairs={{0,4},{2,6},{4,0},{6,2},{8,12},{10,14},{12,8},{14,10},{16,20},{18,... | collective-permute-start | bytes 786440 | tf_op jit(solution)/shard_map/ppermute | solution.py:36
  98.1 5.8 %collective-permute-done.31.got = bf16[256,512]{1,0:T(8,128)(2,1)S(1)} collective-permute-done((bf16[256,512]{1,0:T(8,128)(2,1)S(1)}, bf16[256,512]{1,0:T(8,128)(2,1)S(1)}, u32[]{:S(2)}, u32[]{:S(2)}) %collective-permute-start.31) | collective-permute-done | bytes 262176 | tf_op jit(solution)/shard_map/ppermute | solution.py:36
  104.0 1.9 %collective-permute-start.32 = (bf16[128,512]{1,0:T(8,128)(2,1)S(1)}, bf16[128,512]{1,0:T(8,128)(2,1)S(1)}, u32[]{:S(2)}, u32[]{:S(2)}) collective-permute-start(bf16[128,512]{1,0:T(8,128)(2,1)S(1)} %get-tuple-element.91), channel_id=1, source_target_pairs={{0,8},{2,10},{4,12},{6,14},{8,0},{10,2},{12,4},{14,6},{16,24},{18,... | collective-permute-start | bytes 393224 | tf_op jit(solution)/shard_map/ppermute | solution.py:36
  105.9 3.2 %collective-permute-done.26.got = bf16[256,512]{1,0:T(8,128)(2,1)S(1)} collective-permute-done((bf16[256,512]{1,0:T(8,128)(2,1)S(1)}, bf16[256,512]{1,0:T(8,128)(2,1)S(1)}, u32[]{:S(2)}, u32[]{:S(2)}) %collective-permute-start.26) | collective-permute-done | bytes 262176 | tf_op jit(solution)/shard_map/ppermute | solution.py:36
  109.1 1.9 %collective-permute-start.27 = (bf16[128,512]{1,0:T(8,128)(2,1)S(1)}, bf16[128,512]{1,0:T(8,128)(2,1)S(1)}, u32[]{:S(2)}, u32[]{:S(2)}) collective-permute-start(bf16[128,512]{1,0:T(8,128)(2,1)S(1)} %get-tuple-element.80), channel_id=1, source_target_pairs={{0,8},{2,10},{4,12},{6,14},{8,0},{10,2},{12,4},{14,6},{16,24},{18,... | collective-permute-start | bytes 393224 | tf_op jit(solution)/shard_map/ppermute | solution.py:36
  111.1 3.0 %collective-permute-start.33 = (bf16[64,512]{1,0:T(8,128)(2,1)S(1)}, bf16[64,512]{1,0:T(8,128)(2,1)S(1)}, u32[]{:S(2)}, u32[]{:S(2)}) collective-permute-start(bf16[64,512]{1,0:T(8,128)(2,1)S(1)} %get-tuple-element.93), channel_id=1, source_target_pairs={{0,16},{2,18},{4,20},{6,22},{8,24},{10,26},{12,28},{14,30},{16,0},... | collective-permute-start | bytes 196616 | tf_op jit(solution)/shard_map/ppermute | solution.py:36
  114.4 3.7 %collective-permute-start.28 = (bf16[64,512]{1,0:T(8,128)(2,1)S(1)}, bf16[64,512]{1,0:T(8,128)(2,1)S(1)}, u32[]{:S(2)}, u32[]{:S(2)}) collective-permute-start(bf16[64,512]{1,0:T(8,128)(2,1)S(1)} %get-tuple-element.82), channel_id=1, source_target_pairs={{0,16},{2,18},{4,20},{6,22},{8,24},{10,26},{12,28},{14,30},{16,0},... | collective-permute-start | bytes 196616 | tf_op jit(solution)/shard_map/ppermute | solution.py:36
  118.2 2.3 %collective-permute-done.28.got = bf16[64,512]{1,0:T(8,128)(2,1)S(1)} collective-permute-done((bf16[64,512]{1,0:T(8,128)(2,1)S(1)}, bf16[64,512]{1,0:T(8,128)(2,1)S(1)}, u32[]{:S(2)}, u32[]{:S(2)}) %collective-permute-start.28) | collective-permute-done | bytes 65568 | tf_op jit(solution)/shard_map/ppermute | solution.py:36
  120.6 13.9 %all_to_all.5.refs_0_ = f32[32,1,128]{2,1,0:T(1,128)S(1)} all-to-all(f32[32,1,128]{2,1,0:T(1,128)S(1)} %get-tuple-element.95), channel_id=1, replica_groups=mesh['hi'=8,'core'=2,'feat'=2] {'hi','core','feat'}, dimensions={0} | all-to-all | bytes 32768 | tf_op jit(solution)/shard_map/all_to_all | solution.py:412
  134.6 1.2 update.1
  (93 shorter events, 13.5 us)
Async XLA Ops:
  1.6 7.8 %collective-permute-start = (bf16[64,512]{1,0:T(8,128)(2,1)S(1)}, bf16[64,512]{1,0:T(8,128)(2,1)S(1)}, u32[]{:S(2)}, u32[]{:S(2)}) collective-permute-start(bf16[64,512]{1,0:T(8,128)(2,1)S(1)} %get-tuple-element.111), channel_id=1, source_target_pairs={{0,16},{2,18},{4,20},{6,22},{8,24},{10,26},{12,28},{14,30},{16,0},... | collective-permute-start | bytes 196616 | tf_op jit(solution)/shard_map/ppermute | solution.py:36
  5.8 6.5 %collective-permute-start.4 = (bf16[64,512]{1,0:T(8,128)(2,1)S(1)}, bf16[64,512]{1,0:T(8,128)(2,1)S(1)}, u32[]{:S(2)}, u32[]{:S(2)}) collective-permute-start(bf16[64,512]{1,0:T(8,128)(2,1)S(1)} %get-tuple-element.108), channel_id=1, source_target_pairs={{0,16},{2,18},{4,20},{6,22},{8,24},{10,26},{12,28},{14,30},{16,0},... | collective-permute-start | bytes 196616 | tf_op jit(solution)/shard_map/ppermute | solution.py:36
  9.5 6.4 %collective-permute-start.1 = (bf16[128,512]{1,0:T(8,128)(2,1)S(1)}, bf16[128,512]{1,0:T(8,128)(2,1)S(1)}, u32[]{:S(2)}, u32[]{:S(2)}) collective-permute-start(bf16[128,512]{1,0:T(8,128)(2,1)S(1)} %pad_maximum_fusion.4), channel_id=1, source_target_pairs={{0,8},{2,10},{4,12},{6,14},{8,0},{10,2},{12,4},{14,6},{16,24},{18,... | collective-permute-start | bytes 393224 | tf_op jit(solution)/shard_map/ppermute | solution.py:36
  12.2 8.4 %collective-permute-start.5 = (bf16[128,512]{1,0:T(8,128)(2,1)S(1)}, bf16[128,512]{1,0:T(8,128)(2,1)S(1)}, u32[]{:S(2)}, u32[]{:S(2)}) collective-permute-start(bf16[128,512]{1,0:T(8,128)(2,1)S(1)} %pad_maximum_fusion.5), channel_id=1, source_target_pairs={{0,8},{2,10},{4,12},{6,14},{8,0},{10,2},{12,4},{14,6},{16,24},{18,... | collective-permute-start | bytes 393224 | tf_op jit(solution)/shard_map/ppermute | solution.py:36
  16.0 7.9 %collective-permute-start.2 = (bf16[256,512]{1,0:T(8,128)(2,1)S(1)}, bf16[256,512]{1,0:T(8,128)(2,1)S(1)}, u32[]{:S(2)}, u32[]{:S(2)}) collective-permute-start(bf16[256,512]{1,0:T(8,128)(2,1)S(1)} %pad_maximum_fusion.2), channel_id=1, source_target_pairs={{0,4},{2,6},{4,0},{6,2},{8,12},{10,14},{12,8},{14,10},{16,20},{18,... | collective-permute-start | bytes 786440 | tf_op jit(solution)/shard_map/ppermute | solution.py:36
  17.1 1.0 copy-start.2
  18.2 0.7 copy-start.9
  18.9 0.7 copy-start.12
  20.6 7.8 %collective-permute-start.6 = (bf16[256,512]{1,0:T(8,128)(2,1)S(1)}, bf16[256,512]{1,0:T(8,128)(2,1)S(1)}, u32[]{:S(2)}, u32[]{:S(2)}) collective-permute-start(bf16[256,512]{1,0:T(8,128)(2,1)S(1)} %pad_maximum_fusion.3), channel_id=1, source_target_pairs={{0,4},{2,6},{4,0},{6,2},{8,12},{10,14},{12,8},{14,10},{16,20},{18,... | collective-permute-start | bytes 786440 | tf_op jit(solution)/shard_map/ppermute | solution.py:36
  23.9 9.2 %copy-start = (bf16[2048,1024]{1,0:T(8,128)(2,1)S(1)}, bf16[2048,1024]{1,0:T(8,128)(2,1)}, u32[]{:S(2)}) copy-start(bf16[2048,1024]{1,0:T(8,128)(2,1)} %freq.11) | copy-start | bytes 12582916
  23.9 9.2 %copy-start.10 = (f32[1024]{0:T(1024)S(1)}, f32[1024]{0:T(1024)}, u32[]{:S(2)}) copy-start(f32[1024]{0:T(1024)} %param.19) | copy-start | bytes 12292
  23.9 4.7 %collective-permute-start.3 = (bf16[512,512]{1,0:T(8,128)(2,1)S(1)}, bf16[512,512]{1,0:T(8,128)(2,1)S(1)}, u32[]{:S(2)}, u32[]{:S(2)}) collective-permute-start(bf16[512,512]{1,0:T(8,128)(2,1)S(1)} %pad_maximum_fusion), channel_id=1, source_target_pairs={{0,2},{2,0},{4,6},{6,4},{8,10},{10,8},{12,14},{14,12},{16,18},{18,... | collective-permute-start | bytes 1572872 | tf_op jit(solution)/shard_map/ppermute | solution.py:36
  28.4 2.0 %collective-permute-start.7 = (bf16[512,512]{1,0:T(8,128)(2,1)S(1)}, bf16[512,512]{1,0:T(8,128)(2,1)S(1)}, u32[]{:S(2)}, u32[]{:S(2)}) collective-permute-start(bf16[512,512]{1,0:T(8,128)(2,1)S(1)} %pad_maximum_fusion.1), channel_id=1, source_target_pairs={{0,2},{2,0},{4,6},{6,4},{8,10},{10,8},{12,14},{14,12},{16,18},{18,... | collective-permute-start | bytes 1572872 | tf_op jit(solution)/shard_map/ppermute | solution.py:36
  30.5 9.2 %collective-permute-start.8 = (bf16[256,512]{1,0:T(8,128)(2,1)S(1)}, bf16[256,512]{1,0:T(8,128)(2,1)S(1)}, u32[]{:S(2)}, u32[]{:S(2)}) collective-permute-start(bf16[256,512]{1,0:T(8,128)(2,1)S(1)} %get-tuple-element.59.first), channel_id=1, source_target_pairs={{0,1},{1,0},{2,3},{3,2},{4,5},{5,4},{6,7},{7,6},{8,9},{9,8},{10,11... | collective-permute-start | bytes 786440 | tf_op jit(solution)/shard_map/ppermute | solution.py:36
  32.3 12.2 %collective-permute-start.9 = (bf16[256,512]{1,0:T(8,128)(2,1)S(1)}, bf16[256,512]{1,0:T(8,128)(2,1)S(1)}, u32[]{:S(2)}, u32[]{:S(2)}) collective-permute-start(bf16[256,512]{1,0:T(8,128)(2,1)S(1)} %get-tuple-element.60.second), channel_id=1, source_target_pairs={{0,1},{1,0},{2,3},{3,2},{4,5},{5,4},{6,7},{7,6},{8,9},{9,8},{10,11... | collective-permute-start | bytes 786440 | tf_op jit(solution)/shard_map/ppermute | solution.py:36
  33.8 10.7 %copy-start.3 = (f32[256,16]{0,1:T(8,128)S(1)}, f32[256,16]{0,1:T(8,128)}, u32[]{:S(2)}) copy-start(f32[256,16]{0,1:T(8,128)} %param.25) | copy-start | bytes 49156
  33.8 10.7 %copy-start.11 = (s32[256]{0:T(256)S(1)}, s32[256]{0:T(256)}, u32[]{:S(2)}) copy-start(s32[256]{0:T(256)} %param.16) | copy-start | bytes 3076
  40.1 25.5 %copy-start.8 = (f32[256,16]{0,1:T(8,128)S(1)}, f32[256,16]{0,1:T(8,128)}, u32[]{:S(2)}) copy-start(f32[256,16]{0,1:T(8,128)} %param.21) | copy-start | bytes 49156
  40.2 25.5 %copy-start.13 = (f32[256]{0:T(256)S(1)}, f32[256]{0:T(256)}, u32[]{:S(2)}) copy-start(f32[256]{0:T(256)} %param.20) | copy-start | bytes 3076
  46.5 1.3 collective-permute-start.10
  47.7 4.9 %collective-permute-start.13 = (f32[8,1152]{1,0:T(8,128)S(1)}, f32[8,1152]{1,0:T(8,128)S(1)}, u32[]{:S(2)}, u32[]{:S(2)}) collective-permute-start(f32[8,1152]{1,0:T(8,128)S(1)} %add.30), channel_id=1, source_target_pairs={{0,12},{2,14},{4,8},{6,10},{8,4},{10,6},{12,0},{14,2},{16,28},{18,... | collective-permute-start | bytes 110600 | tf_op jit(solution)/shard_map/ppermute | solution.py:36
  50.3 4.0 %collective-permute-start.11 = (f32[8,1152]{1,0:T(8,128)S(1)}, f32[8,1152]{1,0:T(8,128)S(1)}, u32[]{:S(2)}, u32[]{:S(2)}) collective-permute-start(f32[8,1152]{1,0:T(8,128)S(1)} %add.30), channel_id=1, source_target_pairs={{0,4},{2,6},{4,0},{6,2},{8,12},{10,14},{12,8},{14,10},{16,20},{18,... | collective-permute-start | bytes 110600 | tf_op jit(solution)/shard_map/ppermute | solution.py:36
  50.8 4.0 %collective-permute-start.12 = (f32[8,1152]{1,0:T(8,128)S(1)}, f32[8,1152]{1,0:T(8,128)S(1)}, u32[]{:S(2)}, u32[]{:S(2)}) collective-permute-start(f32[8,1152]{1,0:T(8,128)S(1)} %add.30), channel_id=1, source_target_pairs={{0,8},{2,10},{4,12},{6,14},{8,0},{10,2},{12,4},{14,6},{16,24},{18,... | collective-permute-start | bytes 110600 | tf_op jit(solution)/shard_map/ppermute | solution.py:36
  54.8 5.6 %collective-permute-start.14 = (f32[8,1152]{1,0:T(8,128)S(1)}, f32[8,1152]{1,0:T(8,128)S(1)}, u32[]{:S(2)}, u32[]{:S(2)}) collective-permute-start(f32[8,1152]{1,0:T(8,128)S(1)} %add_add_fusion.1), channel_id=1, source_target_pairs={{0,16},{2,18},{4,20},{6,22},{8,24},{10,26},{12,28},{14,30},{16,0},... | collective-permute-start | bytes 110600 | tf_op jit(solution)/shard_map/ppermute | solution.py:36
  60.4 1.2 collective-permute-start.15
  61.9 3.8 %collective-permute-start.16 = (f32[16,256]{1,0:T(8,128)S(1)}, f32[16,256]{1,0:T(8,128)S(1)}, u32[]{:S(2)}, u32[]{:S(2)}) collective-permute-start(f32[16,256]{1,0:T(8,128)S(1)} %get-tuple-element.64.near), channel_id=1, source_target_pairs={{0,1},{1,0},{2,3},{3,2},{4,5},{5,4},{6,7},{7,6},{8,9},{9,8},{10,11... | collective-permute-start | bytes 49160 | tf_op jit(solution)/shard_map/ppermute | solution.py:36
  65.9 1.2 collective-permute-start.17
  67.1 4.9 %collective-permute-start.20 = (f32[8,1152]{1,0:T(8,128)S(1)}, f32[8,1152]{1,0:T(8,128)S(1)}, u32[]{:S(2)}, u32[]{:S(2)}) collective-permute-start(f32[8,1152]{1,0:T(8,128)S(1)} %add.35), channel_id=1, source_target_pairs={{0,12},{2,14},{4,8},{6,10},{8,4},{10,6},{12,0},{14,2},{16,28},{18,... | collective-permute-start | bytes 110600 | tf_op jit(solution)/shard_map/ppermute | solution.py:36
  68.2 4.1 %collective-permute-start.18 = (f32[8,1152]{1,0:T(8,128)S(1)}, f32[8,1152]{1,0:T(8,128)S(1)}, u32[]{:S(2)}, u32[]{:S(2)}) collective-permute-start(f32[8,1152]{1,0:T(8,128)S(1)} %add.35), channel_id=1, source_target_pairs={{0,4},{2,6},{4,0},{6,2},{8,12},{10,14},{12,8},{14,10},{16,20},{18,... | collective-permute-start | bytes 110600 | tf_op jit(solution)/shard_map/ppermute | solution.py:36
  68.8 4.0 %collective-permute-start.19 = (f32[8,1152]{1,0:T(8,128)S(1)}, f32[8,1152]{1,0:T(8,128)S(1)}, u32[]{:S(2)}, u32[]{:S(2)}) collective-permute-start(f32[8,1152]{1,0:T(8,128)S(1)} %add.35), channel_id=1, source_target_pairs={{0,8},{2,10},{4,12},{6,14},{8,0},{10,2},{12,4},{14,6},{16,24},{18,... | collective-permute-start | bytes 110600 | tf_op jit(solution)/shard_map/ppermute | solution.py:36
  72.8 4.9 %collective-permute-start.21 = (f32[8,1152]{1,0:T(8,128)S(1)}, f32[8,1152]{1,0:T(8,128)S(1)}, u32[]{:S(2)}, u32[]{:S(2)}) collective-permute-start(f32[8,1152]{1,0:T(8,128)S(1)} %add_add_fusion), channel_id=1, source_target_pairs={{0,16},{2,18},{4,20},{6,22},{8,24},{10,26},{12,28},{14,30},{16,0},... | collective-permute-start | bytes 110600 | tf_op jit(solution)/shard_map/ppermute | solution.py:36
  77.7 1.2 collective-permute-start.22
  79.5 9.2 %collective-permute-start.29 = (bf16[256,512]{1,0:T(8,128)(2,1)S(1)}, bf16[256,512]{1,0:T(8,128)(2,1)S(1)}, u32[]{:S(2)}, u32[]{:S(2)}) collective-permute-start(bf16[256,512]{1,0:T(8,128)(2,1)S(1)} %get-tuple-element.84), channel_id=1, source_target_pairs={{0,1},{1,0},{2,3},{3,2},{4,5},{5,4},{6,7},{7,6},{8,9},{9,8},{10,11... | collective-permute-start | bytes 786440 | tf_op jit(solution)/shard_map/ppermute | solution.py:36
  81.6 12.3 %collective-permute-start.23 = (bf16[256,512]{1,0:T(8,128)(2,1)S(1)}, bf16[256,512]{1,0:T(8,128)(2,1)S(1)}, u32[]{:S(2)}, u32[]{:S(2)}) collective-permute-start(bf16[256,512]{1,0:T(8,128)(2,1)S(1)} %second_away.1), channel_id=1, source_target_pairs={{0,1},{1,0},{2,3},{3,2},{4,5},{5,4},{6,7},{7,6},{8,9},{9,8},{10,11... | collective-permute-start | bytes 786440 | tf_op jit(solution)/shard_map/ppermute | solution.py:36
  83.0 10.9 %collective-permute-start.24 = (f32[16,256]{1,0:T(8,128)S(1)}, f32[16,256]{1,0:T(8,128)S(1)}, u32[]{:S(2)}, u32[]{:S(2)}) collective-permute-start(f32[16,256]{1,0:T(8,128)S(1)} %get-tuple-element.74.refs_0_), channel_id=1, source_target_pairs={{0,1},{1,0},{2,3},{3,2},{4,5},{5,4},{6,7},{7,6},{8,9},{9,8},{10,11... | collective-permute-start | bytes 49160 | tf_op jit(solution)/shard_map/ppermute | solution.py:36
  89.3 5.3 %collective-permute-start.30 = (bf16[512,512]{1,0:T(8,128)(2,1)S(1)}, bf16[512,512]{1,0:T(8,128)(2,1)S(1)}, u32[]{:S(2)}, u32[]{:S(2)}) collective-permute-start(bf16[512,512]{1,0:T(8,128)(2,1)S(1)} %get-tuple-element.87), channel_id=1, source_target_pairs={{0,2},{2,0},{4,6},{6,4},{8,10},{10,8},{12,14},{14,12},{16,18},{18,... | collective-permute-start | bytes 1572872 | tf_op jit(solution)/shard_map/ppermute | solution.py:36
  93.9 40.6 %copy-start.1 = (f32[64,1024]{1,0:T(8,128)S(1)}, f32[64,1024]{1,0:T(8,128)}, u32[]{:S(2)}) copy-start(f32[64,1024]{1,0:T(8,128)} %refs_5_.1) | copy-start | bytes 786436
  93.9 40.6 %copy-start.4 = (f32[64,1024]{1,0:T(8,128)S(1)}, f32[64,1024]{1,0:T(8,128)}, u32[]{:S(2)}) copy-start(f32[64,1024]{1,0:T(8,128)} %refs_6_.1) | copy-start | bytes 786436
  93.9 40.6 %copy-start.5 = (f32[64,1024]{1,0:T(8,128)S(1)}, f32[64,1024]{1,0:T(8,128)}, u32[]{:S(2)}) copy-start(f32[64,1024]{1,0:T(8,128)} %refs_7_.1) | copy-start | bytes 786436
  93.9 40.6 %copy-start.6 = (f32[256,16]{0,1:T(8,128)S(1)}, f32[256,16]{0,1:T(8,128)}, u32[]{:S(2)}) copy-start(f32[256,16]{0,1:T(8,128)} %param.26) | copy-start | bytes 49156
  94.0 40.6 %copy-start.7 = (f32[256,16]{0,1:T(8,128)S(1)}, f32[256,16]{0,1:T(8,128)}, u32[]{:S(2)}) copy-start(f32[256,16]{0,1:T(8,128)} %param.27) | copy-start | bytes 49156
  94.5 2.0 %collective-permute-start.25 = (bf16[512,512]{1,0:T(8,128)(2,1)S(1)}, bf16[512,512]{1,0:T(8,128)(2,1)S(1)}, u32[]{:S(2)}, u32[]{:S(2)}) collective-permute-start(bf16[512,512]{1,0:T(8,128)(2,1)S(1)} %get-tuple-element.76), channel_id=1, source_target_pairs={{0,2},{2,0},{4,6},{6,4},{8,10},{10,8},{12,14},{14,12},{16,18},{18,... | collective-permute-start | bytes 1572872 | tf_op jit(solution)/shard_map/ppermute | solution.py:36
  94.7 9.2 %collective-permute-start.31 = (bf16[256,512]{1,0:T(8,128)(2,1)S(1)}, bf16[256,512]{1,0:T(8,128)(2,1)S(1)}, u32[]{:S(2)}, u32[]{:S(2)}) collective-permute-start(bf16[256,512]{1,0:T(8,128)(2,1)S(1)} %get-tuple-element.89), channel_id=1, source_target_pairs={{0,4},{2,6},{4,0},{6,2},{8,12},{10,14},{12,8},{14,10},{16,20},{18,... | collective-permute-start | bytes 786440 | tf_op jit(solution)/shard_map/ppermute | solution.py:36
  96.6 12.5 %collective-permute-start.26 = (bf16[256,512]{1,0:T(8,128)(2,1)S(1)}, bf16[256,512]{1,0:T(8,128)(2,1)S(1)}, u32[]{:S(2)}, u32[]{:S(2)}) collective-permute-start(bf16[256,512]{1,0:T(8,128)(2,1)S(1)} %get-tuple-element.78), channel_id=1, source_target_pairs={{0,4},{2,6},{4,0},{6,2},{8,12},{10,14},{12,8},{14,10},{16,20},{18,... | collective-permute-start | bytes 786440 | tf_op jit(solution)/shard_map/ppermute | solution.py:36
  104.0 7.0 %collective-permute-start.32 = (bf16[128,512]{1,0:T(8,128)(2,1)S(1)}, bf16[128,512]{1,0:T(8,128)(2,1)S(1)}, u32[]{:S(2)}, u32[]{:S(2)}) collective-permute-start(bf16[128,512]{1,0:T(8,128)(2,1)S(1)} %get-tuple-element.91), channel_id=1, source_target_pairs={{0,8},{2,10},{4,12},{6,14},{8,0},{10,2},{12,4},{14,6},{16,24},{18,... | collective-permute-start | bytes 393224 | tf_op jit(solution)/shard_map/ppermute | solution.py:36
  109.1 5.2 %collective-permute-start.27 = (bf16[128,512]{1,0:T(8,128)(2,1)S(1)}, bf16[128,512]{1,0:T(8,128)(2,1)S(1)}, u32[]{:S(2)}, u32[]{:S(2)}) collective-permute-start(bf16[128,512]{1,0:T(8,128)(2,1)S(1)} %get-tuple-element.80), channel_id=1, source_target_pairs={{0,8},{2,10},{4,12},{6,14},{8,0},{10,2},{12,4},{14,6},{16,24},{18,... | collective-permute-start | bytes 393224 | tf_op jit(solution)/shard_map/ppermute | solution.py:36
  111.1 7.0 %collective-permute-start.33 = (bf16[64,512]{1,0:T(8,128)(2,1)S(1)}, bf16[64,512]{1,0:T(8,128)(2,1)S(1)}, u32[]{:S(2)}, u32[]{:S(2)}) collective-permute-start(bf16[64,512]{1,0:T(8,128)(2,1)S(1)} %get-tuple-element.93), channel_id=1, source_target_pairs={{0,16},{2,18},{4,20},{6,22},{8,24},{10,26},{12,28},{14,30},{16,0},... | collective-permute-start | bytes 196616 | tf_op jit(solution)/shard_map/ppermute | solution.py:36
  114.4 6.1 %collective-permute-start.28 = (bf16[64,512]{1,0:T(8,128)(2,1)S(1)}, bf16[64,512]{1,0:T(8,128)(2,1)S(1)}, u32[]{:S(2)}, u32[]{:S(2)}) collective-permute-start(bf16[64,512]{1,0:T(8,128)(2,1)S(1)} %get-tuple-element.82), channel_id=1, source_target_pairs={{0,16},{2,18},{4,20},{6,22},{8,24},{10,26},{12,28},{14,30},{16,0},... | collective-permute-start | bytes 196616 | tf_op jit(solution)/shard_map/ppermute | solution.py:36

commit v3 on v2

--- a/solution.py
+++ b/solution.py
@@ -13,11 +13,15 @@
 BETA_TWO = 0.999
 ADAM_EPS = 1e-08
 DECAY = 0.01
-CHUNKS = 2
+SHARES = (3, 5)
+CHUNKS = len(SHARES)
+TOGETHER = 1
 LANES = 128
 SCRATCH = 16 << 20
-BIAS_A = 1
+BIAS_A = 8_000_000_000
 BIAS_C = 1
+T1 = 1
+T2 = 0
 BF = jnp.bfloat16
 F32 = jnp.float32
 BLK = ("hi", "core")
@@ -38,6 +42,10 @@
 
 def dot(a, b, dims=((1,), (0,))):
     return lax.dot_general(a, b, (dims, ((), ())), preferred_element_type=F32)
+
+
+def after(x, earlier):
+    return lax.optimization_barrier((x, earlier))[0]
 
 
 def split_low(x):
@@ -98,7 +106,17 @@
 
 def freq_rows(freq_ref, half, start, count):
     total = freq_ref.shape[0] // 2
-    return freq_ref[pl.ds(pl.multiple_of(half * total + start, count), count), :]
+    return freq_ref[pl.ds(pl.multiple_of(half * total + start, LANES), count), :]
+
+
+def pieces_of(whole):
+    ends = [whole * sum(SHARES[:k]) // sum(SHARES) for k in range(CHUNKS + 1)]
+    return [slice(a, b) for a, b in zip(ends[:-1], ends[1:])]
+
+
+def core_halves(mid):
+    core = lax.axis_index("core")
+    return [pl.ds(pl.multiple_of(k * mid, LANES), mid) for k in (core, 1 - core)]
 
 
 def prepare(inputs, width_class, col_mask, masked):
@@ -106,7 +124,7 @@
     n_blk = lax.axis_size("hi") * 2
     rows = d_in // n_blk
     classes = col_mask.shape[0]
-    me = lax.axis_index("hi") * 2 + lax.axis_index("core")
+    me = lax.axis_index("hi") * 2
     chosen = width_class[...] == lax.broadcasted_iota(jnp.int32, (classes, inputs.shape[0]), 0)
     keep_cols = dot(chosen.astype(F32), col_mask[...].astype(F32), ((0,), (0,)))
     plain = inputs[...] * keep_cols.astype(BF)
@@ -124,22 +142,28 @@
         masked[:, t * tile : (t + 1) * tile] = dot(plain, select).astype(BF)
 
 
-def hidden_units(masked, held, hidden, damp):
-    value = jnp.tanh(dot(masked[...], held[...]))
+def hidden_units(masked, *refs):
+    helds, (hidden, damp) = refs[: 1 if len(refs) == 3 else 2], refs[-2:]
+    if len(helds) == 1:
+        value = dot(masked[...], helds[0][...])
+    else:
+        parts = core_halves(masked.shape[1] // 2)
+        value = sum(dot(masked[:, part], held[...]) for part, held in zip(parts, helds))
+    value = jnp.tanh(value)
     hidden[...] = value.astype(BF)
     damp[...] = 1.0 - value * value
 
 
-def own_pre(first, second, freq, phases, pre):
-    width = first.shape[1]
-    half = my_half()
-    value = dot(first[...], freq_rows(freq, half, 0, width))
-    value = value + dot(second[...], freq_rows(freq, half, width, width))
-    pre[...] = value + phases[...]
-
-
-def far_pre(pre, far, freq, out):
-    out[...] = pre[...] + dot(far[...], freq_rows(freq, 1 - my_half(), 0, far.shape[1]))
+def first_pre(hidden, far, freq, phases, pre):
+    width = hidden.shape[1]
+    value = phases[...] + dot(hidden[...], freq_rows(freq, my_half(), 0, width))
+    pre[...] = value + dot(far[...], freq_rows(freq, 1 - my_half(), 0, width))
+
+
+def second_pre(pre, hidden, freq, out):
+    width = hidden.shape[1]
+    start = freq.shape[0] // 2 - width
+    out[...] = pre[...] + dot(hidden[...], freq_rows(freq, my_half(), start, width))
 
 
 def payload(keep, send, value, scalar):
@@ -154,7 +178,8 @@
 def make_features(pre, far, freq, alpha, row_mask, features, slope, keep, send):
     width = far.shape[1]
     scale = (2.0 / (pre.shape[1] * lax.axis_size("feat"))) ** 0.5
-    angle = pre[...] + dot(far[...], freq_rows(freq, 1 - my_half(), width, width))
+    start = freq.shape[0] // 2 - width
+    angle = pre[...] + dot(far[...], freq_rows(freq, 1 - my_half(), start, width))
     sine, cosine = sine_cosine(angle)
     value = (scale * cosine).astype(BF)
     features[...] = value
@@ -200,8 +225,9 @@
 
 def second_away(pre_grad, freq, away):
     width = away.shape[1]
+    start = freq.shape[0] // 2 - width
     away[...] = dot(
-        pre_grad[...], freq_rows(freq, 1 - my_half(), width, width), ((1,), (1,))
+        pre_grad[...], freq_rows(freq, 1 - my_half(), start, width), ((1,), (1,))
     ).astype(BF)
 
 
@@ -218,8 +244,9 @@
         hidden_grad = near[:, part] + got[...].astype(F32)
         first_grad = (damp[...] * hidden_grad).astype(BF)
         mid = send.shape[0]
-        send[...] = dot(masked[:, mid:], first_grad, ((0,), (0,))).astype(BF)
-        keep[...] = dot(masked[:, :mid], first_grad, ((0,), (0,)))
+        own, other = core_halves(mid)
+        send[...] = dot(masked[:, other], first_grad, ((0,), (0,))).astype(BF)
+        keep[...] = dot(masked[:, own], first_grad, ((0,), (0,)))
         if pulls:
             pulled, pulled_far, resid_grad = pulls
             refs[-1][...] = pulled[...] + pulled_far[...] + NOISE * resid_grad[...].astype(F32)
@@ -229,8 +256,11 @@
 
 def add_halves(keep, got, send, rest):
     mid = rest.shape[0]
-    send[...] = (keep[mid:] + got[mid:].astype(F32)).astype(BF)
-    rest[...] = keep[:mid] + got[:mid].astype(F32)
+    start = 0
+    if got.shape[0] != keep.shape[0]:
+        start = pl.multiple_of((1 - lax.axis_index("core")) * 2 * mid, mid)
+    send[...] = (keep[mid:] + got[pl.ds(start + mid, mid)].astype(F32)).astype(BF)
+    rest[...] = keep[:mid] + got[pl.ds(start, mid)].astype(F32)
 
 
 def finish_gradients(keep, got, *refs):
@@ -255,10 +285,9 @@
     last = squares.shape[1] - 1
     resid_out[...] = jnp.sqrt(squares[0:1, last:])
     clip = jnp.minimum(1.0, CLIP_AT / (norm + 1e-06))
-    width = weight.shape[1] // CHUNKS
     work = [
-        (slice(c * width, (c + 1) * width), (weight, moment, second), grad[...], 0.02, refs[8:12])
-        for c, grad in enumerate(grads)
+        (part, (weight, moment, second), grad[...], 0.02, refs[8:12])
+        for part, grad in zip(pieces_of(weight.shape[1]), grads)
     ]
     held = (alpha, alpha_moment, alpha_second)
     work.append((slice(None), held, turned(alpha_grad[...]), 0.05, refs[12:16]))
@@ -298,7 +327,8 @@
         points, samples = alpha_weight.shape
         n_low = frequencies.shape[1]
         h_own = hidden_weight.shape[1]
-        width = h_own // CHUNKS
+        pieces = pieces_of(h_own)
+        widths = [p.stop - p.start for p in pieces]
         row_mask, width_class, phases, targets = (
             x.reshape(1, -1) for x in (row_mask, width_class, phases, targets)
         )
@@ -308,26 +338,35 @@
         (masked,) = call(
             "prepare", prepare, [((points, d_in), BF)], inputs, width_class, col_mask
         )
-        units = [((points, width), BF), ((points, width), F32)]
-        hidden, damps = [], []
+        partly = []
         for c in range(CHUNKS):
-            held = low[:, c * width : (c + 1) * width]
-            for m in reversed(masks):
+            held = low[:, pieces[c]]
+            for k, m in enumerate(reversed(masks[1:])):
                 held = jnp.concatenate([held, swap(held, BLK, n_blk, m)], axis=0)
-            unit, damp = call("hidden", hidden_units, units, masked, held)
-            hidden.append(unit)
-            damps.append(damp)
-        fars = [swap(h, "feat", n_feat, 1) for h in hidden]
+                if c == 0 and k == 0:
+                    held = after(held, masked)
+            partly.append(held)
+        units = [[((points, w), BF), ((points, w), F32)] for w in widths]
         wide = ((points, n_low), F32)
-        (pre,) = call("own_pre", own_pre, [wide], *hidden, frequencies, phases)
-        (pre,) = call("far_pre", far_pre, [wide], pre, fars[0], frequencies, weight=BIAS_A)
+        held = lax.all_gather(partly[0], "core", axis=0, tiled=True)
+        hidden, damp = call("hidden", hidden_units, units[0], masked, held)
+        partly[1] = after(partly[1], hidden)
+        far = swap(hidden, "feat", n_feat, 1)
+        (pre,) = call(
+            "first_pre", first_pre, [wide], hidden, far, frequencies, phases, weight=BIAS_A
+        )
+        helds = [partly[1], swap(partly[1], BLK, n_blk, 1)]
+        hidden, damp_b = call("hidden", hidden_units, units[1], masked, *helds, pre)
+        damps = [damp, damp_b]
+        far = swap(hidden, "feat", n_feat, 1)
+        (pre,) = call("second_pre", second_pre, [wide], pre, hidden, frequencies)
         pair = [((samples // 2, n_low + LANES), F32)] * 2
         features, slope, keep, send = call(
             "features",
             make_features,
             [((points, n_low), BF), wide, *pair],
             pre,
-            fars[1],
+            far,
             frequencies,
             alpha,
             row_mask,
@@ -351,11 +390,11 @@
             features,
         )
         mine, other = sum_over_blk(keep, send)
-        away = ((points, width), BF)
+        away = [((points, width), BF) for width in widths]
         back, pre_grad, first = call(
             "pre_gradient",
             pre_gradient,
-            [parts, ((points, n_low), BF), away],
+            [parts, ((points, n_low), BF), away[0]],
             mine,
             other,
             moments,
@@ -365,7 +404,7 @@
             frequencies,
         )
         gots = [swap(first, "feat", n_feat, 1)]
-        (second,) = call("second_away", second_away, [away], pre_grad, frequencies)
+        (second,) = call("second_away", second_away, away[1:], pre_grad, frequencies)
         gots.append(swap(second, "feat", n_feat, 1))
         near, pulled = call(
             "own_gradient",
@@ -381,18 +420,31 @@
         grads, totals = [], []
         for c in range(CHUNKS):
             mid = d_in // 2
+            width = widths[c]
             shapes = [((mid, width), BF), ((mid, width), F32)]
-            part = slice(c * width, (c + 1) * width)
             operands = [near, gots[c], damps[c], masked]
+            if T2 and c:
+                operands[2] = after(damps[c], early)
             if c == CHUNKS - 1:
                 operands += [pulled, pulled_far, resid_grad]
                 shapes = shapes + [thin]
-            send, keep, *alpha_grad = call("weight_terms", weight_terms(part), shapes, *operands)
+            send, keep, *alpha_grad = call("weight_terms", weight_terms(pieces[c]), shapes, *operands)
             for m in masks[:-1]:
-                got = swap(send, BLK, n_blk, m)
+                if c < TOGETHER and m == masks[0]:
+                    got = lax.all_gather(send, "core", axis=0, tiled=True)
+                else:
+                    got = swap(send, BLK, n_blk, m)
                 mid = mid // 2
                 shapes = [((mid, width), BF), ((mid, width), F32)]
-                send, keep = call("add_halves", add_halves, shapes, keep, got)
+                ahead = c == 0 and m == masks[1]
+                if T1 and c and m == masks[0]:
+                    keep = after(keep, sent)
+                weight = BIAS_C if ahead else 1
+                send, keep = call("add_halves", add_halves, shapes, keep, got, weight=weight)
+                if ahead:
+                    sent = send
+                if c == 0 and m == masks[0]:
+                    early = send
             got = swap(send, BLK, n_blk, masks[-1])
             last = c == CHUNKS - 1
             outs = [((mid, width), F32), ((size, 1, LANES) if last else (1, LANES), F32)]
@@ -404,7 +456,6 @@
                 got,
                 *alpha_grad,
                 *totals,
-                weight=1 if last else BIAS_C,
             )
             grads.append(grad)
             totals = [total]

time: 136 us -> 144 us (1.059)
  waiting for transfers between devices: 62.8 us -> 72.9 us
  starting transfers between devices: 43.8 us -> 37.8 us
  blocking collectives: 13.9 us -> 17.1 us
    ppermute x34 -> x32, waiting for transfers between devices: 62.8 us -> 72.9 us  [swap(): return lax.ppermute(x, axis, [(i, i ^ mask) for i in range(size)])]
    ppermute x34 -> x32, starting transfers between devices: 43.8 us -> 37.8 us  [swap(): return lax.ppermute(x, axis, [(i, i ^ mask) for i in range(size)])]
    all_gather x0 -> x2, blocking collectives: none -> 4.87 us  [the longest x1 2.5 us: on_device(): held = lax.all_gather(partly[0], 'core', axis=0, tiled=True)]
    all_to_all x1, blocking collectives: 13.9 us -> 12.2 us  [on_device(): spread = lax.all_to_all(spread, (*BLK, 'feat'), 0, 0, tiled=True)]
  transfers between devices with their start and end apart: 34 -> 32, of which waited for: 28 -> 26; matrix products, arithmetic and copies ran while one was open for 0% -> 0% of each run, Pallas kernels for 4% -> 3%
where the time goes in v3:
time: 144 us; the launch traced here: 143 us
  waiting for transfers between devices  72.9 us (51%)
  starting transfers between devices  37.8 us (26%)
  blocking collectives  17.1 us (12%)
  Pallas kernels  11 us (8%)
  local copies, waits for them, and re-layouts  2.49 us (2%)
    ppermute x32, waiting for transfers between devices, swap(): return lax.ppermute(x, axis, [(i, i ^ mask) for i in range(size)])  72.9 us
    ppermute x32, starting transfers between devices, swap(): return lax.ppermute(x, axis, [(i, i ^ mask) for i in range(size)])  37.8 us
    all_to_all x1, blocking collectives, on_device(): spread = lax.all_to_all(spread, (*BLK, 'feat'), 0, 0, tiled=True)  12.2 us
    pallas_call x22, Pallas kernels, call(): pl.pallas_call(body, out_shape=[shapes(shape, dtype) for shape, dtype in...  11 us
  transfers between devices with their start and end apart: 32, of which 26 were waited for; matrix products, arithmetic and copies ran while one was open for 0% of the time, Pallas kernels for 3%

profile of v3, /device:TPU:0, one launch (start us, length us, event | category | flops | bytes accessed | tf_op | source)
XLA Modules:
  0.0 143.4 jit_solution(12120974001586620477)
XLA Ops:
  1.6 4.1 %collective-permute-start = (bf16[64,384]{1,0:T(8,128)(2,1)S(1)}, bf16[64,384]{1,0:T(8,128)(2,1)S(1)}, u32[]{:S(2)}, u32[]{:S(2)}) collective-permute-start(bf16[64,384]{1,0:T(8,128)(2,1)S(1)} %slice.8), channel_id=1, source_target_pairs={{0,16},{2,18},{4,20},{6,22},{8,24},{10,26},{12,28},{14,30},{16,0},... | collective-permute-start | bytes 147464 | tf_op jit(solution)/shard_map/ppermute | solution.py:40
  5.9 1.0 copy-done.2
  8.3 1.0 prepare.1.masked
  9.3 2.0 %collective-permute-start.1 = (bf16[128,384]{1,0:T(8,128)(2,1)S(1)}, bf16[128,384]{1,0:T(8,128)(2,1)S(1)}, u32[]{:S(2)}, u32[]{:S(2)}) collective-permute-start(bf16[128,384]{1,0:T(8,128)(2,1)S(1)} %pad_maximum_fusion.5), channel_id=1, source_target_pairs={{0,8},{2,10},{4,12},{6,14},{8,0},{10,2},{12,4},{14,6},{16,24},{18,... | collective-permute-start | bytes 294920 | tf_op jit(solution)/shard_map/ppermute | solution.py:40
  11.3 1.5 %collective-permute-done.4 = bf16[64,640]{1,0:T(8,128)(2,1)S(1)} collective-permute-done((bf16[64,640]{1,0:T(8,128)(2,1)S(1)}, bf16[64,640]{1,0:T(8,128)(2,1)S(1)}, u32[]{:S(2)}, u32[]{:S(2)}) %collective-permute-start.4) | collective-permute-done | bytes 81952 | tf_op jit(solution)/shard_map/ppermute | solution.py:40
  12.9 2.2 %collective-permute-done.1 = bf16[128,384]{1,0:T(8,128)(2,1)S(1)} collective-permute-done((bf16[128,384]{1,0:T(8,128)(2,1)S(1)}, bf16[128,384]{1,0:T(8,128)(2,1)S(1)}, u32[]{:S(2)}, u32[]{:S(2)}) %collective-permute-start.1) | collective-permute-done | bytes 98336 | tf_op jit(solution)/shard_map/ppermute | solution.py:40
  15.1 1.9 %collective-permute-start.2 = (bf16[256,384]{1,0:T(8,128)(2,1)S(1)}, bf16[256,384]{1,0:T(8,128)(2,1)S(1)}, u32[]{:S(2)}, u32[]{:S(2)}) collective-permute-start(bf16[256,384]{1,0:T(8,128)(2,1)S(1)} %pad_maximum_fusion.3), channel_id=1, source_target_pairs={{0,4},{2,6},{4,0},{6,2},{8,12},{10,14},{12,8},{14,10},{16,20},{18,... | collective-permute-start | bytes 589832 | tf_op jit(solution)/shard_map/ppermute | solution.py:40
  17.0 1.2 collective-permute-done.5
  18.2 1.6 %collective-permute-start.6 = (bf16[256,640]{1,0:T(8,128)(2,1)S(1)}, bf16[256,640]{1,0:T(8,128)(2,1)S(1)}, u32[]{:S(2)}, u32[]{:S(2)}) collective-permute-start(bf16[256,640]{1,0:T(8,128)(2,1)S(1)} %pad_maximum_fusion.2), channel_id=1, source_target_pairs={{0,4},{2,6},{4,0},{6,2},{8,12},{10,14},{12,8},{14,10},{16,20},{18,... | collective-permute-start | bytes 983048 | tf_op jit(solution)/shard_map/ppermute | solution.py:40
  19.8 3.1 %collective-permute-done.2 = bf16[256,384]{1,0:T(8,128)(2,1)S(1)} collective-permute-done((bf16[256,384]{1,0:T(8,128)(2,1)S(1)}, bf16[256,384]{1,0:T(8,128)(2,1)S(1)}, u32[]{:S(2)}, u32[]{:S(2)}) %collective-permute-start.2) | collective-permute-done | bytes 196640 | tf_op jit(solution)/shard_map/ppermute | solution.py:40
  23.0 2.5 %all_gather.6.refs_0_ = bf16[1024,384]{1,0:T(8,128)(2,1)S(1)} all-gather(bf16[512,384]{1,0:T(8,128)(2,1)S(1)} %pad_maximum_fusion.1), channel_id=1, replica_groups=mesh['hi'=8,'core'=2,'feat'=2] {'core'}, dimensions={0}, use_global_device_ids=true | all-gather | bytes 1179648 | tf_op jit(solution)/shard_map/all_gather | solution.py:351
  25.9 1.7 %collective-permute-start.3 = (bf16[256,384]{1,0:T(8,128)(2,1)S(1)}, bf16[256,384]{1,0:T(8,128)(2,1)S(1)}, u32[]{:S(2)}, u32[]{:S(2)}) collective-permute-start(bf16[256,384]{1,0:T(8,128)(2,1)S(1)} %get-tuple-element.63.hidden), channel_id=1, source_target_pairs={{0,1},{1,0},{2,3},{3,2},{4,5},{5,4},{6,7},{7,6},{8,9},{9,8},{10,11... | collective-permute-start | bytes 589832 | tf_op jit(solution)/shard_map/ppermute | solution.py:40
  28.2 4.7 %collective-permute-done.3.far = bf16[256,384]{1,0:T(8,128)(2,1)S(1)} collective-permute-done((bf16[256,384]{1,0:T(8,128)(2,1)S(1)}, bf16[256,384]{1,0:T(8,128)(2,1)S(1)}, u32[]{:S(2)}, u32[]{:S(2)}) %collective-permute-start.3) | collective-permute-done | bytes 196640 | tf_op jit(solution)/shard_map/ppermute | solution.py:40
  34.3 1.7 %collective-permute-start.8 = (bf16[256,640]{1,0:T(8,128)(2,1)S(1)}, bf16[256,640]{1,0:T(8,128)(2,1)S(1)}, u32[]{:S(2)}, u32[]{:S(2)}) collective-permute-start(bf16[256,640]{1,0:T(8,128)(2,1)S(1)} %get-tuple-element.65.hidden), channel_id=1, source_target_pairs={{0,1},{1,0},{2,3},{3,2},{4,5},{5,4},{6,7},{7,6},{8,9},{9,8},{10,11... | collective-permute-start | bytes 983048 | tf_op jit(solution)/shard_map/ppermute | solution.py:40
  36.6 6.6 %collective-permute-done.8.far = bf16[256,640]{1,0:T(8,128)(2,1)S(1)} collective-permute-done((bf16[256,640]{1,0:T(8,128)(2,1)S(1)}, bf16[256,640]{1,0:T(8,128)(2,1)S(1)}, u32[]{:S(2)}, u32[]{:S(2)}) %collective-permute-start.8) | collective-permute-done | bytes 327712 | tf_op jit(solution)/shard_map/ppermute | solution.py:40
  43.2 2.1 %features.1 = (bf16[256,1024]{1,0:T(8,128)(2,1)S(1)}, f32[256,1024]{1,0:T(8,128)S(1)}, f32[8,1152]{1,0:T(8,128)S(1)}, f32[8,1152]{1,0:T(8,128)S(1)}) custom-call(f32[256,1024]{1,0:T(8,128)S(1)} %second_pre.1.pre, bf16[256,640]{1,0:T(8,128)(2,1)S(1)} %collective-permute-done.8.far, bf16[2048,1024]{1,0:T(8,128)(2,1)S(1)} %copy-done, f32[16,256]{1,0:T(8,128)S(1)} %bitcast.14, ...), custom_call_target="tpu_custom_call" | custom-call | flops 1 | bytes 1 | tf_op jit(solution)/shard_map/features/pallas_call | solution.py:85
  45.4 1.2 collective-permute-done.9
  46.6 1.6 %collective-permute-start.10 = (f32[8,1152]{1,0:T(8,128)S(1)}, f32[8,1152]{1,0:T(8,128)S(1)}, u32[]{:S(2)}, u32[]{:S(2)}) collective-permute-start(f32[8,1152]{1,0:T(8,128)S(1)} %add.30), channel_id=1, source_target_pairs={{0,4},{2,6},{4,0},{6,2},{8,12},{10,14},{12,8},{14,10},{16,20},{18,... | collective-permute-start | bytes 110600 | tf_op jit(solution)/shard_map/ppermute | solution.py:40
  48.2 1.9 %collective-permute-start.12 = (f32[8,1152]{1,0:T(8,128)S(1)}, f32[8,1152]{1,0:T(8,128)S(1)}, u32[]{:S(2)}, u32[]{:S(2)}) collective-permute-start(f32[8,1152]{1,0:T(8,128)S(1)} %add.30), channel_id=1, source_target_pairs={{0,12},{2,14},{4,8},{6,10},{8,4},{10,6},{12,0},{14,2},{16,28},{18,... | collective-permute-start | bytes 110600 | tf_op jit(solution)/shard_map/ppermute | solution.py:40
  50.6 1.6 %collective-permute-done.11 = f32[8,1152]{1,0:T(8,128)S(1)} collective-permute-done((f32[8,1152]{1,0:T(8,128)S(1)}, f32[8,1152]{1,0:T(8,128)S(1)}, u32[]{:S(2)}, u32[]{:S(2)}) %collective-permute-start.11) | collective-permute-done | bytes 36896 | tf_op jit(solution)/shard_map/ppermute | solution.py:40
  53.1 2.7 %collective-permute-start.13 = (f32[8,1152]{1,0:T(8,128)S(1)}, f32[8,1152]{1,0:T(8,128)S(1)}, u32[]{:S(2)}, u32[]{:S(2)}) collective-permute-start(f32[8,1152]{1,0:T(8,128)S(1)} %add_add_fusion.1), channel_id=1, source_target_pairs={{0,16},{2,18},{4,20},{6,22},{8,24},{10,26},{12,28},{14,30},{16,0},... | collective-permute-start | bytes 110600 | tf_op jit(solution)/shard_map/ppermute | solution.py:40
  55.8 2.2 %collective-permute-done.13 = f32[8,1152]{1,0:T(8,128)S(1)} collective-permute-done((f32[8,1152]{1,0:T(8,128)S(1)}, f32[8,1152]{1,0:T(8,128)S(1)}, u32[]{:S(2)}, u32[]{:S(2)}) %collective-permute-start.13) | collective-permute-done | bytes 36896 | tf_op jit(solution)/shard_map/ppermute | solution.py:40
  58.0 1.2 collective-permute-done.14.other
  59.5 1.6 %collective-permute-start.15 = (f32[16,256]{1,0:T(8,128)S(1)}, f32[16,256]{1,0:T(8,128)S(1)}, u32[]{:S(2)}, u32[]{:S(2)}) collective-permute-start(f32[16,256]{1,0:T(8,128)S(1)} %get-tuple-element.69.near), channel_id=1, source_target_pairs={{0,1},{1,0},{2,3},{3,2},{4,5},{5,4},{6,7},{7,6},{8,9},{9,8},{10,11... | collective-permute-start | bytes 49160 | tf_op jit(solution)/shard_map/ppermute | solution.py:40
  61.1 2.2 %collective-permute-done.15.far = f32[16,256]{1,0:T(8,128)S(1)} collective-permute-done((f32[16,256]{1,0:T(8,128)S(1)}, f32[16,256]{1,0:T(8,128)S(1)}, u32[]{:S(2)}, u32[]{:S(2)}) %collective-permute-start.15) | collective-permute-done | bytes 16416 | tf_op jit(solution)/shard_map/ppermute | solution.py:40
  63.5 1.2 collective-permute-done.16
  65.7 1.5 %collective-permute-start.18 = (f32[8,1152]{1,0:T(8,128)S(1)}, f32[8,1152]{1,0:T(8,128)S(1)}, u32[]{:S(2)}, u32[]{:S(2)}) collective-permute-start(f32[8,1152]{1,0:T(8,128)S(1)} %add.35), channel_id=1, source_target_pairs={{0,8},{2,10},{4,12},{6,14},{8,0},{10,2},{12,4},{14,6},{16,24},{18,... | collective-permute-start | bytes 110600 | tf_op jit(solution)/shard_map/ppermute | solution.py:40
  67.2 1.0 collective-permute-start.19
  69.6 2.4 %collective-permute-done.19 = f32[8,1152]{1,0:T(8,128)S(1)} collective-permute-done((f32[8,1152]{1,0:T(8,128)S(1)}, f32[8,1152]{1,0:T(8,128)S(1)}, u32[]{:S(2)}, u32[]{:S(2)}) %collective-permute-start.19) | collective-permute-done | bytes 36896 | tf_op jit(solution)/shard_map/ppermute | solution.py:40
  72.0 1.6 %collective-permute-start.20 = (f32[8,1152]{1,0:T(8,128)S(1)}, f32[8,1152]{1,0:T(8,128)S(1)}, u32[]{:S(2)}, u32[]{:S(2)}) collective-permute-start(f32[8,1152]{1,0:T(8,128)S(1)} %add_add_fusion), channel_id=1, source_target_pairs={{0,16},{2,18},{4,20},{6,22},{8,24},{10,26},{12,28},{14,30},{16,0},... | collective-permute-start | bytes 110600 | tf_op jit(solution)/shard_map/ppermute | solution.py:40
  73.6 3.7 %collective-permute-done.20 = f32[8,1152]{1,0:T(8,128)S(1)} collective-permute-done((f32[8,1152]{1,0:T(8,128)S(1)}, f32[8,1152]{1,0:T(8,128)S(1)}, u32[]{:S(2)}, u32[]{:S(2)}) %collective-permute-start.20) | collective-permute-done | bytes 36896 | tf_op jit(solution)/shard_map/ppermute | solution.py:40
  77.3 1.2 collective-permute-done.21.other
  79.8 1.6 %collective-permute-start.22 = (bf16[256,640]{1,0:T(8,128)(2,1)S(1)}, bf16[256,640]{1,0:T(8,128)(2,1)S(1)}, u32[]{:S(2)}, u32[]{:S(2)}) collective-permute-start(bf16[256,640]{1,0:T(8,128)(2,1)S(1)} %second_away.1), channel_id=1, source_target_pairs={{0,1},{1,0},{2,3},{3,2},{4,5},{5,4},{6,7},{7,6},{8,9},{9,8},{10,11... | collective-permute-start | bytes 983048 | tf_op jit(solution)/shard_map/ppermute | solution.py:40
  82.8 7.2 %collective-permute-done.23.refs_1_ = f32[16,256]{1,0:T(8,128)S(1)} collective-permute-done((f32[16,256]{1,0:T(8,128)S(1)}, f32[16,256]{1,0:T(8,128)S(1)}, u32[]{:S(2)}, u32[]{:S(2)}) %collective-permute-start.23) | collective-permute-done | bytes 16416 | tf_op jit(solution)/shard_map/ppermute | solution.py:40
  90.7 1.6 %collective-permute-start.24 = (bf16[256,384]{1,0:T(8,128)(2,1)S(1)}, bf16[256,384]{1,0:T(8,128)(2,1)S(1)}, u32[]{:S(2)}, u32[]{:S(2)}) collective-permute-start(bf16[256,384]{1,0:T(8,128)(2,1)S(1)} %get-tuple-element.81), channel_id=1, source_target_pairs={{0,1},{1,0},{2,3},{3,2},{4,5},{5,4},{6,7},{7,6},{8,9},{9,8},{10,11... | collective-permute-start | bytes 589832 | tf_op jit(solution)/shard_map/ppermute | solution.py:40
  92.3 5.7 %collective-permute-done.24.got = bf16[256,384]{1,0:T(8,128)(2,1)S(1)} collective-permute-done((bf16[256,384]{1,0:T(8,128)(2,1)S(1)}, bf16[256,384]{1,0:T(8,128)(2,1)S(1)}, u32[]{:S(2)}, u32[]{:S(2)}) %collective-permute-start.24) | collective-permute-done | bytes 196640 | tf_op jit(solution)/shard_map/ppermute | solution.py:40
  98.6 2.4 %all_gather.7.got = bf16[1024,384]{1,0:T(8,128)(2,1)S(1)} all-gather(bf16[512,384]{1,0:T(8,128)(2,1)S(1)} %get-tuple-element.84), channel_id=1, replica_groups=mesh['hi'=8,'core'=2,'feat'=2] {'core'}, dimensions={0}, use_global_device_ids=true | all-gather | bytes 1179648 | tf_op jit(solution)/shard_map/all_gather | solution.py:434
  101.0 1.3 collective-permute-start.25
  102.3 5.7 %collective-permute-done.25.got = bf16[256,384]{1,0:T(8,128)(2,1)S(1)} collective-permute-done((bf16[256,384]{1,0:T(8,128)(2,1)S(1)}, bf16[256,384]{1,0:T(8,128)(2,1)S(1)}, u32[]{:S(2)}, u32[]{:S(2)}) %collective-permute-start.25) | collective-permute-done | bytes 196640 | tf_op jit(solution)/shard_map/ppermute | solution.py:40
  108.2 1.3 collective-permute-start.27
  109.5 7.7 %collective-permute-done.27.got = bf16[256,640]{1,0:T(8,128)(2,1)S(1)} collective-permute-done((bf16[256,640]{1,0:T(8,128)(2,1)S(1)}, bf16[256,640]{1,0:T(8,128)(2,1)S(1)}, u32[]{:S(2)}, u32[]{:S(2)}) %collective-permute-start.27) | collective-permute-done | bytes 327712 | tf_op jit(solution)/shard_map/ppermute | solution.py:40
  117.5 1.8 %collective-permute-start.30 = (bf16[128,384]{1,0:T(8,128)(2,1)S(1)}, bf16[128,384]{1,0:T(8,128)(2,1)S(1)}, u32[]{:S(2)}, u32[]{:S(2)}) collective-permute-start(bf16[128,384]{1,0:T(8,128)(2,1)S(1)} %get-tuple-element.87), channel_id=1, source_target_pairs={{0,8},{2,10},{4,12},{6,14},{8,0},{10,2},{12,4},{14,6},{16,24},{18,... | collective-permute-start | bytes 294920 | tf_op jit(solution)/shard_map/ppermute | solution.py:40
  119.3 3.6 %collective-permute-done.28.got = bf16[128,640]{1,0:T(8,128)(2,1)S(1)} collective-permute-done((bf16[128,640]{1,0:T(8,128)(2,1)S(1)}, bf16[128,640]{1,0:T(8,128)(2,1)S(1)}, u32[]{:S(2)}, u32[]{:S(2)}) %collective-permute-start.28) | collective-permute-done | bytes 163872 | tf_op jit(solution)/shard_map/ppermute | solution.py:40
  122.9 1.6 %collective-permute-start.29 = (bf16[64,640]{1,0:T(8,128)(2,1)S(1)}, bf16[64,640]{1,0:T(8,128)(2,1)S(1)}, u32[]{:S(2)}, u32[]{:S(2)}) collective-permute-start(bf16[64,640]{1,0:T(8,128)(2,1)S(1)} %get-tuple-element.95), channel_id=1, source_target_pairs={{0,16},{2,18},{4,20},{6,22},{8,24},{10,26},{12,28},{14,30},{16,0},... | collective-permute-start | bytes 245768 | tf_op jit(solution)/shard_map/ppermute | solution.py:40
  124.6 1.6 %collective-permute-start.31 = (bf16[64,384]{1,0:T(8,128)(2,1)S(1)}, bf16[64,384]{1,0:T(8,128)(2,1)S(1)}, u32[]{:S(2)}, u32[]{:S(2)}) collective-permute-start(bf16[64,384]{1,0:T(8,128)(2,1)S(1)} %get-tuple-element.99), channel_id=1, source_target_pairs={{0,16},{2,18},{4,20},{6,22},{8,24},{10,26},{12,28},{14,30},{16,0},... | collective-permute-start | bytes 147464 | tf_op jit(solution)/shard_map/ppermute | solution.py:40
  126.1 3.5 %collective-permute-done.31.got = bf16[64,384]{1,0:T(8,128)(2,1)S(1)} collective-permute-done((bf16[64,384]{1,0:T(8,128)(2,1)S(1)}, bf16[64,384]{1,0:T(8,128)(2,1)S(1)}, u32[]{:S(2)}, u32[]{:S(2)}) %collective-permute-start.31) | collective-permute-done | bytes 49184 | tf_op jit(solution)/shard_map/ppermute | solution.py:40
  130.0 12.2 %all_to_all.5.refs_0_ = f32[32,1,128]{2,1,0:T(1,128)S(1)} all-to-all(f32[32,1,128]{2,1,0:T(1,128)S(1)} %get-tuple-element.101), channel_id=1, replica_groups=mesh['hi'=8,'core'=2,'feat'=2] {'hi','core','feat'}, dimensions={0} | all-to-all | bytes 32768 | tf_op jit(solution)/shard_map/all_to_all | solution.py:463
  142.2 1.2 update.1
  (84 shorter events, 14.8 us)
Async XLA Ops:
  1.6 7.7 %collective-permute-start = (bf16[64,384]{1,0:T(8,128)(2,1)S(1)}, bf16[64,384]{1,0:T(8,128)(2,1)S(1)}, u32[]{:S(2)}, u32[]{:S(2)}) collective-permute-start(bf16[64,384]{1,0:T(8,128)(2,1)S(1)} %slice.8), channel_id=1, source_target_pairs={{0,16},{2,18},{4,20},{6,22},{8,24},{10,26},{12,28},{14,30},{16,0},... | collective-permute-start | bytes 147464 | tf_op jit(solution)/shard_map/ppermute | solution.py:40
  5.8 7.0 %collective-permute-start.4 = (bf16[64,640]{1,0:T(8,128)(2,1)S(1)}, bf16[64,640]{1,0:T(8,128)(2,1)S(1)}, u32[]{:S(2)}, u32[]{:S(2)}) collective-permute-start(bf16[64,640]{1,0:T(8,128)(2,1)S(1)} %slice.9), channel_id=1, source_target_pairs={{0,16},{2,18},{4,20},{6,22},{8,24},{10,26},{12,28},{14,30},{16,0},... | collective-permute-start | bytes 245768 | tf_op jit(solution)/shard_map/ppermute | solution.py:40
  5.9 1.0 copy-start.2
  6.9 0.7 copy-start.9
  7.6 0.7 copy-start.11
  9.3 5.7 %collective-permute-start.1 = (bf16[128,384]{1,0:T(8,128)(2,1)S(1)}, bf16[128,384]{1,0:T(8,128)(2,1)S(1)}, u32[]{:S(2)}, u32[]{:S(2)}) collective-permute-start(bf16[128,384]{1,0:T(8,128)(2,1)S(1)} %pad_maximum_fusion.5), channel_id=1, source_target_pairs={{0,8},{2,10},{4,12},{6,14},{8,0},{10,2},{12,4},{14,6},{16,24},{18,... | collective-permute-start | bytes 294920 | tf_op jit(solution)/shard_map/ppermute | solution.py:40
  12.8 5.4 %collective-permute-start.5 = (bf16[128,640]{1,0:T(8,128)(2,1)S(1)}, bf16[128,640]{1,0:T(8,128)(2,1)S(1)}, u32[]{:S(2)}, u32[]{:S(2)}) collective-permute-start(bf16[128,640]{1,0:T(8,128)(2,1)S(1)} %pad_maximum_fusion.4), channel_id=1, source_target_pairs={{0,8},{2,10},{4,12},{6,14},{8,0},{10,2},{12,4},{14,6},{16,24},{18,... | collective-permute-start | bytes 491528 | tf_op jit(solution)/shard_map/ppermute | solution.py:40
  15.1 7.8 %collective-permute-start.2 = (bf16[256,384]{1,0:T(8,128)(2,1)S(1)}, bf16[256,384]{1,0:T(8,128)(2,1)S(1)}, u32[]{:S(2)}, u32[]{:S(2)}) collective-permute-start(bf16[256,384]{1,0:T(8,128)(2,1)S(1)} %pad_maximum_fusion.3), channel_id=1, source_target_pairs={{0,4},{2,6},{4,0},{6,2},{8,12},{10,14},{12,8},{14,10},{16,20},{18,... | collective-permute-start | bytes 589832 | tf_op jit(solution)/shard_map/ppermute | solution.py:40
  18.2 9.9 %collective-permute-start.6 = (bf16[256,640]{1,0:T(8,128)(2,1)S(1)}, bf16[256,640]{1,0:T(8,128)(2,1)S(1)}, u32[]{:S(2)}, u32[]{:S(2)}) collective-permute-start(bf16[256,640]{1,0:T(8,128)(2,1)S(1)} %pad_maximum_fusion.2), channel_id=1, source_target_pairs={{0,4},{2,6},{4,0},{6,2},{8,12},{10,14},{12,8},{14,10},{16,20},{18,... | collective-permute-start | bytes 983048 | tf_op jit(solution)/shard_map/ppermute | solution.py:40
  22.9 10.0 %copy-start = (bf16[2048,1024]{1,0:T(8,128)(2,1)S(1)}, bf16[2048,1024]{1,0:T(8,128)(2,1)}, u32[]{:S(2)}) copy-start(bf16[2048,1024]{1,0:T(8,128)(2,1)} %freq.11) | copy-start | bytes 12582916
  25.5 7.5 %copy-start.13 = (f32[1024]{0:T(1024)S(1)}, f32[1024]{0:T(1024)}, u32[]{:S(2)}) copy-start(f32[1024]{0:T(1024)} %param.19) | copy-start | bytes 12292
  25.9 7.0 %collective-permute-start.3 = (bf16[256,384]{1,0:T(8,128)(2,1)S(1)}, bf16[256,384]{1,0:T(8,128)(2,1)S(1)}, u32[]{:S(2)}, u32[]{:S(2)}) collective-permute-start(bf16[256,384]{1,0:T(8,128)(2,1)S(1)} %get-tuple-element.63.hidden), channel_id=1, source_target_pairs={{0,1},{1,0},{2,3},{3,2},{4,5},{5,4},{6,7},{7,6},{8,9},{9,8},{10,11... | collective-permute-start | bytes 589832 | tf_op jit(solution)/shard_map/ppermute | solution.py:40
  28.2 5.5 %collective-permute-start.7 = (bf16[512,640]{1,0:T(8,128)(2,1)S(1)}, bf16[512,640]{1,0:T(8,128)(2,1)S(1)}, u32[]{:S(2)}, u32[]{:S(2)}) collective-permute-start(bf16[512,640]{1,0:T(8,128)(2,1)S(1)} %pad_maximum_fusion.refs_0_), channel_id=1, source_target_pairs={{0,2},{2,0},{4,6},{6,4},{8,10},{10,8},{12,14},{14,12},{16,18},{18,... | collective-permute-start | bytes 1966088 | tf_op jit(solution)/shard_map/ppermute | solution.py:40
  34.2 9.0 %copy-start.3 = (f32[256,16]{0,1:T(8,128)S(1)}, f32[256,16]{0,1:T(8,128)}, u32[]{:S(2)}) copy-start(f32[256,16]{0,1:T(8,128)} %param.25) | copy-start | bytes 49156
  34.3 9.0 %copy-start.10 = (s32[256]{0:T(256)S(1)}, s32[256]{0:T(256)}, u32[]{:S(2)}) copy-start(s32[256]{0:T(256)} %param.16) | copy-start | bytes 3076
  34.3 9.0 %collective-permute-start.8 = (bf16[256,640]{1,0:T(8,128)(2,1)S(1)}, bf16[256,640]{1,0:T(8,128)(2,1)S(1)}, u32[]{:S(2)}, u32[]{:S(2)}) collective-permute-start(bf16[256,640]{1,0:T(8,128)(2,1)S(1)} %get-tuple-element.65.hidden), channel_id=1, source_target_pairs={{0,1},{1,0},{2,3},{3,2},{4,5},{5,4},{6,7},{7,6},{8,9},{9,8},{10,11... | collective-permute-start | bytes 983048 | tf_op jit(solution)/shard_map/ppermute | solution.py:40
  43.2 20.0 %copy-start.8 = (f32[256,16]{0,1:T(8,128)S(1)}, f32[256,16]{0,1:T(8,128)}, u32[]{:S(2)}) copy-start(f32[256,16]{0,1:T(8,128)} %param.21) | copy-start | bytes 49156
  43.2 20.0 %copy-start.12 = (f32[256]{0:T(256)S(1)}, f32[256]{0:T(256)}, u32[]{:S(2)}) copy-start(f32[256]{0:T(256)} %param.20) | copy-start | bytes 3076
  45.3 1.3 collective-permute-start.9
  46.6 4.0 %collective-permute-start.10 = (f32[8,1152]{1,0:T(8,128)S(1)}, f32[8,1152]{1,0:T(8,128)S(1)}, u32[]{:S(2)}, u32[]{:S(2)}) collective-permute-start(f32[8,1152]{1,0:T(8,128)S(1)} %add.30), channel_id=1, source_target_pairs={{0,4},{2,6},{4,0},{6,2},{8,12},{10,14},{12,8},{14,10},{16,20},{18,... | collective-permute-start | bytes 110600 | tf_op jit(solution)/shard_map/ppermute | solution.py:40
  48.2 4.0 %collective-permute-start.11 = (f32[8,1152]{1,0:T(8,128)S(1)}, f32[8,1152]{1,0:T(8,128)S(1)}, u32[]{:S(2)}, u32[]{:S(2)}) collective-permute-start(f32[8,1152]{1,0:T(8,128)S(1)} %add.30), channel_id=1, source_target_pairs={{0,8},{2,10},{4,12},{6,14},{8,0},{10,2},{12,4},{14,6},{16,24},{18,... | collective-permute-start | bytes 110600 | tf_op jit(solution)/shard_map/ppermute | solution.py:40
  48.2 4.9 %collective-permute-start.12 = (f32[8,1152]{1,0:T(8,128)S(1)}, f32[8,1152]{1,0:T(8,128)S(1)}, u32[]{:S(2)}, u32[]{:S(2)}) collective-permute-start(f32[8,1152]{1,0:T(8,128)S(1)} %add.30), channel_id=1, source_target_pairs={{0,12},{2,14},{4,8},{6,10},{8,4},{10,6},{12,0},{14,2},{16,28},{18,... | collective-permute-start | bytes 110600 | tf_op jit(solution)/shard_map/ppermute | solution.py:40
  53.1 4.9 %collective-permute-start.13 = (f32[8,1152]{1,0:T(8,128)S(1)}, f32[8,1152]{1,0:T(8,128)S(1)}, u32[]{:S(2)}, u32[]{:S(2)}) collective-permute-start(f32[8,1152]{1,0:T(8,128)S(1)} %add_add_fusion.1), channel_id=1, source_target_pairs={{0,16},{2,18},{4,20},{6,22},{8,24},{10,26},{12,28},{14,30},{16,0},... | collective-permute-start | bytes 110600 | tf_op jit(solution)/shard_map/ppermute | solution.py:40
  58.0 1.2 collective-permute-start.14
  59.5 3.8 %collective-permute-start.15 = (f32[16,256]{1,0:T(8,128)S(1)}, f32[16,256]{1,0:T(8,128)S(1)}, u32[]{:S(2)}, u32[]{:S(2)}) collective-permute-start(f32[16,256]{1,0:T(8,128)S(1)} %get-tuple-element.69.near), channel_id=1, source_target_pairs={{0,1},{1,0},{2,3},{3,2},{4,5},{5,4},{6,7},{7,6},{8,9},{9,8},{10,11... | collective-permute-start | bytes 49160 | tf_op jit(solution)/shard_map/ppermute | solution.py:40
  63.5 1.2 collective-permute-start.16
  64.7 4.0 %collective-permute-start.17 = (f32[8,1152]{1,0:T(8,128)S(1)}, f32[8,1152]{1,0:T(8,128)S(1)}, u32[]{:S(2)}, u32[]{:S(2)}) collective-permute-start(f32[8,1152]{1,0:T(8,128)S(1)} %add.35), channel_id=1, source_target_pairs={{0,4},{2,6},{4,0},{6,2},{8,12},{10,14},{12,8},{14,10},{16,20},{18,... | collective-permute-start | bytes 110600 | tf_op jit(solution)/shard_map/ppermute | solution.py:40
  65.7 4.0 %collective-permute-start.18 = (f32[8,1152]{1,0:T(8,128)S(1)}, f32[8,1152]{1,0:T(8,128)S(1)}, u32[]{:S(2)}, u32[]{:S(2)}) collective-permute-start(f32[8,1152]{1,0:T(8,128)S(1)} %add.35), channel_id=1, source_target_pairs={{0,8},{2,10},{4,12},{6,14},{8,0},{10,2},{12,4},{14,6},{16,24},{18,... | collective-permute-start | bytes 110600 | tf_op jit(solution)/shard_map/ppermute | solution.py:40
  67.2 4.9 %collective-permute-start.19 = (f32[8,1152]{1,0:T(8,128)S(1)}, f32[8,1152]{1,0:T(8,128)S(1)}, u32[]{:S(2)}, u32[]{:S(2)}) collective-permute-start(f32[8,1152]{1,0:T(8,128)S(1)} %add.35), channel_id=1, source_target_pairs={{0,12},{2,14},{4,8},{6,10},{8,4},{10,6},{12,0},{14,2},{16,28},{18,... | collective-permute-start | bytes 110600 | tf_op jit(solution)/shard_map/ppermute | solution.py:40
  72.0 5.3 %collective-permute-start.20 = (f32[8,1152]{1,0:T(8,128)S(1)}, f32[8,1152]{1,0:T(8,128)S(1)}, u32[]{:S(2)}, u32[]{:S(2)}) collective-permute-start(f32[8,1152]{1,0:T(8,128)S(1)} %add_add_fusion), channel_id=1, source_target_pairs={{0,16},{2,18},{4,20},{6,22},{8,24},{10,26},{12,28},{14,30},{16,0},... | collective-permute-start | bytes 110600 | tf_op jit(solution)/shard_map/ppermute | solution.py:40
  77.3 1.2 collective-permute-start.21
  79.8 10.2 %collective-permute-start.22 = (bf16[256,640]{1,0:T(8,128)(2,1)S(1)}, bf16[256,640]{1,0:T(8,128)(2,1)S(1)}, u32[]{:S(2)}, u32[]{:S(2)}) collective-permute-start(bf16[256,640]{1,0:T(8,128)(2,1)S(1)} %second_away.1), channel_id=1, source_target_pairs={{0,1},{1,0},{2,3},{3,2},{4,5},{5,4},{6,7},{7,6},{8,9},{9,8},{10,11... | collective-permute-start | bytes 983048 | tf_op jit(solution)/shard_map/ppermute | solution.py:40
  82.2 7.7 %collective-permute-start.23 = (f32[16,256]{1,0:T(8,128)S(1)}, f32[16,256]{1,0:T(8,128)S(1)}, u32[]{:S(2)}, u32[]{:S(2)}) collective-permute-start(f32[16,256]{1,0:T(8,128)S(1)} %get-tuple-element.79.refs_0_), channel_id=1, source_target_pairs={{0,1},{1,0},{2,3},{3,2},{4,5},{5,4},{6,7},{7,6},{8,9},{9,8},{10,11... | collective-permute-start | bytes 49160 | tf_op jit(solution)/shard_map/ppermute | solution.py:40
  90.7 17.4 %collective-permute-start.26 = (bf16[512,640]{1,0:T(8,128)(2,1)S(1)}, bf16[512,640]{1,0:T(8,128)(2,1)S(1)}, u32[]{:S(2)}, u32[]{:S(2)}) collective-permute-start(bf16[512,640]{1,0:T(8,128)(2,1)S(1)} %get-tuple-element.89), channel_id=1, source_target_pairs={{0,2},{2,0},{4,6},{6,4},{8,10},{10,8},{12,14},{14,12},{16,18},{18,... | collective-permute-start | bytes 1966088 | tf_op jit(solution)/shard_map/ppermute | solution.py:40
  90.7 7.3 %collective-permute-start.24 = (bf16[256,384]{1,0:T(8,128)(2,1)S(1)}, bf16[256,384]{1,0:T(8,128)(2,1)S(1)}, u32[]{:S(2)}, u32[]{:S(2)}) collective-permute-start(bf16[256,384]{1,0:T(8,128)(2,1)S(1)} %get-tuple-element.81), channel_id=1, source_target_pairs={{0,1},{1,0},{2,3},{3,2},{4,5},{5,4},{6,7},{7,6},{8,9},{9,8},{10,11... | collective-permute-start | bytes 589832 | tf_op jit(solution)/shard_map/ppermute | solution.py:40
  101.0 7.0 %collective-permute-start.25 = (bf16[256,384]{1,0:T(8,128)(2,1)S(1)}, bf16[256,384]{1,0:T(8,128)(2,1)S(1)}, u32[]{:S(2)}, u32[]{:S(2)}) collective-permute-start(bf16[256,384]{1,0:T(8,128)(2,1)S(1)} %get-tuple-element.86), channel_id=1, source_target_pairs={{0,4},{2,6},{4,0},{6,2},{8,12},{10,14},{12,8},{14,10},{16,20},{18,... | collective-permute-start | bytes 589832 | tf_op jit(solution)/shard_map/ppermute | solution.py:40
  108.2 34.0 %copy-start.1 = (f32[64,1024]{1,0:T(8,128)S(1)}, f32[64,1024]{1,0:T(8,128)}, u32[]{:S(2)}) copy-start(f32[64,1024]{1,0:T(8,128)} %refs_5_.1) | copy-start | bytes 786436
  108.2 34.0 %copy-start.4 = (f32[64,1024]{1,0:T(8,128)S(1)}, f32[64,1024]{1,0:T(8,128)}, u32[]{:S(2)}) copy-start(f32[64,1024]{1,0:T(8,128)} %refs_6_.1) | copy-start | bytes 786436
  108.2 34.0 %copy-start.5 = (f32[64,1024]{1,0:T(8,128)S(1)}, f32[64,1024]{1,0:T(8,128)}, u32[]{:S(2)}) copy-start(f32[64,1024]{1,0:T(8,128)} %refs_7_.1) | copy-start | bytes 786436
  108.2 34.0 %copy-start.6 = (f32[256,16]{0,1:T(8,128)S(1)}, f32[256,16]{0,1:T(8,128)}, u32[]{:S(2)}) copy-start(f32[256,16]{0,1:T(8,128)} %param.26) | copy-start | bytes 49156
  108.2 34.0 %copy-start.7 = (f32[256,16]{0,1:T(8,128)S(1)}, f32[256,16]{0,1:T(8,128)}, u32[]{:S(2)}) copy-start(f32[256,16]{0,1:T(8,128)} %param.27) | copy-start | bytes 49156
  108.2 9.0 %collective-permute-start.27 = (bf16[256,640]{1,0:T(8,128)(2,1)S(1)}, bf16[256,640]{1,0:T(8,128)(2,1)S(1)}, u32[]{:S(2)}, u32[]{:S(2)}) collective-permute-start(bf16[256,640]{1,0:T(8,128)(2,1)S(1)} %get-tuple-element.91), channel_id=1, source_target_pairs={{0,4},{2,6},{4,0},{6,2},{8,12},{10,14},{12,8},{14,10},{16,20},{18,... | collective-permute-start | bytes 983048 | tf_op jit(solution)/shard_map/ppermute | solution.py:40
  117.3 5.6 %collective-permute-start.28 = (bf16[128,640]{1,0:T(8,128)(2,1)S(1)}, bf16[128,640]{1,0:T(8,128)(2,1)S(1)}, u32[]{:S(2)}, u32[]{:S(2)}) collective-permute-start(bf16[128,640]{1,0:T(8,128)(2,1)S(1)} %get-tuple-element.93), channel_id=1, source_target_pairs={{0,8},{2,10},{4,12},{6,14},{8,0},{10,2},{12,4},{14,6},{16,24},{18,... | collective-permute-start | bytes 491528 | tf_op jit(solution)/shard_map/ppermute | solution.py:40
  117.5 7.0 %collective-permute-start.30 = (bf16[128,384]{1,0:T(8,128)(2,1)S(1)}, bf16[128,384]{1,0:T(8,128)(2,1)S(1)}, u32[]{:S(2)}, u32[]{:S(2)}) collective-permute-start(bf16[128,384]{1,0:T(8,128)(2,1)S(1)} %get-tuple-element.87), channel_id=1, source_target_pairs={{0,8},{2,10},{4,12},{6,14},{8,0},{10,2},{12,4},{14,6},{16,24},{18,... | collective-permute-start | bytes 294920 | tf_op jit(solution)/shard_map/ppermute | solution.py:40
  122.9 6.8 %collective-permute-start.29 = (bf16[64,640]{1,0:T(8,128)(2,1)S(1)}, bf16[64,640]{1,0:T(8,128)(2,1)S(1)}, u32[]{:S(2)}, u32[]{:S(2)}) collective-permute-start(bf16[64,640]{1,0:T(8,128)(2,1)S(1)} %get-tuple-element.95), channel_id=1, source_target_pairs={{0,16},{2,18},{4,20},{6,22},{8,24},{10,26},{12,28},{14,30},{16,0},... | collective-permute-start | bytes 245768 | tf_op jit(solution)/shard_map/ppermute | solution.py:40
  124.6 5.1 %collective-permute-start.31 = (bf16[64,384]{1,0:T(8,128)(2,1)S(1)}, bf16[64,384]{1,0:T(8,128)(2,1)S(1)}, u32[]{:S(2)}, u32[]{:S(2)}) collective-permute-start(bf16[64,384]{1,0:T(8,128)(2,1)S(1)} %get-tuple-element.99), channel_id=1, source_target_pairs={{0,16},{2,18},{4,20},{6,22},{8,24},{10,26},{12,28},{14,30},{16,0},... | collective-permute-start | bytes 147464 | tf_op jit(solution)/shard_map/ppermute | solution.py:40

commit v4 on v3

--- a/solution.py
+++ b/solution.py
@@ -20,7 +20,7 @@
 SCRATCH = 16 << 20
 BIAS_A = 8_000_000_000
 BIAS_C = 1
-T1 = 1
+T1 = 0
 T2 = 0
 BF = jnp.bfloat16
 F32 = jnp.float32

time: 144 us -> 132 us (0.917)
  waiting for transfers between devices: 72.9 us -> 61.9 us
    ppermute x32, waiting for transfers between devices: 72.9 us -> 61.9 us  [swap(): return lax.ppermute(x, axis, [(i, i ^ mask) for i in range(size)])]
  transfers between devices with their start and end apart: 32 -> 32, of which waited for: 26 -> 28; matrix products, arithmetic and copies ran while one was open for 0% -> 0% of each run, Pallas kernels for 3% -> 4%
where the time goes in v4:
time: 132 us
  waiting for transfers between devices  61.9 us (47%)
  starting transfers between devices  37.4 us (28%)
  blocking collectives  16.8 us (13%)
  Pallas kernels  11 us (8%)
  local copies, waits for them, and re-layouts  2.48 us (2%)
    ppermute x32, waiting for transfers between devices, swap(): return lax.ppermute(x, axis, [(i, i ^ mask) for i in range(size)])  61.9 us
    ppermute x32, starting transfers between devices, swap(): return lax.ppermute(x, axis, [(i, i ^ mask) for i in range(size)])  37.4 us
    all_to_all x1, blocking collectives, on_device(): spread = lax.all_to_all(spread, (*BLK, 'feat'), 0, 0, tiled=True)  11.9 us
    pallas_call x22, Pallas kernels, call(): pl.pallas_call(body, out_shape=[shapes(shape, dtype) for shape, dtype in...  11 us
  transfers between devices with their start and end apart: 32, of which 28 were waited for; matrix products, arithmetic and copies ran while one was open for 0% of the time, Pallas kernels for 4%

profile of v4, /device:TPU:0, one launch (start us, length us, event | category | flops | bytes accessed | tf_op | source)
XLA Modules:
  0.0 131.8 jit_solution(10561470962893791341)
XLA Ops:
  0.6 1.0 convert_element_type.3
  1.6 4.1 %collective-permute-start = (bf16[64,384]{1,0:T(8,128)(2,1)S(1)}, bf16[64,384]{1,0:T(8,128)(2,1)S(1)}, u32[]{:S(2)}, u32[]{:S(2)}) collective-permute-start(bf16[64,384]{1,0:T(8,128)(2,1)S(1)} %slice.8), channel_id=1, source_target_pairs={{0,16},{2,18},{4,20},{6,22},{8,24},{10,26},{12,28},{14,30},{16,0},... | collective-permute-start | bytes 147464 | tf_op jit(solution)/shard_map/ppermute | solution.py:40
  5.9 1.0 copy-done.2
  8.3 1.0 prepare.1.masked
  9.3 2.0 %collective-permute-start.1 = (bf16[128,384]{1,0:T(8,128)(2,1)S(1)}, bf16[128,384]{1,0:T(8,128)(2,1)S(1)}, u32[]{:S(2)}, u32[]{:S(2)}) collective-permute-start(bf16[128,384]{1,0:T(8,128)(2,1)S(1)} %pad_maximum_fusion.5), channel_id=1, source_target_pairs={{0,8},{2,10},{4,12},{6,14},{8,0},{10,2},{12,4},{14,6},{16,24},{18,... | collective-permute-start | bytes 294920 | tf_op jit(solution)/shard_map/ppermute | solution.py:40
  11.3 1.5 %collective-permute-done.4 = bf16[64,640]{1,0:T(8,128)(2,1)S(1)} collective-permute-done((bf16[64,640]{1,0:T(8,128)(2,1)S(1)}, bf16[64,640]{1,0:T(8,128)(2,1)S(1)}, u32[]{:S(2)}, u32[]{:S(2)}) %collective-permute-start.4) | collective-permute-done | bytes 81952 | tf_op jit(solution)/shard_map/ppermute | solution.py:40
  12.9 2.2 %collective-permute-done.1 = bf16[128,384]{1,0:T(8,128)(2,1)S(1)} collective-permute-done((bf16[128,384]{1,0:T(8,128)(2,1)S(1)}, bf16[128,384]{1,0:T(8,128)(2,1)S(1)}, u32[]{:S(2)}, u32[]{:S(2)}) %collective-permute-start.1) | collective-permute-done | bytes 98336 | tf_op jit(solution)/shard_map/ppermute | solution.py:40
  15.1 1.9 %collective-permute-start.2 = (bf16[256,384]{1,0:T(8,128)(2,1)S(1)}, bf16[256,384]{1,0:T(8,128)(2,1)S(1)}, u32[]{:S(2)}, u32[]{:S(2)}) collective-permute-start(bf16[256,384]{1,0:T(8,128)(2,1)S(1)} %pad_maximum_fusion.3), channel_id=1, source_target_pairs={{0,4},{2,6},{4,0},{6,2},{8,12},{10,14},{12,8},{14,10},{16,20},{18,... | collective-permute-start | bytes 589832 | tf_op jit(solution)/shard_map/ppermute | solution.py:40
  17.0 1.2 collective-permute-done.5
  18.2 1.6 %collective-permute-start.6 = (bf16[256,640]{1,0:T(8,128)(2,1)S(1)}, bf16[256,640]{1,0:T(8,128)(2,1)S(1)}, u32[]{:S(2)}, u32[]{:S(2)}) collective-permute-start(bf16[256,640]{1,0:T(8,128)(2,1)S(1)} %pad_maximum_fusion.2), channel_id=1, source_target_pairs={{0,4},{2,6},{4,0},{6,2},{8,12},{10,14},{12,8},{14,10},{16,20},{18,... | collective-permute-start | bytes 983048 | tf_op jit(solution)/shard_map/ppermute | solution.py:40
  19.8 3.1 %collective-permute-done.2 = bf16[256,384]{1,0:T(8,128)(2,1)S(1)} collective-permute-done((bf16[256,384]{1,0:T(8,128)(2,1)S(1)}, bf16[256,384]{1,0:T(8,128)(2,1)S(1)}, u32[]{:S(2)}, u32[]{:S(2)}) %collective-permute-start.2) | collective-permute-done | bytes 196640 | tf_op jit(solution)/shard_map/ppermute | solution.py:40
  23.0 2.5 %all_gather.6.refs_0_ = bf16[1024,384]{1,0:T(8,128)(2,1)S(1)} all-gather(bf16[512,384]{1,0:T(8,128)(2,1)S(1)} %pad_maximum_fusion.1), channel_id=1, replica_groups=mesh['hi'=8,'core'=2,'feat'=2] {'core'}, dimensions={0}, use_global_device_ids=true | all-gather | bytes 1179648 | tf_op jit(solution)/shard_map/all_gather | solution.py:351
  25.9 1.7 %collective-permute-start.3 = (bf16[256,384]{1,0:T(8,128)(2,1)S(1)}, bf16[256,384]{1,0:T(8,128)(2,1)S(1)}, u32[]{:S(2)}, u32[]{:S(2)}) collective-permute-start(bf16[256,384]{1,0:T(8,128)(2,1)S(1)} %get-tuple-element.62.hidden), channel_id=1, source_target_pairs={{0,1},{1,0},{2,3},{3,2},{4,5},{5,4},{6,7},{7,6},{8,9},{9,8},{10,11... | collective-permute-start | bytes 589832 | tf_op jit(solution)/shard_map/ppermute | solution.py:40
  28.2 4.7 %collective-permute-done.3.far = bf16[256,384]{1,0:T(8,128)(2,1)S(1)} collective-permute-done((bf16[256,384]{1,0:T(8,128)(2,1)S(1)}, bf16[256,384]{1,0:T(8,128)(2,1)S(1)}, u32[]{:S(2)}, u32[]{:S(2)}) %collective-permute-start.3) | collective-permute-done | bytes 196640 | tf_op jit(solution)/shard_map/ppermute | solution.py:40
  34.3 1.7 %collective-permute-start.8 = (bf16[256,640]{1,0:T(8,128)(2,1)S(1)}, bf16[256,640]{1,0:T(8,128)(2,1)S(1)}, u32[]{:S(2)}, u32[]{:S(2)}) collective-permute-start(bf16[256,640]{1,0:T(8,128)(2,1)S(1)} %get-tuple-element.64.hidden), channel_id=1, source_target_pairs={{0,1},{1,0},{2,3},{3,2},{4,5},{5,4},{6,7},{7,6},{8,9},{9,8},{10,11... | collective-permute-start | bytes 983048 | tf_op jit(solution)/shard_map/ppermute | solution.py:40
  36.6 6.6 %collective-permute-done.8.far = bf16[256,640]{1,0:T(8,128)(2,1)S(1)} collective-permute-done((bf16[256,640]{1,0:T(8,128)(2,1)S(1)}, bf16[256,640]{1,0:T(8,128)(2,1)S(1)}, u32[]{:S(2)}, u32[]{:S(2)}) %collective-permute-start.8) | collective-permute-done | bytes 327712 | tf_op jit(solution)/shard_map/ppermute | solution.py:40
  43.3 2.1 %features.1 = (bf16[256,1024]{1,0:T(8,128)(2,1)S(1)}, f32[256,1024]{1,0:T(8,128)S(1)}, f32[8,1152]{1,0:T(8,128)S(1)}, f32[8,1152]{1,0:T(8,128)S(1)}) custom-call(f32[256,1024]{1,0:T(8,128)S(1)} %second_pre.1.pre, bf16[256,640]{1,0:T(8,128)(2,1)S(1)} %collective-permute-done.8.far, bf16[2048,1024]{1,0:T(8,128)(2,1)S(1)} %copy-done, f32[16,256]{1,0:T(8,128)S(1)} %bitcast.14, ...), custom_call_target="tpu_custom_call" | custom-call | flops 1 | bytes 1 | tf_op jit(solution)/shard_map/features/pallas_call | solution.py:85
  45.4 1.2 collective-permute-done.9
  46.6 1.6 %collective-permute-start.10 = (f32[8,1152]{1,0:T(8,128)S(1)}, f32[8,1152]{1,0:T(8,128)S(1)}, u32[]{:S(2)}, u32[]{:S(2)}) collective-permute-start(f32[8,1152]{1,0:T(8,128)S(1)} %add.30), channel_id=1, source_target_pairs={{0,4},{2,6},{4,0},{6,2},{8,12},{10,14},{12,8},{14,10},{16,20},{18,... | collective-permute-start | bytes 110600 | tf_op jit(solution)/shard_map/ppermute | solution.py:40
  48.2 1.9 %collective-permute-start.12 = (f32[8,1152]{1,0:T(8,128)S(1)}, f32[8,1152]{1,0:T(8,128)S(1)}, u32[]{:S(2)}, u32[]{:S(2)}) collective-permute-start(f32[8,1152]{1,0:T(8,128)S(1)} %add.30), channel_id=1, source_target_pairs={{0,12},{2,14},{4,8},{6,10},{8,4},{10,6},{12,0},{14,2},{16,28},{18,... | collective-permute-start | bytes 110600 | tf_op jit(solution)/shard_map/ppermute | solution.py:40
  50.6 1.6 %collective-permute-done.11 = f32[8,1152]{1,0:T(8,128)S(1)} collective-permute-done((f32[8,1152]{1,0:T(8,128)S(1)}, f32[8,1152]{1,0:T(8,128)S(1)}, u32[]{:S(2)}, u32[]{:S(2)}) %collective-permute-start.11) | collective-permute-done | bytes 36896 | tf_op jit(solution)/shard_map/ppermute | solution.py:40
  53.1 2.7 %collective-permute-start.13 = (f32[8,1152]{1,0:T(8,128)S(1)}, f32[8,1152]{1,0:T(8,128)S(1)}, u32[]{:S(2)}, u32[]{:S(2)}) collective-permute-start(f32[8,1152]{1,0:T(8,128)S(1)} %add_add_fusion.1), channel_id=1, source_target_pairs={{0,16},{2,18},{4,20},{6,22},{8,24},{10,26},{12,28},{14,30},{16,0},... | collective-permute-start | bytes 110600 | tf_op jit(solution)/shard_map/ppermute | solution.py:40
  55.8 2.2 %collective-permute-done.13 = f32[8,1152]{1,0:T(8,128)S(1)} collective-permute-done((f32[8,1152]{1,0:T(8,128)S(1)}, f32[8,1152]{1,0:T(8,128)S(1)}, u32[]{:S(2)}, u32[]{:S(2)}) %collective-permute-start.13) | collective-permute-done | bytes 36896 | tf_op jit(solution)/shard_map/ppermute | solution.py:40
  58.0 1.2 collective-permute-done.14.other
  59.5 1.6 %collective-permute-start.15 = (f32[16,256]{1,0:T(8,128)S(1)}, f32[16,256]{1,0:T(8,128)S(1)}, u32[]{:S(2)}, u32[]{:S(2)}) collective-permute-start(f32[16,256]{1,0:T(8,128)S(1)} %get-tuple-element.68.near), channel_id=1, source_target_pairs={{0,1},{1,0},{2,3},{3,2},{4,5},{5,4},{6,7},{7,6},{8,9},{9,8},{10,11... | collective-permute-start | bytes 49160 | tf_op jit(solution)/shard_map/ppermute | solution.py:40
  61.1 2.2 %collective-permute-done.15.far = f32[16,256]{1,0:T(8,128)S(1)} collective-permute-done((f32[16,256]{1,0:T(8,128)S(1)}, f32[16,256]{1,0:T(8,128)S(1)}, u32[]{:S(2)}, u32[]{:S(2)}) %collective-permute-start.15) | collective-permute-done | bytes 16416 | tf_op jit(solution)/shard_map/ppermute | solution.py:40
  63.5 1.2 collective-permute-done.16
  64.7 1.0 collective-permute-start.17
  65.7 1.5 %collective-permute-start.18 = (f32[8,1152]{1,0:T(8,128)S(1)}, f32[8,1152]{1,0:T(8,128)S(1)}, u32[]{:S(2)}, u32[]{:S(2)}) collective-permute-start(f32[8,1152]{1,0:T(8,128)S(1)} %add.35), channel_id=1, source_target_pairs={{0,8},{2,10},{4,12},{6,14},{8,0},{10,2},{12,4},{14,6},{16,24},{18,... | collective-permute-start | bytes 110600 | tf_op jit(solution)/shard_map/ppermute | solution.py:40
  67.2 1.0 collective-permute-start.19
  69.6 2.4 %collective-permute-done.19 = f32[8,1152]{1,0:T(8,128)S(1)} collective-permute-done((f32[8,1152]{1,0:T(8,128)S(1)}, f32[8,1152]{1,0:T(8,128)S(1)}, u32[]{:S(2)}, u32[]{:S(2)}) %collective-permute-start.19) | collective-permute-done | bytes 36896 | tf_op jit(solution)/shard_map/ppermute | solution.py:40
  72.0 1.5 %collective-permute-start.20 = (f32[8,1152]{1,0:T(8,128)S(1)}, f32[8,1152]{1,0:T(8,128)S(1)}, u32[]{:S(2)}, u32[]{:S(2)}) collective-permute-start(f32[8,1152]{1,0:T(8,128)S(1)} %add_add_fusion), channel_id=1, source_target_pairs={{0,16},{2,18},{4,20},{6,22},{8,24},{10,26},{12,28},{14,30},{16,0},... | collective-permute-start | bytes 110600 | tf_op jit(solution)/shard_map/ppermute | solution.py:40
  73.6 3.7 %collective-permute-done.20 = f32[8,1152]{1,0:T(8,128)S(1)} collective-permute-done((f32[8,1152]{1,0:T(8,128)S(1)}, f32[8,1152]{1,0:T(8,128)S(1)}, u32[]{:S(2)}, u32[]{:S(2)}) %collective-permute-start.20) | collective-permute-done | bytes 36896 | tf_op jit(solution)/shard_map/ppermute | solution.py:40
  77.3 1.2 collective-permute-done.21.other
  79.8 1.6 %collective-permute-start.22 = (bf16[256,640]{1,0:T(8,128)(2,1)S(1)}, bf16[256,640]{1,0:T(8,128)(2,1)S(1)}, u32[]{:S(2)}, u32[]{:S(2)}) collective-permute-start(bf16[256,640]{1,0:T(8,128)(2,1)S(1)} %second_away.1), channel_id=1, source_target_pairs={{0,1},{1,0},{2,3},{3,2},{4,5},{5,4},{6,7},{7,6},{8,9},{9,8},{10,11... | collective-permute-start | bytes 983048 | tf_op jit(solution)/shard_map/ppermute | solution.py:40
  82.8 7.2 %collective-permute-done.23.refs_1_ = f32[16,256]{1,0:T(8,128)S(1)} collective-permute-done((f32[16,256]{1,0:T(8,128)S(1)}, f32[16,256]{1,0:T(8,128)S(1)}, u32[]{:S(2)}, u32[]{:S(2)}) %collective-permute-start.23) | collective-permute-done | bytes 16416 | tf_op jit(solution)/shard_map/ppermute | solution.py:40
  90.7 1.6 %collective-permute-start.28 = (bf16[256,384]{1,0:T(8,128)(2,1)S(1)}, bf16[256,384]{1,0:T(8,128)(2,1)S(1)}, u32[]{:S(2)}, u32[]{:S(2)}) collective-permute-start(bf16[256,384]{1,0:T(8,128)(2,1)S(1)} %get-tuple-element.88), channel_id=1, source_target_pairs={{0,1},{1,0},{2,3},{3,2},{4,5},{5,4},{6,7},{7,6},{8,9},{9,8},{10,11... | collective-permute-start | bytes 589832 | tf_op jit(solution)/shard_map/ppermute | solution.py:40
  92.9 1.3 collective-permute-start.25
  94.3 3.8 %collective-permute-done.28.got = bf16[256,384]{1,0:T(8,128)(2,1)S(1)} collective-permute-done((bf16[256,384]{1,0:T(8,128)(2,1)S(1)}, bf16[256,384]{1,0:T(8,128)(2,1)S(1)}, u32[]{:S(2)}, u32[]{:S(2)}) %collective-permute-start.28) | collective-permute-done | bytes 196640 | tf_op jit(solution)/shard_map/ppermute | solution.py:40
  98.5 2.4 %all_gather.7.got = bf16[1024,384]{1,0:T(8,128)(2,1)S(1)} all-gather(bf16[512,384]{1,0:T(8,128)(2,1)S(1)} %get-tuple-element.91), channel_id=1, replica_groups=mesh['hi'=8,'core'=2,'feat'=2] {'core'}, dimensions={0}, use_global_device_ids=true | all-gather | bytes 1179648 | tf_op jit(solution)/shard_map/all_gather | solution.py:434
  101.0 1.3 collective-permute-start.29
  103.1 4.8 %collective-permute-done.29.got = bf16[256,384]{1,0:T(8,128)(2,1)S(1)} collective-permute-done((bf16[256,384]{1,0:T(8,128)(2,1)S(1)}, bf16[256,384]{1,0:T(8,128)(2,1)S(1)}, u32[]{:S(2)}, u32[]{:S(2)}) %collective-permute-start.29) | collective-permute-done | bytes 196640 | tf_op jit(solution)/shard_map/ppermute | solution.py:40
  108.5 2.6 %collective-permute-start.27 = (bf16[64,640]{1,0:T(8,128)(2,1)S(1)}, bf16[64,640]{1,0:T(8,128)(2,1)S(1)}, u32[]{:S(2)}, u32[]{:S(2)}) collective-permute-start(bf16[64,640]{1,0:T(8,128)(2,1)S(1)} %get-tuple-element.86), channel_id=1, source_target_pairs={{0,16},{2,18},{4,20},{6,22},{8,24},{10,26},{12,28},{14,30},{16,0},... | collective-permute-start | bytes 245768 | tf_op jit(solution)/shard_map/ppermute | solution.py:40
  111.0 1.9 %collective-permute-done.30.got = bf16[128,384]{1,0:T(8,128)(2,1)S(1)} collective-permute-done((bf16[128,384]{1,0:T(8,128)(2,1)S(1)}, bf16[128,384]{1,0:T(8,128)(2,1)S(1)}, u32[]{:S(2)}, u32[]{:S(2)}) %collective-permute-start.30) | collective-permute-done | bytes 98336 | tf_op jit(solution)/shard_map/ppermute | solution.py:40
  113.0 1.8 %collective-permute-start.31 = (bf16[64,384]{1,0:T(8,128)(2,1)S(1)}, bf16[64,384]{1,0:T(8,128)(2,1)S(1)}, u32[]{:S(2)}, u32[]{:S(2)}) collective-permute-start(bf16[64,384]{1,0:T(8,128)(2,1)S(1)} %get-tuple-element.97), channel_id=1, source_target_pairs={{0,16},{2,18},{4,20},{6,22},{8,24},{10,26},{12,28},{14,30},{16,0},... | collective-permute-start | bytes 147464 | tf_op jit(solution)/shard_map/ppermute | solution.py:40
  114.7 3.5 %collective-permute-done.31.got = bf16[64,384]{1,0:T(8,128)(2,1)S(1)} collective-permute-done((bf16[64,384]{1,0:T(8,128)(2,1)S(1)}, bf16[64,384]{1,0:T(8,128)(2,1)S(1)}, u32[]{:S(2)}, u32[]{:S(2)}) %collective-permute-start.31) | collective-permute-done | bytes 49184 | tf_op jit(solution)/shard_map/ppermute | solution.py:40
  118.6 11.9 %all_to_all.5.refs_0_ = f32[32,1,128]{2,1,0:T(1,128)S(1)} all-to-all(f32[32,1,128]{2,1,0:T(1,128)S(1)} %get-tuple-element.99), channel_id=1, replica_groups=mesh['hi'=8,'core'=2,'feat'=2] {'hi','core','feat'}, dimensions={0} | all-to-all | bytes 32768 | tf_op jit(solution)/shard_map/all_to_all | solution.py:463
  130.6 1.2 update.1
  (84 shorter events, 14.2 us)
Async XLA Ops:
  1.6 7.7 %collective-permute-start = (bf16[64,384]{1,0:T(8,128)(2,1)S(1)}, bf16[64,384]{1,0:T(8,128)(2,1)S(1)}, u32[]{:S(2)}, u32[]{:S(2)}) collective-permute-start(bf16[64,384]{1,0:T(8,128)(2,1)S(1)} %slice.8), channel_id=1, source_target_pairs={{0,16},{2,18},{4,20},{6,22},{8,24},{10,26},{12,28},{14,30},{16,0},... | collective-permute-start | bytes 147464 | tf_op jit(solution)/shard_map/ppermute | solution.py:40
  5.8 7.0 %collective-permute-start.4 = (bf16[64,640]{1,0:T(8,128)(2,1)S(1)}, bf16[64,640]{1,0:T(8,128)(2,1)S(1)}, u32[]{:S(2)}, u32[]{:S(2)}) collective-permute-start(bf16[64,640]{1,0:T(8,128)(2,1)S(1)} %slice.9), channel_id=1, source_target_pairs={{0,16},{2,18},{4,20},{6,22},{8,24},{10,26},{12,28},{14,30},{16,0},... | collective-permute-start | bytes 245768 | tf_op jit(solution)/shard_map/ppermute | solution.py:40
  5.9 1.0 copy-start.2
  6.9 0.7 copy-start.9
  7.6 0.7 copy-start.11
  9.3 5.7 %collective-permute-start.1 = (bf16[128,384]{1,0:T(8,128)(2,1)S(1)}, bf16[128,384]{1,0:T(8,128)(2,1)S(1)}, u32[]{:S(2)}, u32[]{:S(2)}) collective-permute-start(bf16[128,384]{1,0:T(8,128)(2,1)S(1)} %pad_maximum_fusion.5), channel_id=1, source_target_pairs={{0,8},{2,10},{4,12},{6,14},{8,0},{10,2},{12,4},{14,6},{16,24},{18,... | collective-permute-start | bytes 294920 | tf_op jit(solution)/shard_map/ppermute | solution.py:40
  12.8 5.4 %collective-permute-start.5 = (bf16[128,640]{1,0:T(8,128)(2,1)S(1)}, bf16[128,640]{1,0:T(8,128)(2,1)S(1)}, u32[]{:S(2)}, u32[]{:S(2)}) collective-permute-start(bf16[128,640]{1,0:T(8,128)(2,1)S(1)} %pad_maximum_fusion.4), channel_id=1, source_target_pairs={{0,8},{2,10},{4,12},{6,14},{8,0},{10,2},{12,4},{14,6},{16,24},{18,... | collective-permute-start | bytes 491528 | tf_op jit(solution)/shard_map/ppermute | solution.py:40
  15.1 7.8 %collective-permute-start.2 = (bf16[256,384]{1,0:T(8,128)(2,1)S(1)}, bf16[256,384]{1,0:T(8,128)(2,1)S(1)}, u32[]{:S(2)}, u32[]{:S(2)}) collective-permute-start(bf16[256,384]{1,0:T(8,128)(2,1)S(1)} %pad_maximum_fusion.3), channel_id=1, source_target_pairs={{0,4},{2,6},{4,0},{6,2},{8,12},{10,14},{12,8},{14,10},{16,20},{18,... | collective-permute-start | bytes 589832 | tf_op jit(solution)/shard_map/ppermute | solution.py:40
  18.2 9.9 %collective-permute-start.6 = (bf16[256,640]{1,0:T(8,128)(2,1)S(1)}, bf16[256,640]{1,0:T(8,128)(2,1)S(1)}, u32[]{:S(2)}, u32[]{:S(2)}) collective-permute-start(bf16[256,640]{1,0:T(8,128)(2,1)S(1)} %pad_maximum_fusion.2), channel_id=1, source_target_pairs={{0,4},{2,6},{4,0},{6,2},{8,12},{10,14},{12,8},{14,10},{16,20},{18,... | collective-permute-start | bytes 983048 | tf_op jit(solution)/shard_map/ppermute | solution.py:40
  22.9 10.0 %copy-start = (bf16[2048,1024]{1,0:T(8,128)(2,1)S(1)}, bf16[2048,1024]{1,0:T(8,128)(2,1)}, u32[]{:S(2)}) copy-start(bf16[2048,1024]{1,0:T(8,128)(2,1)} %freq.11) | copy-start | bytes 12582916
  25.5 7.5 %copy-start.13 = (f32[1024]{0:T(1024)S(1)}, f32[1024]{0:T(1024)}, u32[]{:S(2)}) copy-start(f32[1024]{0:T(1024)} %param.19) | copy-start | bytes 12292
  25.9 7.0 %collective-permute-start.3 = (bf16[256,384]{1,0:T(8,128)(2,1)S(1)}, bf16[256,384]{1,0:T(8,128)(2,1)S(1)}, u32[]{:S(2)}, u32[]{:S(2)}) collective-permute-start(bf16[256,384]{1,0:T(8,128)(2,1)S(1)} %get-tuple-element.62.hidden), channel_id=1, source_target_pairs={{0,1},{1,0},{2,3},{3,2},{4,5},{5,4},{6,7},{7,6},{8,9},{9,8},{10,11... | collective-permute-start | bytes 589832 | tf_op jit(solution)/shard_map/ppermute | solution.py:40
  28.2 5.5 %collective-permute-start.7 = (bf16[512,640]{1,0:T(8,128)(2,1)S(1)}, bf16[512,640]{1,0:T(8,128)(2,1)S(1)}, u32[]{:S(2)}, u32[]{:S(2)}) collective-permute-start(bf16[512,640]{1,0:T(8,128)(2,1)S(1)} %pad_maximum_fusion.refs_0_), channel_id=1, source_target_pairs={{0,2},{2,0},{4,6},{6,4},{8,10},{10,8},{12,14},{14,12},{16,18},{18,... | collective-permute-start | bytes 1966088 | tf_op jit(solution)/shard_map/ppermute | solution.py:40
  34.3 9.0 %copy-start.3 = (f32[256,16]{0,1:T(8,128)S(1)}, f32[256,16]{0,1:T(8,128)}, u32[]{:S(2)}) copy-start(f32[256,16]{0,1:T(8,128)} %param.25) | copy-start | bytes 49156
  34.3 9.0 %copy-start.10 = (s32[256]{0:T(256)S(1)}, s32[256]{0:T(256)}, u32[]{:S(2)}) copy-start(s32[256]{0:T(256)} %param.16) | copy-start | bytes 3076
  34.3 9.0 %collective-permute-start.8 = (bf16[256,640]{1,0:T(8,128)(2,1)S(1)}, bf16[256,640]{1,0:T(8,128)(2,1)S(1)}, u32[]{:S(2)}, u32[]{:S(2)}) collective-permute-start(bf16[256,640]{1,0:T(8,128)(2,1)S(1)} %get-tuple-element.64.hidden), channel_id=1, source_target_pairs={{0,1},{1,0},{2,3},{3,2},{4,5},{5,4},{6,7},{7,6},{8,9},{9,8},{10,11... | collective-permute-start | bytes 983048 | tf_op jit(solution)/shard_map/ppermute | solution.py:40
  43.2 20.0 %copy-start.8 = (f32[256,16]{0,1:T(8,128)S(1)}, f32[256,16]{0,1:T(8,128)}, u32[]{:S(2)}) copy-start(f32[256,16]{0,1:T(8,128)} %param.21) | copy-start | bytes 49156
  43.2 20.0 %copy-start.12 = (f32[256]{0:T(256)S(1)}, f32[256]{0:T(256)}, u32[]{:S(2)}) copy-start(f32[256]{0:T(256)} %param.20) | copy-start | bytes 3076
  45.3 1.3 collective-permute-start.9
  46.6 4.0 %collective-permute-start.10 = (f32[8,1152]{1,0:T(8,128)S(1)}, f32[8,1152]{1,0:T(8,128)S(1)}, u32[]{:S(2)}, u32[]{:S(2)}) collective-permute-start(f32[8,1152]{1,0:T(8,128)S(1)} %add.30), channel_id=1, source_target_pairs={{0,4},{2,6},{4,0},{6,2},{8,12},{10,14},{12,8},{14,10},{16,20},{18,... | collective-permute-start | bytes 110600 | tf_op jit(solution)/shard_map/ppermute | solution.py:40
  48.2 4.0 %collective-permute-start.11 = (f32[8,1152]{1,0:T(8,128)S(1)}, f32[8,1152]{1,0:T(8,128)S(1)}, u32[]{:S(2)}, u32[]{:S(2)}) collective-permute-start(f32[8,1152]{1,0:T(8,128)S(1)} %add.30), channel_id=1, source_target_pairs={{0,8},{2,10},{4,12},{6,14},{8,0},{10,2},{12,4},{14,6},{16,24},{18,... | collective-permute-start | bytes 110600 | tf_op jit(solution)/shard_map/ppermute | solution.py:40
  48.2 4.9 %collective-permute-start.12 = (f32[8,1152]{1,0:T(8,128)S(1)}, f32[8,1152]{1,0:T(8,128)S(1)}, u32[]{:S(2)}, u32[]{:S(2)}) collective-permute-start(f32[8,1152]{1,0:T(8,128)S(1)} %add.30), channel_id=1, source_target_pairs={{0,12},{2,14},{4,8},{6,10},{8,4},{10,6},{12,0},{14,2},{16,28},{18,... | collective-permute-start | bytes 110600 | tf_op jit(solution)/shard_map/ppermute | solution.py:40
  53.1 4.9 %collective-permute-start.13 = (f32[8,1152]{1,0:T(8,128)S(1)}, f32[8,1152]{1,0:T(8,128)S(1)}, u32[]{:S(2)}, u32[]{:S(2)}) collective-permute-start(f32[8,1152]{1,0:T(8,128)S(1)} %add_add_fusion.1), channel_id=1, source_target_pairs={{0,16},{2,18},{4,20},{6,22},{8,24},{10,26},{12,28},{14,30},{16,0},... | collective-permute-start | bytes 110600 | tf_op jit(solution)/shard_map/ppermute | solution.py:40
  58.0 1.2 collective-permute-start.14
  59.5 3.8 %collective-permute-start.15 = (f32[16,256]{1,0:T(8,128)S(1)}, f32[16,256]{1,0:T(8,128)S(1)}, u32[]{:S(2)}, u32[]{:S(2)}) collective-permute-start(f32[16,256]{1,0:T(8,128)S(1)} %get-tuple-element.68.near), channel_id=1, source_target_pairs={{0,1},{1,0},{2,3},{3,2},{4,5},{5,4},{6,7},{7,6},{8,9},{9,8},{10,11... | collective-permute-start | bytes 49160 | tf_op jit(solution)/shard_map/ppermute | solution.py:40
  63.5 1.2 collective-permute-start.16
  64.7 4.0 %collective-permute-start.17 = (f32[8,1152]{1,0:T(8,128)S(1)}, f32[8,1152]{1,0:T(8,128)S(1)}, u32[]{:S(2)}, u32[]{:S(2)}) collective-permute-start(f32[8,1152]{1,0:T(8,128)S(1)} %add.35), channel_id=1, source_target_pairs={{0,4},{2,6},{4,0},{6,2},{8,12},{10,14},{12,8},{14,10},{16,20},{18,... | collective-permute-start | bytes 110600 | tf_op jit(solution)/shard_map/ppermute | solution.py:40
  65.7 4.0 %collective-permute-start.18 = (f32[8,1152]{1,0:T(8,128)S(1)}, f32[8,1152]{1,0:T(8,128)S(1)}, u32[]{:S(2)}, u32[]{:S(2)}) collective-permute-start(f32[8,1152]{1,0:T(8,128)S(1)} %add.35), channel_id=1, source_target_pairs={{0,8},{2,10},{4,12},{6,14},{8,0},{10,2},{12,4},{14,6},{16,24},{18,... | collective-permute-start | bytes 110600 | tf_op jit(solution)/shard_map/ppermute | solution.py:40
  67.2 4.9 %collective-permute-start.19 = (f32[8,1152]{1,0:T(8,128)S(1)}, f32[8,1152]{1,0:T(8,128)S(1)}, u32[]{:S(2)}, u32[]{:S(2)}) collective-permute-start(f32[8,1152]{1,0:T(8,128)S(1)} %add.35), channel_id=1, source_target_pairs={{0,12},{2,14},{4,8},{6,10},{8,4},{10,6},{12,0},{14,2},{16,28},{18,... | collective-permute-start | bytes 110600 | tf_op jit(solution)/shard_map/ppermute | solution.py:40
  72.0 5.3 %collective-permute-start.20 = (f32[8,1152]{1,0:T(8,128)S(1)}, f32[8,1152]{1,0:T(8,128)S(1)}, u32[]{:S(2)}, u32[]{:S(2)}) collective-permute-start(f32[8,1152]{1,0:T(8,128)S(1)} %add_add_fusion), channel_id=1, source_target_pairs={{0,16},{2,18},{4,20},{6,22},{8,24},{10,26},{12,28},{14,30},{16,0},... | collective-permute-start | bytes 110600 | tf_op jit(solution)/shard_map/ppermute | solution.py:40
  77.3 1.2 collective-permute-start.21
  79.8 10.2 %collective-permute-start.22 = (bf16[256,640]{1,0:T(8,128)(2,1)S(1)}, bf16[256,640]{1,0:T(8,128)(2,1)S(1)}, u32[]{:S(2)}, u32[]{:S(2)}) collective-permute-start(bf16[256,640]{1,0:T(8,128)(2,1)S(1)} %second_away.1), channel_id=1, source_target_pairs={{0,1},{1,0},{2,3},{3,2},{4,5},{5,4},{6,7},{7,6},{8,9},{9,8},{10,11... | collective-permute-start | bytes 983048 | tf_op jit(solution)/shard_map/ppermute | solution.py:40
  82.2 7.7 %collective-permute-start.23 = (f32[16,256]{1,0:T(8,128)S(1)}, f32[16,256]{1,0:T(8,128)S(1)}, u32[]{:S(2)}, u32[]{:S(2)}) collective-permute-start(f32[16,256]{1,0:T(8,128)S(1)} %get-tuple-element.78.refs_0_), channel_id=1, source_target_pairs={{0,1},{1,0},{2,3},{3,2},{4,5},{5,4},{6,7},{7,6},{8,9},{9,8},{10,11... | collective-permute-start | bytes 49160 | tf_op jit(solution)/shard_map/ppermute | solution.py:40
  90.6 2.2 %collective-permute-start.24 = (bf16[512,640]{1,0:T(8,128)(2,1)S(1)}, bf16[512,640]{1,0:T(8,128)(2,1)S(1)}, u32[]{:S(2)}, u32[]{:S(2)}) collective-permute-start(bf16[512,640]{1,0:T(8,128)(2,1)S(1)} %get-tuple-element.80), channel_id=1, source_target_pairs={{0,2},{2,0},{4,6},{6,4},{8,10},{10,8},{12,14},{14,12},{16,18},{18,... | collective-permute-start | bytes 1966088 | tf_op jit(solution)/shard_map/ppermute | solution.py:40
  90.7 7.3 %collective-permute-start.28 = (bf16[256,384]{1,0:T(8,128)(2,1)S(1)}, bf16[256,384]{1,0:T(8,128)(2,1)S(1)}, u32[]{:S(2)}, u32[]{:S(2)}) collective-permute-start(bf16[256,384]{1,0:T(8,128)(2,1)S(1)} %get-tuple-element.88), channel_id=1, source_target_pairs={{0,1},{1,0},{2,3},{3,2},{4,5},{5,4},{6,7},{7,6},{8,9},{9,8},{10,11... | collective-permute-start | bytes 589832 | tf_op jit(solution)/shard_map/ppermute | solution.py:40
  92.9 9.8 %collective-permute-start.25 = (bf16[256,640]{1,0:T(8,128)(2,1)S(1)}, bf16[256,640]{1,0:T(8,128)(2,1)S(1)}, u32[]{:S(2)}, u32[]{:S(2)}) collective-permute-start(bf16[256,640]{1,0:T(8,128)(2,1)S(1)} %get-tuple-element.82), channel_id=1, source_target_pairs={{0,4},{2,6},{4,0},{6,2},{8,12},{10,14},{12,8},{14,10},{16,20},{18,... | collective-permute-start | bytes 983048 | tf_op jit(solution)/shard_map/ppermute | solution.py:40
  101.0 7.0 %collective-permute-start.29 = (bf16[256,384]{1,0:T(8,128)(2,1)S(1)}, bf16[256,384]{1,0:T(8,128)(2,1)S(1)}, u32[]{:S(2)}, u32[]{:S(2)}) collective-permute-start(bf16[256,384]{1,0:T(8,128)(2,1)S(1)} %get-tuple-element.93), channel_id=1, source_target_pairs={{0,4},{2,6},{4,0},{6,2},{8,12},{10,14},{12,8},{14,10},{16,20},{18,... | collective-permute-start | bytes 589832 | tf_op jit(solution)/shard_map/ppermute | solution.py:40
  102.8 27.8 %copy-start.1 = (f32[64,1024]{1,0:T(8,128)S(1)}, f32[64,1024]{1,0:T(8,128)}, u32[]{:S(2)}) copy-start(f32[64,1024]{1,0:T(8,128)} %refs_5_.1) | copy-start | bytes 786436
  102.8 27.8 %copy-start.4 = (f32[64,1024]{1,0:T(8,128)S(1)}, f32[64,1024]{1,0:T(8,128)}, u32[]{:S(2)}) copy-start(f32[64,1024]{1,0:T(8,128)} %refs_6_.1) | copy-start | bytes 786436
  102.8 27.8 %copy-start.5 = (f32[64,1024]{1,0:T(8,128)S(1)}, f32[64,1024]{1,0:T(8,128)}, u32[]{:S(2)}) copy-start(f32[64,1024]{1,0:T(8,128)} %refs_7_.1) | copy-start | bytes 786436
  102.8 27.8 %copy-start.6 = (f32[256,16]{0,1:T(8,128)S(1)}, f32[256,16]{0,1:T(8,128)}, u32[]{:S(2)}) copy-start(f32[256,16]{0,1:T(8,128)} %param.26) | copy-start | bytes 49156
  102.8 27.8 %copy-start.7 = (f32[256,16]{0,1:T(8,128)S(1)}, f32[256,16]{0,1:T(8,128)}, u32[]{:S(2)}) copy-start(f32[256,16]{0,1:T(8,128)} %param.27) | copy-start | bytes 49156
  102.9 5.6 %collective-permute-start.26 = (bf16[128,640]{1,0:T(8,128)(2,1)S(1)}, bf16[128,640]{1,0:T(8,128)(2,1)S(1)}, u32[]{:S(2)}, u32[]{:S(2)}) collective-permute-start(bf16[128,640]{1,0:T(8,128)(2,1)S(1)} %get-tuple-element.84), channel_id=1, source_target_pairs={{0,8},{2,10},{4,12},{6,14},{8,0},{10,2},{12,4},{14,6},{16,24},{18,... | collective-permute-start | bytes 491528 | tf_op jit(solution)/shard_map/ppermute | solution.py:40
  108.0 4.9 %collective-permute-start.30 = (bf16[128,384]{1,0:T(8,128)(2,1)S(1)}, bf16[128,384]{1,0:T(8,128)(2,1)S(1)}, u32[]{:S(2)}, u32[]{:S(2)}) collective-permute-start(bf16[128,384]{1,0:T(8,128)(2,1)S(1)} %get-tuple-element.95), channel_id=1, source_target_pairs={{0,8},{2,10},{4,12},{6,14},{8,0},{10,2},{12,4},{14,6},{16,24},{18,... | collective-permute-start | bytes 294920 | tf_op jit(solution)/shard_map/ppermute | solution.py:40
  108.5 10.0 %collective-permute-start.27 = (bf16[64,640]{1,0:T(8,128)(2,1)S(1)}, bf16[64,640]{1,0:T(8,128)(2,1)S(1)}, u32[]{:S(2)}, u32[]{:S(2)}) collective-permute-start(bf16[64,640]{1,0:T(8,128)(2,1)S(1)} %get-tuple-element.86), channel_id=1, source_target_pairs={{0,16},{2,18},{4,20},{6,22},{8,24},{10,26},{12,28},{14,30},{16,0},... | collective-permute-start | bytes 245768 | tf_op jit(solution)/shard_map/ppermute | solution.py:40
  113.0 5.3 %collective-permute-start.31 = (bf16[64,384]{1,0:T(8,128)(2,1)S(1)}, bf16[64,384]{1,0:T(8,128)(2,1)S(1)}, u32[]{:S(2)}, u32[]{:S(2)}) collective-permute-start(bf16[64,384]{1,0:T(8,128)(2,1)S(1)} %get-tuple-element.97), channel_id=1, source_target_pairs={{0,16},{2,18},{4,20},{6,22},{8,24},{10,26},{12,28},{14,30},{16,0},... | collective-permute-start | bytes 147464 | tf_op jit(solution)/shard_map/ppermute | solution.py:40

commit v5 on v4

--- a/solution.py
+++ b/solution.py
@@ -19,9 +19,6 @@
 LANES = 128
 SCRATCH = 16 << 20
 BIAS_A = 8_000_000_000
-BIAS_C = 1
-T1 = 0
-T2 = 0
 BF = jnp.bfloat16
 F32 = jnp.float32
 BLK = ("hi", "core")
@@ -220,14 +217,15 @@
     right = jnp.concatenate([moments[...], parts], axis=0)
     grad = (slope[...] * dot(left, right, ((0,), (0,)))).astype(BF)
     pre_grad[...] = grad
-    away[...] = dot(grad, freq_rows(freq, 1 - my_half(), 0, away.shape[1]), ((1,), (1,))).astype(BF)
+    width = away.shape[1]
+    start = freq.shape[0] // 2 - width
+    away[...] = dot(grad, freq_rows(freq, 1 - my_half(), start, width), ((1,), (1,))).astype(BF)
 
 
 def second_away(pre_grad, freq, away):
     width = away.shape[1]
-    start = freq.shape[0] // 2 - width
     away[...] = dot(
-        pre_grad[...], freq_rows(freq, 1 - my_half(), start, width), ((1,), (1,))
+        pre_grad[...], freq_rows(freq, 1 - my_half(), 0, width), ((1,), (1,))
     ).astype(BF)
 
 
@@ -341,10 +339,8 @@
         partly = []
         for c in range(CHUNKS):
             held = low[:, pieces[c]]
-            for k, m in enumerate(reversed(masks[1:])):
+            for m in reversed(masks[1:]):
                 held = jnp.concatenate([held, swap(held, BLK, n_blk, m)], axis=0)
-                if c == 0 and k == 0:
-                    held = after(held, masked)
             partly.append(held)
         units = [[((points, w), BF), ((points, w), F32)] for w in widths]
         wide = ((points, n_low), F32)
@@ -394,7 +390,7 @@
         back, pre_grad, first = call(
             "pre_gradient",
             pre_gradient,
-            [parts, ((points, n_low), BF), away[0]],
+            [parts, ((points, n_low), BF), away[1]],
             mine,
             other,
             moments,
@@ -404,8 +400,8 @@
             frequencies,
         )
         gots = [swap(first, "feat", n_feat, 1)]
-        (second,) = call("second_away", second_away, away[1:], pre_grad, frequencies)
-        gots.append(swap(second, "feat", n_feat, 1))
+        (second,) = call("second_away", second_away, away[:1], pre_grad, frequencies)
+        gots.insert(0, swap(second, "feat", n_feat, 1))
         near, pulled = call(
             "own_gradient",
             own_gradient,
@@ -418,14 +414,12 @@
         pulled_far = swap(pulled, "feat", n_feat, 1)
 
         grads, totals = [], []
-        for c in range(CHUNKS):
+        for c in reversed(range(CHUNKS)):
             mid = d_in // 2
             width = widths[c]
             shapes = [((mid, width), BF), ((mid, width), F32)]
             operands = [near, gots[c], damps[c], masked]
-            if T2 and c:
-                operands[2] = after(damps[c], early)
-            if c == CHUNKS - 1:
+            if c == 0:
                 operands += [pulled, pulled_far, resid_grad]
                 shapes = shapes + [thin]
             send, keep, *alpha_grad = call("weight_terms", weight_terms(pieces[c]), shapes, *operands)
@@ -436,17 +430,9 @@
                     got = swap(send, BLK, n_blk, m)
                 mid = mid // 2
                 shapes = [((mid, width), BF), ((mid, width), F32)]
-                ahead = c == 0 and m == masks[1]
-                if T1 and c and m == masks[0]:
-                    keep = after(keep, sent)
-                weight = BIAS_C if ahead else 1
-                send, keep = call("add_halves", add_halves, shapes, keep, got, weight=weight)
-                if ahead:
-                    sent = send
-                if c == 0 and m == masks[0]:
-                    early = send
+                send, keep = call("add_halves", add_halves, shapes, keep, got)
             got = swap(send, BLK, n_blk, masks[-1])
-            last = c == CHUNKS - 1
+            last = c == 0
             outs = [((mid, width), F32), ((size, 1, LANES) if last else (1, LANES), F32)]
             grad, total = call(
                 "finish",
@@ -457,7 +443,7 @@
                 *alpha_grad,
                 *totals,
             )
-            grads.append(grad)
+            grads.insert(0, grad)
             totals = [total]
         (spread,) = totals
         spread = lax.all_to_all(spread, (*BLK, "feat"), 0, 0, tiled=True)

time: 132 us -> 131 us (level)
  local copies, waits for them, and re-layouts: 2.48 us -> 0.08 us
  starting transfers between devices: 37.4 us -> 39.1 us
    unnamed x28, local copies, waits for them, and re-layouts: 2.46 us -> 0.06 us
    ppermute x32, starting transfers between devices: 37.4 us -> 39.1 us  [swap(): return lax.ppermute(x, axis, [(i, i ^ mask) for i in range(size)])]
  transfers between devices with their start and end apart: 32 -> 32, of which waited for: 28 -> 26; matrix products, arithmetic and copies ran while one was open for 0% -> 0% of each run, Pallas kernels for 4% -> 4%
where the time goes in v5:
time: 131 us
  waiting for transfers between devices  61.5 us (47%)
  starting transfers between devices  39.1 us (30%)
  blocking collectives  16.7 us (13%)
  Pallas kernels  11.1 us (8%)
    ppermute x32, waiting for transfers between devices, swap(): return lax.ppermute(x, axis, [(i, i ^ mask) for i in range(size)])  61.5 us
    ppermute x32, starting transfers between devices, swap(): return lax.ppermute(x, axis, [(i, i ^ mask) for i in range(size)])  39.1 us
    all_to_all x1, blocking collectives, on_device(): spread = lax.all_to_all(spread, (*BLK, 'feat'), 0, 0, tiled=True)  11.8 us
    pallas_call x22, Pallas kernels, call(): pl.pallas_call(body, out_shape=[shapes(shape, dtype) for shape, dtype in...  11.1 us
  transfers between devices with their start and end apart: 32, of which 26 were waited for; matrix products, arithmetic and copies ran while one was open for 0% of the time, Pallas kernels for 4%

profile of v5, /device:TPU:0, one launch (start us, length us, event | category | flops | bytes accessed | tf_op | source)
XLA Modules:
  0.0 130.7 jit_solution(13020937489524278010)
XLA Ops:
  0.7 1.0 convert_element_type.3
  1.7 4.1 %collective-permute-start = (bf16[64,384]{1,0:T(8,128)(2,1)S(1)}, bf16[64,384]{1,0:T(8,128)(2,1)S(1)}, u32[]{:S(2)}, u32[]{:S(2)}) collective-permute-start(bf16[64,384]{1,0:T(8,128)(2,1)S(1)} %slice.8), channel_id=1, source_target_pairs={{0,16},{2,18},{4,20},{6,22},{8,24},{10,26},{12,28},{14,30},{16,0},... | collective-permute-start | bytes 147464 | tf_op jit(solution)/shard_map/ppermute | solution.py:37
  5.9 2.5 %collective-permute-done = bf16[64,384]{1,0:T(8,128)(2,1)S(1)} collective-permute-done((bf16[64,384]{1,0:T(8,128)(2,1)S(1)}, bf16[64,384]{1,0:T(8,128)(2,1)S(1)}, u32[]{:S(2)}, u32[]{:S(2)}) %collective-permute-start) | collective-permute-done | bytes 49184 | tf_op jit(solution)/shard_map/ppermute | solution.py:37
  8.5 2.8 %collective-permute-start.1 = (bf16[128,384]{1,0:T(8,128)(2,1)S(1)}, bf16[128,384]{1,0:T(8,128)(2,1)S(1)}, u32[]{:S(2)}, u32[]{:S(2)}) collective-permute-start(bf16[128,384]{1,0:T(8,128)(2,1)S(1)} %pad_maximum_fusion.5), channel_id=1, source_target_pairs={{0,8},{2,10},{4,12},{6,14},{8,0},{10,2},{12,4},{14,6},{16,24},{18,... | collective-permute-start | bytes 294920 | tf_op jit(solution)/shard_map/ppermute | solution.py:37
  11.3 1.6 %collective-permute-done.4 = bf16[64,640]{1,0:T(8,128)(2,1)S(1)} collective-permute-done((bf16[64,640]{1,0:T(8,128)(2,1)S(1)}, bf16[64,640]{1,0:T(8,128)(2,1)S(1)}, u32[]{:S(2)}, u32[]{:S(2)}) %collective-permute-start.4) | collective-permute-done | bytes 81952 | tf_op jit(solution)/shard_map/ppermute | solution.py:37
  13.0 2.0 %collective-permute-done.1 = bf16[128,384]{1,0:T(8,128)(2,1)S(1)} collective-permute-done((bf16[128,384]{1,0:T(8,128)(2,1)S(1)}, bf16[128,384]{1,0:T(8,128)(2,1)S(1)}, u32[]{:S(2)}, u32[]{:S(2)}) %collective-permute-start.1) | collective-permute-done | bytes 98336 | tf_op jit(solution)/shard_map/ppermute | solution.py:37
  15.0 1.6 %collective-permute-start.2 = (bf16[256,384]{1,0:T(8,128)(2,1)S(1)}, bf16[256,384]{1,0:T(8,128)(2,1)S(1)}, u32[]{:S(2)}, u32[]{:S(2)}) collective-permute-start(bf16[256,384]{1,0:T(8,128)(2,1)S(1)} %pad_maximum_fusion.3), channel_id=1, source_target_pairs={{0,4},{2,6},{4,0},{6,2},{8,12},{10,14},{12,8},{14,10},{16,20},{18,... | collective-permute-start | bytes 589832 | tf_op jit(solution)/shard_map/ppermute | solution.py:37
  16.6 1.0 prepare.1.masked
  18.3 1.6 %collective-permute-start.6 = (bf16[256,640]{1,0:T(8,128)(2,1)S(1)}, bf16[256,640]{1,0:T(8,128)(2,1)S(1)}, u32[]{:S(2)}, u32[]{:S(2)}) collective-permute-start(bf16[256,640]{1,0:T(8,128)(2,1)S(1)} %pad_maximum_fusion.2), channel_id=1, source_target_pairs={{0,4},{2,6},{4,0},{6,2},{8,12},{10,14},{12,8},{14,10},{16,20},{18,... | collective-permute-start | bytes 983048 | tf_op jit(solution)/shard_map/ppermute | solution.py:37
  19.9 3.0 %collective-permute-done.2 = bf16[256,384]{1,0:T(8,128)(2,1)S(1)} collective-permute-done((bf16[256,384]{1,0:T(8,128)(2,1)S(1)}, bf16[256,384]{1,0:T(8,128)(2,1)S(1)}, u32[]{:S(2)}, u32[]{:S(2)}) %collective-permute-start.2) | collective-permute-done | bytes 196640 | tf_op jit(solution)/shard_map/ppermute | solution.py:37
  22.9 2.5 %all_gather.6.refs_0_ = bf16[1024,384]{1,0:T(8,128)(2,1)S(1)} all-gather(bf16[512,384]{1,0:T(8,128)(2,1)S(1)} %pad_maximum_fusion.1), channel_id=1, replica_groups=mesh['hi'=8,'core'=2,'feat'=2] {'core'}, dimensions={0}, use_global_device_ids=true | all-gather | bytes 1179648 | tf_op jit(solution)/shard_map/all_gather | solution.py:347
  25.8 1.6 %collective-permute-start.3 = (bf16[256,384]{1,0:T(8,128)(2,1)S(1)}, bf16[256,384]{1,0:T(8,128)(2,1)S(1)}, u32[]{:S(2)}, u32[]{:S(2)}) collective-permute-start(bf16[256,384]{1,0:T(8,128)(2,1)S(1)} %get-tuple-element.60.hidden), channel_id=1, source_target_pairs={{0,1},{1,0},{2,3},{3,2},{4,5},{5,4},{6,7},{7,6},{8,9},{9,8},{10,11... | collective-permute-start | bytes 589832 | tf_op jit(solution)/shard_map/ppermute | solution.py:37
  27.4 1.0 collective-permute-done.6
  28.5 4.3 %collective-permute-done.3.far = bf16[256,384]{1,0:T(8,128)(2,1)S(1)} collective-permute-done((bf16[256,384]{1,0:T(8,128)(2,1)S(1)}, bf16[256,384]{1,0:T(8,128)(2,1)S(1)}, u32[]{:S(2)}, u32[]{:S(2)}) %collective-permute-start.3) | collective-permute-done | bytes 196640 | tf_op jit(solution)/shard_map/ppermute | solution.py:37
  34.2 1.6 %collective-permute-start.8 = (bf16[256,640]{1,0:T(8,128)(2,1)S(1)}, bf16[256,640]{1,0:T(8,128)(2,1)S(1)}, u32[]{:S(2)}, u32[]{:S(2)}) collective-permute-start(bf16[256,640]{1,0:T(8,128)(2,1)S(1)} %get-tuple-element.62.hidden), channel_id=1, source_target_pairs={{0,1},{1,0},{2,3},{3,2},{4,5},{5,4},{6,7},{7,6},{8,9},{9,8},{10,11... | collective-permute-start | bytes 983048 | tf_op jit(solution)/shard_map/ppermute | solution.py:37
  36.4 6.8 %collective-permute-done.8.far = bf16[256,640]{1,0:T(8,128)(2,1)S(1)} collective-permute-done((bf16[256,640]{1,0:T(8,128)(2,1)S(1)}, bf16[256,640]{1,0:T(8,128)(2,1)S(1)}, u32[]{:S(2)}, u32[]{:S(2)}) %collective-permute-start.8) | collective-permute-done | bytes 327712 | tf_op jit(solution)/shard_map/ppermute | solution.py:37
  43.2 2.1 %features.1 = (bf16[256,1024]{1,0:T(8,128)(2,1)S(1)}, f32[256,1024]{1,0:T(8,128)S(1)}, f32[8,1152]{1,0:T(8,128)S(1)}, f32[8,1152]{1,0:T(8,128)S(1)}) custom-call(f32[256,1024]{1,0:T(8,128)S(1)} %second_pre.1.pre, bf16[256,640]{1,0:T(8,128)(2,1)S(1)} %collective-permute-done.8.far, bf16[2048,1024]{1,0:T(8,128)(2,1)S(1)} %copy-done, f32[16,256]{1,0:T(8,128)S(1)} %bitcast.14, ...), custom_call_target="tpu_custom_call" | custom-call | flops 1 | bytes 1 | tf_op jit(solution)/shard_map/features/pallas_call | solution.py:82
  45.3 1.2 collective-permute-done.9
  47.1 1.1 collective-permute-start.10
  48.1 1.9 %collective-permute-start.11 = (f32[8,1152]{1,0:T(8,128)S(1)}, f32[8,1152]{1,0:T(8,128)S(1)}, u32[]{:S(2)}, u32[]{:S(2)}) collective-permute-start(f32[8,1152]{1,0:T(8,128)S(1)} %add.30), channel_id=1, source_target_pairs={{0,8},{2,10},{4,12},{6,14},{8,0},{10,2},{12,4},{14,6},{16,24},{18,... | collective-permute-start | bytes 110600 | tf_op jit(solution)/shard_map/ppermute | solution.py:37
  50.0 1.4 %collective-permute-done.12 = f32[8,1152]{1,0:T(8,128)S(1)} collective-permute-done((f32[8,1152]{1,0:T(8,128)S(1)}, f32[8,1152]{1,0:T(8,128)S(1)}, u32[]{:S(2)}, u32[]{:S(2)}) %collective-permute-start.12) | collective-permute-done | bytes 36896 | tf_op jit(solution)/shard_map/ppermute | solution.py:37
  52.1 2.9 %collective-permute-start.13 = (f32[8,1152]{1,0:T(8,128)S(1)}, f32[8,1152]{1,0:T(8,128)S(1)}, u32[]{:S(2)}, u32[]{:S(2)}) collective-permute-start(f32[8,1152]{1,0:T(8,128)S(1)} %add_add_fusion.1), channel_id=1, source_target_pairs={{0,16},{2,18},{4,20},{6,22},{8,24},{10,26},{12,28},{14,30},{16,0},... | collective-permute-start | bytes 110600 | tf_op jit(solution)/shard_map/ppermute | solution.py:37
  55.0 2.0 %collective-permute-done.13 = f32[8,1152]{1,0:T(8,128)S(1)} collective-permute-done((f32[8,1152]{1,0:T(8,128)S(1)}, f32[8,1152]{1,0:T(8,128)S(1)}, u32[]{:S(2)}, u32[]{:S(2)}) %collective-permute-start.13) | collective-permute-done | bytes 36896 | tf_op jit(solution)/shard_map/ppermute | solution.py:37
  57.0 1.2 collective-permute-done.14.other
  58.5 1.6 %collective-permute-start.15 = (f32[16,256]{1,0:T(8,128)S(1)}, f32[16,256]{1,0:T(8,128)S(1)}, u32[]{:S(2)}, u32[]{:S(2)}) collective-permute-start(f32[16,256]{1,0:T(8,128)S(1)} %get-tuple-element.66.near), channel_id=1, source_target_pairs={{0,1},{1,0},{2,3},{3,2},{4,5},{5,4},{6,7},{7,6},{8,9},{9,8},{10,11... | collective-permute-start | bytes 49160 | tf_op jit(solution)/shard_map/ppermute | solution.py:37
  60.0 2.2 %collective-permute-done.15.far = f32[16,256]{1,0:T(8,128)S(1)} collective-permute-done((f32[16,256]{1,0:T(8,128)S(1)}, f32[16,256]{1,0:T(8,128)S(1)}, u32[]{:S(2)}, u32[]{:S(2)}) %collective-permute-start.15) | collective-permute-done | bytes 16416 | tf_op jit(solution)/shard_map/ppermute | solution.py:37
  62.5 1.2 collective-permute-done.16
  63.7 2.9 %collective-permute-start.19 = (f32[8,1152]{1,0:T(8,128)S(1)}, f32[8,1152]{1,0:T(8,128)S(1)}, u32[]{:S(2)}, u32[]{:S(2)}) collective-permute-start(f32[8,1152]{1,0:T(8,128)S(1)} %add.35), channel_id=1, source_target_pairs={{0,12},{2,14},{4,8},{6,10},{8,4},{10,6},{12,0},{14,2},{16,28},{18,... | collective-permute-start | bytes 110600 | tf_op jit(solution)/shard_map/ppermute | solution.py:37
  67.2 1.4 %collective-permute-done.19 = f32[8,1152]{1,0:T(8,128)S(1)} collective-permute-done((f32[8,1152]{1,0:T(8,128)S(1)}, f32[8,1152]{1,0:T(8,128)S(1)}, u32[]{:S(2)}, u32[]{:S(2)}) %collective-permute-start.19) | collective-permute-done | bytes 36896 | tf_op jit(solution)/shard_map/ppermute | solution.py:37
  68.6 2.0 %collective-permute-done.17 = f32[8,1152]{1,0:T(8,128)S(1)} collective-permute-done((f32[8,1152]{1,0:T(8,128)S(1)}, f32[8,1152]{1,0:T(8,128)S(1)}, u32[]{:S(2)}, u32[]{:S(2)}) %collective-permute-start.17) | collective-permute-done | bytes 36896 | tf_op jit(solution)/shard_map/ppermute | solution.py:37
  71.1 1.7 %collective-permute-start.20 = (f32[8,1152]{1,0:T(8,128)S(1)}, f32[8,1152]{1,0:T(8,128)S(1)}, u32[]{:S(2)}, u32[]{:S(2)}) collective-permute-start(f32[8,1152]{1,0:T(8,128)S(1)} %add_add_fusion), channel_id=1, source_target_pairs={{0,16},{2,18},{4,20},{6,22},{8,24},{10,26},{12,28},{14,30},{16,0},... | collective-permute-start | bytes 110600 | tf_op jit(solution)/shard_map/ppermute | solution.py:37
  72.8 3.2 %collective-permute-done.20 = f32[8,1152]{1,0:T(8,128)S(1)} collective-permute-done((f32[8,1152]{1,0:T(8,128)S(1)}, f32[8,1152]{1,0:T(8,128)S(1)}, u32[]{:S(2)}, u32[]{:S(2)}) %collective-permute-start.20) | collective-permute-done | bytes 36896 | tf_op jit(solution)/shard_map/ppermute | solution.py:37
  76.0 1.2 collective-permute-done.21.other
  78.1 1.6 %collective-permute-start.27 = (bf16[256,640]{1,0:T(8,128)(2,1)S(1)}, bf16[256,640]{1,0:T(8,128)(2,1)S(1)}, u32[]{:S(2)}, u32[]{:S(2)}) collective-permute-start(bf16[256,640]{1,0:T(8,128)(2,1)S(1)} %get-tuple-element.86), channel_id=1, source_target_pairs={{0,1},{1,0},{2,3},{3,2},{4,5},{5,4},{6,7},{7,6},{8,9},{9,8},{10,11... | collective-permute-start | bytes 983048 | tf_op jit(solution)/shard_map/ppermute | solution.py:37
  80.5 7.4 %collective-permute-done.27.got = bf16[256,640]{1,0:T(8,128)(2,1)S(1)} collective-permute-done((bf16[256,640]{1,0:T(8,128)(2,1)S(1)}, bf16[256,640]{1,0:T(8,128)(2,1)S(1)}, u32[]{:S(2)}, u32[]{:S(2)}) %collective-permute-start.27) | collective-permute-done | bytes 327712 | tf_op jit(solution)/shard_map/ppermute | solution.py:37
  89.1 1.6 %collective-permute-start.22 = (bf16[256,384]{1,0:T(8,128)(2,1)S(1)}, bf16[256,384]{1,0:T(8,128)(2,1)S(1)}, u32[]{:S(2)}, u32[]{:S(2)}) collective-permute-start(bf16[256,384]{1,0:T(8,128)(2,1)S(1)} %second_away.1), channel_id=1, source_target_pairs={{0,1},{1,0},{2,3},{3,2},{4,5},{5,4},{6,7},{7,6},{8,9},{9,8},{10,11... | collective-permute-start | bytes 589832 | tf_op jit(solution)/shard_map/ppermute | solution.py:37
  90.8 1.6 %collective-permute-start.29 = (bf16[256,640]{1,0:T(8,128)(2,1)S(1)}, bf16[256,640]{1,0:T(8,128)(2,1)S(1)}, u32[]{:S(2)}, u32[]{:S(2)}) collective-permute-start(bf16[256,640]{1,0:T(8,128)(2,1)S(1)} %get-tuple-element.91), channel_id=1, source_target_pairs={{0,4},{2,6},{4,0},{6,2},{8,12},{10,14},{12,8},{14,10},{16,20},{18,... | collective-permute-start | bytes 983048 | tf_op jit(solution)/shard_map/ppermute | solution.py:37
  92.4 1.5 %collective-permute-start.23 = (f32[16,256]{1,0:T(8,128)S(1)}, f32[16,256]{1,0:T(8,128)S(1)}, u32[]{:S(2)}, u32[]{:S(2)}) collective-permute-start(f32[16,256]{1,0:T(8,128)S(1)} %get-tuple-element.76.refs_0_), channel_id=1, source_target_pairs={{0,1},{1,0},{2,3},{3,2},{4,5},{5,4},{6,7},{7,6},{8,9},{9,8},{10,11... | collective-permute-start | bytes 49160 | tf_op jit(solution)/shard_map/ppermute | solution.py:37
  93.9 2.9 %collective-permute-done.23.refs_1_ = f32[16,256]{1,0:T(8,128)S(1)} collective-permute-done((f32[16,256]{1,0:T(8,128)S(1)}, f32[16,256]{1,0:T(8,128)S(1)}, u32[]{:S(2)}, u32[]{:S(2)}) %collective-permute-start.23) | collective-permute-done | bytes 16416 | tf_op jit(solution)/shard_map/ppermute | solution.py:37
  97.3 2.4 %all_gather.7.got = bf16[1024,384]{1,0:T(8,128)(2,1)S(1)} all-gather(bf16[512,384]{1,0:T(8,128)(2,1)S(1)} %get-tuple-element.78), channel_id=1, replica_groups=mesh['hi'=8,'core'=2,'feat'=2] {'core'}, dimensions={0}, use_global_device_ids=true | all-gather | bytes 1179648 | tf_op jit(solution)/shard_map/all_gather | solution.py:428
  99.8 1.6 %collective-permute-start.24 = (bf16[256,384]{1,0:T(8,128)(2,1)S(1)}, bf16[256,384]{1,0:T(8,128)(2,1)S(1)}, u32[]{:S(2)}, u32[]{:S(2)}) collective-permute-start(bf16[256,384]{1,0:T(8,128)(2,1)S(1)} %get-tuple-element.80), channel_id=1, source_target_pairs={{0,4},{2,6},{4,0},{6,2},{8,12},{10,14},{12,8},{14,10},{16,20},{18,... | collective-permute-start | bytes 589832 | tf_op jit(solution)/shard_map/ppermute | solution.py:37
  101.6 5.2 %collective-permute-done.24.got = bf16[256,384]{1,0:T(8,128)(2,1)S(1)} collective-permute-done((bf16[256,384]{1,0:T(8,128)(2,1)S(1)}, bf16[256,384]{1,0:T(8,128)(2,1)S(1)}, u32[]{:S(2)}, u32[]{:S(2)}) %collective-permute-start.24) | collective-permute-done | bytes 196640 | tf_op jit(solution)/shard_map/ppermute | solution.py:37
  107.5 2.8 %collective-permute-start.31 = (bf16[64,640]{1,0:T(8,128)(2,1)S(1)}, bf16[64,640]{1,0:T(8,128)(2,1)S(1)}, u32[]{:S(2)}, u32[]{:S(2)}) collective-permute-start(bf16[64,640]{1,0:T(8,128)(2,1)S(1)} %get-tuple-element.95), channel_id=1, source_target_pairs={{0,16},{2,18},{4,20},{6,22},{8,24},{10,26},{12,28},{14,30},{16,0},... | collective-permute-start | bytes 245768 | tf_op jit(solution)/shard_map/ppermute | solution.py:37
  110.4 1.8 %collective-permute-done.25.got = bf16[128,384]{1,0:T(8,128)(2,1)S(1)} collective-permute-done((bf16[128,384]{1,0:T(8,128)(2,1)S(1)}, bf16[128,384]{1,0:T(8,128)(2,1)S(1)}, u32[]{:S(2)}, u32[]{:S(2)}) %collective-permute-start.25) | collective-permute-done | bytes 98336 | tf_op jit(solution)/shard_map/ppermute | solution.py:37
  112.2 1.4 %collective-permute-start.26 = (bf16[64,384]{1,0:T(8,128)(2,1)S(1)}, bf16[64,384]{1,0:T(8,128)(2,1)S(1)}, u32[]{:S(2)}, u32[]{:S(2)}) collective-permute-start(bf16[64,384]{1,0:T(8,128)(2,1)S(1)} %get-tuple-element.84), channel_id=1, source_target_pairs={{0,16},{2,18},{4,20},{6,22},{8,24},{10,26},{12,28},{14,30},{16,0},... | collective-permute-start | bytes 147464 | tf_op jit(solution)/shard_map/ppermute | solution.py:37
  113.8 3.7 %collective-permute-done.26.got = bf16[64,384]{1,0:T(8,128)(2,1)S(1)} collective-permute-done((bf16[64,384]{1,0:T(8,128)(2,1)S(1)}, bf16[64,384]{1,0:T(8,128)(2,1)S(1)}, u32[]{:S(2)}, u32[]{:S(2)}) %collective-permute-start.26) | collective-permute-done | bytes 49184 | tf_op jit(solution)/shard_map/ppermute | solution.py:37
  117.7 11.8 %all_to_all.5.refs_0_ = f32[32,1,128]{2,1,0:T(1,128)S(1)} all-to-all(f32[32,1,128]{2,1,0:T(1,128)S(1)} %get-tuple-element.97), channel_id=1, replica_groups=mesh['hi'=8,'core'=2,'feat'=2] {'hi','core','feat'}, dimensions={0} | all-to-all | bytes 32768 | tf_op jit(solution)/shard_map/all_to_all | solution.py:449
  129.5 1.2 update.1
  (84 shorter events, 11.3 us)
Async XLA Ops:
  0.6 15.9 %copy-start.2 = (bf16[256,1024]{1,0:T(8,128)(2,1)S(1)}, bf16[256,1024]{1,0:T(8,128)(2,1)}, u32[]{:S(2)}) copy-start(bf16[256,1024]{1,0:T(8,128)(2,1)} %inputs.1) | copy-start | bytes 1572868
  0.7 15.9 %copy-start.11 = (s32[256]{0:T(256)S(1)}, s32[256]{0:T(256)}, u32[]{:S(2)}) copy-start(s32[256]{0:T(256)} %param.17) | copy-start | bytes 3076
  0.7 15.9 %copy-start.9 = (s32[2,1024]{1,0:T(2,128)S(1)}, s32[2,1024]{1,0:T(2,128)}, u32[]{:S(2)}) copy-start(s32[2,1024]{1,0:T(2,128)} %col_mask.1) | copy-start | bytes 24580
  1.7 6.7 %collective-permute-start = (bf16[64,384]{1,0:T(8,128)(2,1)S(1)}, bf16[64,384]{1,0:T(8,128)(2,1)S(1)}, u32[]{:S(2)}, u32[]{:S(2)}) collective-permute-start(bf16[64,384]{1,0:T(8,128)(2,1)S(1)} %slice.8), channel_id=1, source_target_pairs={{0,16},{2,18},{4,20},{6,22},{8,24},{10,26},{12,28},{14,30},{16,0},... | collective-permute-start | bytes 147464 | tf_op jit(solution)/shard_map/ppermute | solution.py:37
  5.9 7.0 %collective-permute-start.4 = (bf16[64,640]{1,0:T(8,128)(2,1)S(1)}, bf16[64,640]{1,0:T(8,128)(2,1)S(1)}, u32[]{:S(2)}, u32[]{:S(2)}) collective-permute-start(bf16[64,640]{1,0:T(8,128)(2,1)S(1)} %slice.9), channel_id=1, source_target_pairs={{0,16},{2,18},{4,20},{6,22},{8,24},{10,26},{12,28},{14,30},{16,0},... | collective-permute-start | bytes 245768 | tf_op jit(solution)/shard_map/ppermute | solution.py:37
  8.5 6.5 %collective-permute-start.1 = (bf16[128,384]{1,0:T(8,128)(2,1)S(1)}, bf16[128,384]{1,0:T(8,128)(2,1)S(1)}, u32[]{:S(2)}, u32[]{:S(2)}) collective-permute-start(bf16[128,384]{1,0:T(8,128)(2,1)S(1)} %pad_maximum_fusion.5), channel_id=1, source_target_pairs={{0,8},{2,10},{4,12},{6,14},{8,0},{10,2},{12,4},{14,6},{16,24},{18,... | collective-permute-start | bytes 294920 | tf_op jit(solution)/shard_map/ppermute | solution.py:37
  12.9 5.4 %collective-permute-start.5 = (bf16[128,640]{1,0:T(8,128)(2,1)S(1)}, bf16[128,640]{1,0:T(8,128)(2,1)S(1)}, u32[]{:S(2)}, u32[]{:S(2)}) collective-permute-start(bf16[128,640]{1,0:T(8,128)(2,1)S(1)} %pad_maximum_fusion.4), channel_id=1, source_target_pairs={{0,8},{2,10},{4,12},{6,14},{8,0},{10,2},{12,4},{14,6},{16,24},{18,... | collective-permute-start | bytes 491528 | tf_op jit(solution)/shard_map/ppermute | solution.py:37
  15.0 7.8 %collective-permute-start.2 = (bf16[256,384]{1,0:T(8,128)(2,1)S(1)}, bf16[256,384]{1,0:T(8,128)(2,1)S(1)}, u32[]{:S(2)}, u32[]{:S(2)}) collective-permute-start(bf16[256,384]{1,0:T(8,128)(2,1)S(1)} %pad_maximum_fusion.3), channel_id=1, source_target_pairs={{0,4},{2,6},{4,0},{6,2},{8,12},{10,14},{12,8},{14,10},{16,20},{18,... | collective-permute-start | bytes 589832 | tf_op jit(solution)/shard_map/ppermute | solution.py:37
  18.3 10.1 %collective-permute-start.6 = (bf16[256,640]{1,0:T(8,128)(2,1)S(1)}, bf16[256,640]{1,0:T(8,128)(2,1)S(1)}, u32[]{:S(2)}, u32[]{:S(2)}) collective-permute-start(bf16[256,640]{1,0:T(8,128)(2,1)S(1)} %pad_maximum_fusion.2), channel_id=1, source_target_pairs={{0,4},{2,6},{4,0},{6,2},{8,12},{10,14},{12,8},{14,10},{16,20},{18,... | collective-permute-start | bytes 983048 | tf_op jit(solution)/shard_map/ppermute | solution.py:37
  22.8 10.0 %copy-start = (bf16[2048,1024]{1,0:T(8,128)(2,1)S(1)}, bf16[2048,1024]{1,0:T(8,128)(2,1)}, u32[]{:S(2)}) copy-start(bf16[2048,1024]{1,0:T(8,128)(2,1)} %freq.11) | copy-start | bytes 12582916
  25.4 7.5 %copy-start.13 = (f32[1024]{0:T(1024)S(1)}, f32[1024]{0:T(1024)}, u32[]{:S(2)}) copy-start(f32[1024]{0:T(1024)} %param.19) | copy-start | bytes 12292
  25.8 7.0 %collective-permute-start.3 = (bf16[256,384]{1,0:T(8,128)(2,1)S(1)}, bf16[256,384]{1,0:T(8,128)(2,1)S(1)}, u32[]{:S(2)}, u32[]{:S(2)}) collective-permute-start(bf16[256,384]{1,0:T(8,128)(2,1)S(1)} %get-tuple-element.60.hidden), channel_id=1, source_target_pairs={{0,1},{1,0},{2,3},{3,2},{4,5},{5,4},{6,7},{7,6},{8,9},{9,8},{10,11... | collective-permute-start | bytes 589832 | tf_op jit(solution)/shard_map/ppermute | solution.py:37
  28.4 5.1 %collective-permute-start.7 = (bf16[512,640]{1,0:T(8,128)(2,1)S(1)}, bf16[512,640]{1,0:T(8,128)(2,1)S(1)}, u32[]{:S(2)}, u32[]{:S(2)}) collective-permute-start(bf16[512,640]{1,0:T(8,128)(2,1)S(1)} %pad_maximum_fusion.refs_0_), channel_id=1, source_target_pairs={{0,2},{2,0},{4,6},{6,4},{8,10},{10,8},{12,14},{14,12},{16,18},{18,... | collective-permute-start | bytes 1966088 | tf_op jit(solution)/shard_map/ppermute | solution.py:37
  34.2 9.0 %copy-start.3 = (f32[256,16]{0,1:T(8,128)S(1)}, f32[256,16]{0,1:T(8,128)}, u32[]{:S(2)}) copy-start(f32[256,16]{0,1:T(8,128)} %param.25) | copy-start | bytes 49156
  34.2 9.0 %copy-start.10 = (s32[256]{0:T(256)S(1)}, s32[256]{0:T(256)}, u32[]{:S(2)}) copy-start(s32[256]{0:T(256)} %param.16) | copy-start | bytes 3076
  34.2 9.0 %collective-permute-start.8 = (bf16[256,640]{1,0:T(8,128)(2,1)S(1)}, bf16[256,640]{1,0:T(8,128)(2,1)S(1)}, u32[]{:S(2)}, u32[]{:S(2)}) collective-permute-start(bf16[256,640]{1,0:T(8,128)(2,1)S(1)} %get-tuple-element.62.hidden), channel_id=1, source_target_pairs={{0,1},{1,0},{2,3},{3,2},{4,5},{5,4},{6,7},{7,6},{8,9},{9,8},{10,11... | collective-permute-start | bytes 983048 | tf_op jit(solution)/shard_map/ppermute | solution.py:37
  43.2 19.1 %copy-start.8 = (f32[256,16]{0,1:T(8,128)S(1)}, f32[256,16]{0,1:T(8,128)}, u32[]{:S(2)}) copy-start(f32[256,16]{0,1:T(8,128)} %param.21) | copy-start | bytes 49156
  43.2 19.1 %copy-start.12 = (f32[256]{0:T(256)S(1)}, f32[256]{0:T(256)}, u32[]{:S(2)}) copy-start(f32[256]{0:T(256)} %param.20) | copy-start | bytes 3076
  45.3 1.3 collective-permute-start.9
  46.5 4.9 %collective-permute-start.12 = (f32[8,1152]{1,0:T(8,128)S(1)}, f32[8,1152]{1,0:T(8,128)S(1)}, u32[]{:S(2)}, u32[]{:S(2)}) collective-permute-start(f32[8,1152]{1,0:T(8,128)S(1)} %add.30), channel_id=1, source_target_pairs={{0,12},{2,14},{4,8},{6,10},{8,4},{10,6},{12,0},{14,2},{16,28},{18,... | collective-permute-start | bytes 110600 | tf_op jit(solution)/shard_map/ppermute | solution.py:37
  47.1 4.4 %collective-permute-start.10 = (f32[8,1152]{1,0:T(8,128)S(1)}, f32[8,1152]{1,0:T(8,128)S(1)}, u32[]{:S(2)}, u32[]{:S(2)}) collective-permute-start(f32[8,1152]{1,0:T(8,128)S(1)} %add.30), channel_id=1, source_target_pairs={{0,4},{2,6},{4,0},{6,2},{8,12},{10,14},{12,8},{14,10},{16,20},{18,... | collective-permute-start | bytes 110600 | tf_op jit(solution)/shard_map/ppermute | solution.py:37
  48.1 4.0 %collective-permute-start.11 = (f32[8,1152]{1,0:T(8,128)S(1)}, f32[8,1152]{1,0:T(8,128)S(1)}, u32[]{:S(2)}, u32[]{:S(2)}) collective-permute-start(f32[8,1152]{1,0:T(8,128)S(1)} %add.30), channel_id=1, source_target_pairs={{0,8},{2,10},{4,12},{6,14},{8,0},{10,2},{12,4},{14,6},{16,24},{18,... | collective-permute-start | bytes 110600 | tf_op jit(solution)/shard_map/ppermute | solution.py:37
  52.1 4.9 %collective-permute-start.13 = (f32[8,1152]{1,0:T(8,128)S(1)}, f32[8,1152]{1,0:T(8,128)S(1)}, u32[]{:S(2)}, u32[]{:S(2)}) collective-permute-start(f32[8,1152]{1,0:T(8,128)S(1)} %add_add_fusion.1), channel_id=1, source_target_pairs={{0,16},{2,18},{4,20},{6,22},{8,24},{10,26},{12,28},{14,30},{16,0},... | collective-permute-start | bytes 110600 | tf_op jit(solution)/shard_map/ppermute | solution.py:37
  57.0 1.2 collective-permute-start.14
  58.5 3.8 %collective-permute-start.15 = (f32[16,256]{1,0:T(8,128)S(1)}, f32[16,256]{1,0:T(8,128)S(1)}, u32[]{:S(2)}, u32[]{:S(2)}) collective-permute-start(f32[16,256]{1,0:T(8,128)S(1)} %get-tuple-element.66.near), channel_id=1, source_target_pairs={{0,1},{1,0},{2,3},{3,2},{4,5},{5,4},{6,7},{7,6},{8,9},{9,8},{10,11... | collective-permute-start | bytes 49160 | tf_op jit(solution)/shard_map/ppermute | solution.py:37
  62.5 1.2 collective-permute-start.16
  63.7 4.9 %collective-permute-start.19 = (f32[8,1152]{1,0:T(8,128)S(1)}, f32[8,1152]{1,0:T(8,128)S(1)}, u32[]{:S(2)}, u32[]{:S(2)}) collective-permute-start(f32[8,1152]{1,0:T(8,128)S(1)} %add.35), channel_id=1, source_target_pairs={{0,12},{2,14},{4,8},{6,10},{8,4},{10,6},{12,0},{14,2},{16,28},{18,... | collective-permute-start | bytes 110600 | tf_op jit(solution)/shard_map/ppermute | solution.py:37
  66.6 4.0 %collective-permute-start.17 = (f32[8,1152]{1,0:T(8,128)S(1)}, f32[8,1152]{1,0:T(8,128)S(1)}, u32[]{:S(2)}, u32[]{:S(2)}) collective-permute-start(f32[8,1152]{1,0:T(8,128)S(1)} %add.35), channel_id=1, source_target_pairs={{0,4},{2,6},{4,0},{6,2},{8,12},{10,14},{12,8},{14,10},{16,20},{18,... | collective-permute-start | bytes 110600 | tf_op jit(solution)/shard_map/ppermute | solution.py:37
  67.1 4.0 %collective-permute-start.18 = (f32[8,1152]{1,0:T(8,128)S(1)}, f32[8,1152]{1,0:T(8,128)S(1)}, u32[]{:S(2)}, u32[]{:S(2)}) collective-permute-start(f32[8,1152]{1,0:T(8,128)S(1)} %add.35), channel_id=1, source_target_pairs={{0,8},{2,10},{4,12},{6,14},{8,0},{10,2},{12,4},{14,6},{16,24},{18,... | collective-permute-start | bytes 110600 | tf_op jit(solution)/shard_map/ppermute | solution.py:37
  71.1 4.9 %collective-permute-start.20 = (f32[8,1152]{1,0:T(8,128)S(1)}, f32[8,1152]{1,0:T(8,128)S(1)}, u32[]{:S(2)}, u32[]{:S(2)}) collective-permute-start(f32[8,1152]{1,0:T(8,128)S(1)} %add_add_fusion), channel_id=1, source_target_pairs={{0,16},{2,18},{4,20},{6,22},{8,24},{10,26},{12,28},{14,30},{16,0},... | collective-permute-start | bytes 110600 | tf_op jit(solution)/shard_map/ppermute | solution.py:37
  76.0 1.2 collective-permute-start.21
  78.1 9.8 %collective-permute-start.27 = (bf16[256,640]{1,0:T(8,128)(2,1)S(1)}, bf16[256,640]{1,0:T(8,128)(2,1)S(1)}, u32[]{:S(2)}, u32[]{:S(2)}) collective-permute-start(bf16[256,640]{1,0:T(8,128)(2,1)S(1)} %get-tuple-element.86), channel_id=1, source_target_pairs={{0,1},{1,0},{2,3},{3,2},{4,5},{5,4},{6,7},{7,6},{8,9},{9,8},{10,11... | collective-permute-start | bytes 983048 | tf_op jit(solution)/shard_map/ppermute | solution.py:37
  88.5 2.2 %collective-permute-start.28 = (bf16[512,640]{1,0:T(8,128)(2,1)S(1)}, bf16[512,640]{1,0:T(8,128)(2,1)S(1)}, u32[]{:S(2)}, u32[]{:S(2)}) collective-permute-start(bf16[512,640]{1,0:T(8,128)(2,1)S(1)} %get-tuple-element.89), channel_id=1, source_target_pairs={{0,2},{2,0},{4,6},{6,4},{8,10},{10,8},{12,14},{14,12},{16,18},{18,... | collective-permute-start | bytes 1966088 | tf_op jit(solution)/shard_map/ppermute | solution.py:37
  89.1 7.7 %collective-permute-start.22 = (bf16[256,384]{1,0:T(8,128)(2,1)S(1)}, bf16[256,384]{1,0:T(8,128)(2,1)S(1)}, u32[]{:S(2)}, u32[]{:S(2)}) collective-permute-start(bf16[256,384]{1,0:T(8,128)(2,1)S(1)} %second_away.1), channel_id=1, source_target_pairs={{0,1},{1,0},{2,3},{3,2},{4,5},{5,4},{6,7},{7,6},{8,9},{9,8},{10,11... | collective-permute-start | bytes 589832 | tf_op jit(solution)/shard_map/ppermute | solution.py:37
  90.8 10.5 %collective-permute-start.29 = (bf16[256,640]{1,0:T(8,128)(2,1)S(1)}, bf16[256,640]{1,0:T(8,128)(2,1)S(1)}, u32[]{:S(2)}, u32[]{:S(2)}) collective-permute-start(bf16[256,640]{1,0:T(8,128)(2,1)S(1)} %get-tuple-element.91), channel_id=1, source_target_pairs={{0,4},{2,6},{4,0},{6,2},{8,12},{10,14},{12,8},{14,10},{16,20},{18,... | collective-permute-start | bytes 983048 | tf_op jit(solution)/shard_map/ppermute | solution.py:37
  92.4 4.4 %collective-permute-start.23 = (f32[16,256]{1,0:T(8,128)S(1)}, f32[16,256]{1,0:T(8,128)S(1)}, u32[]{:S(2)}, u32[]{:S(2)}) collective-permute-start(f32[16,256]{1,0:T(8,128)S(1)} %get-tuple-element.76.refs_0_), channel_id=1, source_target_pairs={{0,1},{1,0},{2,3},{3,2},{4,5},{5,4},{6,7},{7,6},{8,9},{9,8},{10,11... | collective-permute-start | bytes 49160 | tf_op jit(solution)/shard_map/ppermute | solution.py:37
  99.8 7.0 %collective-permute-start.24 = (bf16[256,384]{1,0:T(8,128)(2,1)S(1)}, bf16[256,384]{1,0:T(8,128)(2,1)S(1)}, u32[]{:S(2)}, u32[]{:S(2)}) collective-permute-start(bf16[256,384]{1,0:T(8,128)(2,1)S(1)} %get-tuple-element.80), channel_id=1, source_target_pairs={{0,4},{2,6},{4,0},{6,2},{8,12},{10,14},{12,8},{14,10},{16,20},{18,... | collective-permute-start | bytes 589832 | tf_op jit(solution)/shard_map/ppermute | solution.py:37
  101.4 28.1 %copy-start.1 = (f32[64,1024]{1,0:T(8,128)S(1)}, f32[64,1024]{1,0:T(8,128)}, u32[]{:S(2)}) copy-start(f32[64,1024]{1,0:T(8,128)} %refs_5_.1) | copy-start | bytes 786436
  101.4 28.1 %copy-start.4 = (f32[64,1024]{1,0:T(8,128)S(1)}, f32[64,1024]{1,0:T(8,128)}, u32[]{:S(2)}) copy-start(f32[64,1024]{1,0:T(8,128)} %refs_6_.1) | copy-start | bytes 786436
  101.4 28.1 %copy-start.5 = (f32[64,1024]{1,0:T(8,128)S(1)}, f32[64,1024]{1,0:T(8,128)}, u32[]{:S(2)}) copy-start(f32[64,1024]{1,0:T(8,128)} %refs_7_.1) | copy-start | bytes 786436
  101.4 28.1 %copy-start.6 = (f32[256,16]{0,1:T(8,128)S(1)}, f32[256,16]{0,1:T(8,128)}, u32[]{:S(2)}) copy-start(f32[256,16]{0,1:T(8,128)} %param.26) | copy-start | bytes 49156
  101.4 28.1 %copy-start.7 = (f32[256,16]{0,1:T(8,128)S(1)}, f32[256,16]{0,1:T(8,128)}, u32[]{:S(2)}) copy-start(f32[256,16]{0,1:T(8,128)} %param.27) | copy-start | bytes 49156
  101.5 6.0 %collective-permute-start.30 = (bf16[128,640]{1,0:T(8,128)(2,1)S(1)}, bf16[128,640]{1,0:T(8,128)(2,1)S(1)}, u32[]{:S(2)}, u32[]{:S(2)}) collective-permute-start(bf16[128,640]{1,0:T(8,128)(2,1)S(1)} %get-tuple-element.93), channel_id=1, source_target_pairs={{0,8},{2,10},{4,12},{6,14},{8,0},{10,2},{12,4},{14,6},{16,24},{18,... | collective-permute-start | bytes 491528 | tf_op jit(solution)/shard_map/ppermute | solution.py:37
  106.9 5.4 %collective-permute-start.25 = (bf16[128,384]{1,0:T(8,128)(2,1)S(1)}, bf16[128,384]{1,0:T(8,128)(2,1)S(1)}, u32[]{:S(2)}, u32[]{:S(2)}) collective-permute-start(bf16[128,384]{1,0:T(8,128)(2,1)S(1)} %get-tuple-element.82), channel_id=1, source_target_pairs={{0,8},{2,10},{4,12},{6,14},{8,0},{10,2},{12,4},{14,6},{16,24},{18,... | collective-permute-start | bytes 294920 | tf_op jit(solution)/shard_map/ppermute | solution.py:37
  107.5 6.1 %collective-permute-start.31 = (bf16[64,640]{1,0:T(8,128)(2,1)S(1)}, bf16[64,640]{1,0:T(8,128)(2,1)S(1)}, u32[]{:S(2)}, u32[]{:S(2)}) collective-permute-start(bf16[64,640]{1,0:T(8,128)(2,1)S(1)} %get-tuple-element.95), channel_id=1, source_target_pairs={{0,16},{2,18},{4,20},{6,22},{8,24},{10,26},{12,28},{14,30},{16,0},... | collective-permute-start | bytes 245768 | tf_op jit(solution)/shard_map/ppermute | solution.py:37
  112.2 5.3 %collective-permute-start.26 = (bf16[64,384]{1,0:T(8,128)(2,1)S(1)}, bf16[64,384]{1,0:T(8,128)(2,1)S(1)}, u32[]{:S(2)}, u32[]{:S(2)}) collective-permute-start(bf16[64,384]{1,0:T(8,128)(2,1)S(1)} %get-tuple-element.84), channel_id=1, source_target_pairs={{0,16},{2,18},{4,20},{6,22},{8,24},{10,26},{12,28},{14,30},{16,0},... | collective-permute-start | bytes 147464 | tf_op jit(solution)/shard_map/ppermute | solution.py:37

commit v6 on v5

--- a/solution.py
+++ b/solution.py
@@ -346,7 +346,6 @@
         wide = ((points, n_low), F32)
         held = lax.all_gather(partly[0], "core", axis=0, tiled=True)
         hidden, damp = call("hidden", hidden_units, units[0], masked, held)
-        partly[1] = after(partly[1], hidden)
         far = swap(hidden, "feat", n_feat, 1)
         (pre,) = call(
             "first_pre", first_pre, [wide], hidden, far, frequencies, phases, weight=BIAS_A

time: 131 us -> 131 us (level)
  no operation moved by 1% of the time
where the time goes in v6:
time: 131 us
  waiting for transfers between devices  61.5 us (47%)
  starting transfers between devices  39.1 us (30%)
  blocking collectives  16.7 us (13%)
  Pallas kernels  11.1 us (8%)
    ppermute x32, waiting for transfers between devices, swap(): return lax.ppermute(x, axis, [(i, i ^ mask) for i in range(size)])  61.5 us
    ppermute x32, starting transfers between devices, swap(): return lax.ppermute(x, axis, [(i, i ^ mask) for i in range(size)])  39.1 us
    all_to_all x1, blocking collectives, on_device(): spread = lax.all_to_all(spread, (*BLK, 'feat'), 0, 0, tiled=True)  11.8 us
    pallas_call x22, Pallas kernels, call(): pl.pallas_call(body, out_shape=[shapes(shape, dtype) for shape, dtype in...  11.1 us
  transfers between devices with their start and end apart: 32, of which 26 were waited for; matrix products, arithmetic and copies ran while one was open for 0% of the time, Pallas kernels for 4%

profile of v6, /device:TPU:0, one launch (start us, length us, event | category | flops | bytes accessed | tf_op | source)
XLA Modules:
  0.0 130.7 jit_solution(13020937489524278010)
XLA Ops:
  0.7 1.0 convert_element_type.3
  1.7 4.1 %collective-permute-start = (bf16[64,384]{1,0:T(8,128)(2,1)S(1)}, bf16[64,384]{1,0:T(8,128)(2,1)S(1)}, u32[]{:S(2)}, u32[]{:S(2)}) collective-permute-start(bf16[64,384]{1,0:T(8,128)(2,1)S(1)} %slice.8), channel_id=1, source_target_pairs={{0,16},{2,18},{4,20},{6,22},{8,24},{10,26},{12,28},{14,30},{16,0},... | collective-permute-start | bytes 147464 | tf_op jit(solution)/shard_map/ppermute | solution.py:37
  5.9 2.5 %collective-permute-done = bf16[64,384]{1,0:T(8,128)(2,1)S(1)} collective-permute-done((bf16[64,384]{1,0:T(8,128)(2,1)S(1)}, bf16[64,384]{1,0:T(8,128)(2,1)S(1)}, u32[]{:S(2)}, u32[]{:S(2)}) %collective-permute-start) | collective-permute-done | bytes 49184 | tf_op jit(solution)/shard_map/ppermute | solution.py:37
  8.5 2.8 %collective-permute-start.1 = (bf16[128,384]{1,0:T(8,128)(2,1)S(1)}, bf16[128,384]{1,0:T(8,128)(2,1)S(1)}, u32[]{:S(2)}, u32[]{:S(2)}) collective-permute-start(bf16[128,384]{1,0:T(8,128)(2,1)S(1)} %pad_maximum_fusion.5), channel_id=1, source_target_pairs={{0,8},{2,10},{4,12},{6,14},{8,0},{10,2},{12,4},{14,6},{16,24},{18,... | collective-permute-start | bytes 294920 | tf_op jit(solution)/shard_map/ppermute | solution.py:37
  11.3 1.6 %collective-permute-done.4 = bf16[64,640]{1,0:T(8,128)(2,1)S(1)} collective-permute-done((bf16[64,640]{1,0:T(8,128)(2,1)S(1)}, bf16[64,640]{1,0:T(8,128)(2,1)S(1)}, u32[]{:S(2)}, u32[]{:S(2)}) %collective-permute-start.4) | collective-permute-done | bytes 81952 | tf_op jit(solution)/shard_map/ppermute | solution.py:37
  13.0 2.0 %collective-permute-done.1 = bf16[128,384]{1,0:T(8,128)(2,1)S(1)} collective-permute-done((bf16[128,384]{1,0:T(8,128)(2,1)S(1)}, bf16[128,384]{1,0:T(8,128)(2,1)S(1)}, u32[]{:S(2)}, u32[]{:S(2)}) %collective-permute-start.1) | collective-permute-done | bytes 98336 | tf_op jit(solution)/shard_map/ppermute | solution.py:37
  15.0 1.6 %collective-permute-start.2 = (bf16[256,384]{1,0:T(8,128)(2,1)S(1)}, bf16[256,384]{1,0:T(8,128)(2,1)S(1)}, u32[]{:S(2)}, u32[]{:S(2)}) collective-permute-start(bf16[256,384]{1,0:T(8,128)(2,1)S(1)} %pad_maximum_fusion.3), channel_id=1, source_target_pairs={{0,4},{2,6},{4,0},{6,2},{8,12},{10,14},{12,8},{14,10},{16,20},{18,... | collective-permute-start | bytes 589832 | tf_op jit(solution)/shard_map/ppermute | solution.py:37
  16.6 1.0 prepare.1.masked
  18.3 1.6 %collective-permute-start.6 = (bf16[256,640]{1,0:T(8,128)(2,1)S(1)}, bf16[256,640]{1,0:T(8,128)(2,1)S(1)}, u32[]{:S(2)}, u32[]{:S(2)}) collective-permute-start(bf16[256,640]{1,0:T(8,128)(2,1)S(1)} %pad_maximum_fusion.2), channel_id=1, source_target_pairs={{0,4},{2,6},{4,0},{6,2},{8,12},{10,14},{12,8},{14,10},{16,20},{18,... | collective-permute-start | bytes 983048 | tf_op jit(solution)/shard_map/ppermute | solution.py:37
  19.9 3.0 %collective-permute-done.2 = bf16[256,384]{1,0:T(8,128)(2,1)S(1)} collective-permute-done((bf16[256,384]{1,0:T(8,128)(2,1)S(1)}, bf16[256,384]{1,0:T(8,128)(2,1)S(1)}, u32[]{:S(2)}, u32[]{:S(2)}) %collective-permute-start.2) | collective-permute-done | bytes 196640 | tf_op jit(solution)/shard_map/ppermute | solution.py:37
  22.9 2.5 %all_gather.6.refs_0_ = bf16[1024,384]{1,0:T(8,128)(2,1)S(1)} all-gather(bf16[512,384]{1,0:T(8,128)(2,1)S(1)} %pad_maximum_fusion.1), channel_id=1, replica_groups=mesh['hi'=8,'core'=2,'feat'=2] {'core'}, dimensions={0}, use_global_device_ids=true | all-gather | bytes 1179648 | tf_op jit(solution)/shard_map/all_gather | solution.py:347
  25.8 1.6 %collective-permute-start.3 = (bf16[256,384]{1,0:T(8,128)(2,1)S(1)}, bf16[256,384]{1,0:T(8,128)(2,1)S(1)}, u32[]{:S(2)}, u32[]{:S(2)}) collective-permute-start(bf16[256,384]{1,0:T(8,128)(2,1)S(1)} %get-tuple-element.59.hidden), channel_id=1, source_target_pairs={{0,1},{1,0},{2,3},{3,2},{4,5},{5,4},{6,7},{7,6},{8,9},{9,8},{10,11... | collective-permute-start | bytes 589832 | tf_op jit(solution)/shard_map/ppermute | solution.py:37
  27.4 1.0 collective-permute-done.6
  28.5 4.3 %collective-permute-done.3.far = bf16[256,384]{1,0:T(8,128)(2,1)S(1)} collective-permute-done((bf16[256,384]{1,0:T(8,128)(2,1)S(1)}, bf16[256,384]{1,0:T(8,128)(2,1)S(1)}, u32[]{:S(2)}, u32[]{:S(2)}) %collective-permute-start.3) | collective-permute-done | bytes 196640 | tf_op jit(solution)/shard_map/ppermute | solution.py:37
  34.2 1.6 %collective-permute-start.8 = (bf16[256,640]{1,0:T(8,128)(2,1)S(1)}, bf16[256,640]{1,0:T(8,128)(2,1)S(1)}, u32[]{:S(2)}, u32[]{:S(2)}) collective-permute-start(bf16[256,640]{1,0:T(8,128)(2,1)S(1)} %get-tuple-element.60.hidden), channel_id=1, source_target_pairs={{0,1},{1,0},{2,3},{3,2},{4,5},{5,4},{6,7},{7,6},{8,9},{9,8},{10,11... | collective-permute-start | bytes 983048 | tf_op jit(solution)/shard_map/ppermute | solution.py:37
  36.4 6.8 %collective-permute-done.8.far = bf16[256,640]{1,0:T(8,128)(2,1)S(1)} collective-permute-done((bf16[256,640]{1,0:T(8,128)(2,1)S(1)}, bf16[256,640]{1,0:T(8,128)(2,1)S(1)}, u32[]{:S(2)}, u32[]{:S(2)}) %collective-permute-start.8) | collective-permute-done | bytes 327712 | tf_op jit(solution)/shard_map/ppermute | solution.py:37
  43.2 2.1 %features.1 = (bf16[256,1024]{1,0:T(8,128)(2,1)S(1)}, f32[256,1024]{1,0:T(8,128)S(1)}, f32[8,1152]{1,0:T(8,128)S(1)}, f32[8,1152]{1,0:T(8,128)S(1)}) custom-call(f32[256,1024]{1,0:T(8,128)S(1)} %second_pre.1.pre, bf16[256,640]{1,0:T(8,128)(2,1)S(1)} %collective-permute-done.8.far, bf16[2048,1024]{1,0:T(8,128)(2,1)S(1)} %copy-done, f32[16,256]{1,0:T(8,128)S(1)} %bitcast.14, ...), custom_call_target="tpu_custom_call" | custom-call | flops 1 | bytes 1 | tf_op jit(solution)/shard_map/features/pallas_call | solution.py:82
  45.3 1.2 collective-permute-done.9
  47.1 1.1 collective-permute-start.10
  48.1 1.9 %collective-permute-start.11 = (f32[8,1152]{1,0:T(8,128)S(1)}, f32[8,1152]{1,0:T(8,128)S(1)}, u32[]{:S(2)}, u32[]{:S(2)}) collective-permute-start(f32[8,1152]{1,0:T(8,128)S(1)} %add.30), channel_id=1, source_target_pairs={{0,8},{2,10},{4,12},{6,14},{8,0},{10,2},{12,4},{14,6},{16,24},{18,... | collective-permute-start | bytes 110600 | tf_op jit(solution)/shard_map/ppermute | solution.py:37
  50.0 1.4 %collective-permute-done.12 = f32[8,1152]{1,0:T(8,128)S(1)} collective-permute-done((f32[8,1152]{1,0:T(8,128)S(1)}, f32[8,1152]{1,0:T(8,128)S(1)}, u32[]{:S(2)}, u32[]{:S(2)}) %collective-permute-start.12) | collective-permute-done | bytes 36896 | tf_op jit(solution)/shard_map/ppermute | solution.py:37
  52.1 2.9 %collective-permute-start.13 = (f32[8,1152]{1,0:T(8,128)S(1)}, f32[8,1152]{1,0:T(8,128)S(1)}, u32[]{:S(2)}, u32[]{:S(2)}) collective-permute-start(f32[8,1152]{1,0:T(8,128)S(1)} %add_add_fusion.1), channel_id=1, source_target_pairs={{0,16},{2,18},{4,20},{6,22},{8,24},{10,26},{12,28},{14,30},{16,0},... | collective-permute-start | bytes 110600 | tf_op jit(solution)/shard_map/ppermute | solution.py:37
  55.0 2.0 %collective-permute-done.13 = f32[8,1152]{1,0:T(8,128)S(1)} collective-permute-done((f32[8,1152]{1,0:T(8,128)S(1)}, f32[8,1152]{1,0:T(8,128)S(1)}, u32[]{:S(2)}, u32[]{:S(2)}) %collective-permute-start.13) | collective-permute-done | bytes 36896 | tf_op jit(solution)/shard_map/ppermute | solution.py:37
  57.0 1.2 collective-permute-done.14.other
  58.5 1.6 %collective-permute-start.15 = (f32[16,256]{1,0:T(8,128)S(1)}, f32[16,256]{1,0:T(8,128)S(1)}, u32[]{:S(2)}, u32[]{:S(2)}) collective-permute-start(f32[16,256]{1,0:T(8,128)S(1)} %get-tuple-element.64.near), channel_id=1, source_target_pairs={{0,1},{1,0},{2,3},{3,2},{4,5},{5,4},{6,7},{7,6},{8,9},{9,8},{10,11... | collective-permute-start | bytes 49160 | tf_op jit(solution)/shard_map/ppermute | solution.py:37
  60.0 2.2 %collective-permute-done.15.far = f32[16,256]{1,0:T(8,128)S(1)} collective-permute-done((f32[16,256]{1,0:T(8,128)S(1)}, f32[16,256]{1,0:T(8,128)S(1)}, u32[]{:S(2)}, u32[]{:S(2)}) %collective-permute-start.15) | collective-permute-done | bytes 16416 | tf_op jit(solution)/shard_map/ppermute | solution.py:37
  62.5 1.2 collective-permute-done.16
  63.7 2.9 %collective-permute-start.19 = (f32[8,1152]{1,0:T(8,128)S(1)}, f32[8,1152]{1,0:T(8,128)S(1)}, u32[]{:S(2)}, u32[]{:S(2)}) collective-permute-start(f32[8,1152]{1,0:T(8,128)S(1)} %add.35), channel_id=1, source_target_pairs={{0,12},{2,14},{4,8},{6,10},{8,4},{10,6},{12,0},{14,2},{16,28},{18,... | collective-permute-start | bytes 110600 | tf_op jit(solution)/shard_map/ppermute | solution.py:37
  67.2 1.4 %collective-permute-done.19 = f32[8,1152]{1,0:T(8,128)S(1)} collective-permute-done((f32[8,1152]{1,0:T(8,128)S(1)}, f32[8,1152]{1,0:T(8,128)S(1)}, u32[]{:S(2)}, u32[]{:S(2)}) %collective-permute-start.19) | collective-permute-done | bytes 36896 | tf_op jit(solution)/shard_map/ppermute | solution.py:37
  68.6 2.0 %collective-permute-done.17 = f32[8,1152]{1,0:T(8,128)S(1)} collective-permute-done((f32[8,1152]{1,0:T(8,128)S(1)}, f32[8,1152]{1,0:T(8,128)S(1)}, u32[]{:S(2)}, u32[]{:S(2)}) %collective-permute-start.17) | collective-permute-done | bytes 36896 | tf_op jit(solution)/shard_map/ppermute | solution.py:37
  71.1 1.7 %collective-permute-start.20 = (f32[8,1152]{1,0:T(8,128)S(1)}, f32[8,1152]{1,0:T(8,128)S(1)}, u32[]{:S(2)}, u32[]{:S(2)}) collective-permute-start(f32[8,1152]{1,0:T(8,128)S(1)} %add_add_fusion), channel_id=1, source_target_pairs={{0,16},{2,18},{4,20},{6,22},{8,24},{10,26},{12,28},{14,30},{16,0},... | collective-permute-start | bytes 110600 | tf_op jit(solution)/shard_map/ppermute | solution.py:37
  72.8 3.2 %collective-permute-done.20 = f32[8,1152]{1,0:T(8,128)S(1)} collective-permute-done((f32[8,1152]{1,0:T(8,128)S(1)}, f32[8,1152]{1,0:T(8,128)S(1)}, u32[]{:S(2)}, u32[]{:S(2)}) %collective-permute-start.20) | collective-permute-done | bytes 36896 | tf_op jit(solution)/shard_map/ppermute | solution.py:37
  76.0 1.2 collective-permute-done.21.other
  78.1 1.6 %collective-permute-start.27 = (bf16[256,640]{1,0:T(8,128)(2,1)S(1)}, bf16[256,640]{1,0:T(8,128)(2,1)S(1)}, u32[]{:S(2)}, u32[]{:S(2)}) collective-permute-start(bf16[256,640]{1,0:T(8,128)(2,1)S(1)} %get-tuple-element.84), channel_id=1, source_target_pairs={{0,1},{1,0},{2,3},{3,2},{4,5},{5,4},{6,7},{7,6},{8,9},{9,8},{10,11... | collective-permute-start | bytes 983048 | tf_op jit(solution)/shard_map/ppermute | solution.py:37
  80.5 7.4 %collective-permute-done.27.got = bf16[256,640]{1,0:T(8,128)(2,1)S(1)} collective-permute-done((bf16[256,640]{1,0:T(8,128)(2,1)S(1)}, bf16[256,640]{1,0:T(8,128)(2,1)S(1)}, u32[]{:S(2)}, u32[]{:S(2)}) %collective-permute-start.27) | collective-permute-done | bytes 327712 | tf_op jit(solution)/shard_map/ppermute | solution.py:37
  89.1 1.6 %collective-permute-start.22 = (bf16[256,384]{1,0:T(8,128)(2,1)S(1)}, bf16[256,384]{1,0:T(8,128)(2,1)S(1)}, u32[]{:S(2)}, u32[]{:S(2)}) collective-permute-start(bf16[256,384]{1,0:T(8,128)(2,1)S(1)} %second_away.1), channel_id=1, source_target_pairs={{0,1},{1,0},{2,3},{3,2},{4,5},{5,4},{6,7},{7,6},{8,9},{9,8},{10,11... | collective-permute-start | bytes 589832 | tf_op jit(solution)/shard_map/ppermute | solution.py:37
  90.8 1.6 %collective-permute-start.29 = (bf16[256,640]{1,0:T(8,128)(2,1)S(1)}, bf16[256,640]{1,0:T(8,128)(2,1)S(1)}, u32[]{:S(2)}, u32[]{:S(2)}) collective-permute-start(bf16[256,640]{1,0:T(8,128)(2,1)S(1)} %get-tuple-element.89), channel_id=1, source_target_pairs={{0,4},{2,6},{4,0},{6,2},{8,12},{10,14},{12,8},{14,10},{16,20},{18,... | collective-permute-start | bytes 983048 | tf_op jit(solution)/shard_map/ppermute | solution.py:37
  92.4 1.5 %collective-permute-start.23 = (f32[16,256]{1,0:T(8,128)S(1)}, f32[16,256]{1,0:T(8,128)S(1)}, u32[]{:S(2)}, u32[]{:S(2)}) collective-permute-start(f32[16,256]{1,0:T(8,128)S(1)} %get-tuple-element.74.refs_0_), channel_id=1, source_target_pairs={{0,1},{1,0},{2,3},{3,2},{4,5},{5,4},{6,7},{7,6},{8,9},{9,8},{10,11... | collective-permute-start | bytes 49160 | tf_op jit(solution)/shard_map/ppermute | solution.py:37
  93.9 2.9 %collective-permute-done.23.refs_1_ = f32[16,256]{1,0:T(8,128)S(1)} collective-permute-done((f32[16,256]{1,0:T(8,128)S(1)}, f32[16,256]{1,0:T(8,128)S(1)}, u32[]{:S(2)}, u32[]{:S(2)}) %collective-permute-start.23) | collective-permute-done | bytes 16416 | tf_op jit(solution)/shard_map/ppermute | solution.py:37
  97.3 2.4 %all_gather.7.got = bf16[1024,384]{1,0:T(8,128)(2,1)S(1)} all-gather(bf16[512,384]{1,0:T(8,128)(2,1)S(1)} %get-tuple-element.76), channel_id=1, replica_groups=mesh['hi'=8,'core'=2,'feat'=2] {'core'}, dimensions={0}, use_global_device_ids=true | all-gather | bytes 1179648 | tf_op jit(solution)/shard_map/all_gather | solution.py:427
  99.8 1.6 %collective-permute-start.24 = (bf16[256,384]{1,0:T(8,128)(2,1)S(1)}, bf16[256,384]{1,0:T(8,128)(2,1)S(1)}, u32[]{:S(2)}, u32[]{:S(2)}) collective-permute-start(bf16[256,384]{1,0:T(8,128)(2,1)S(1)} %get-tuple-element.78), channel_id=1, source_target_pairs={{0,4},{2,6},{4,0},{6,2},{8,12},{10,14},{12,8},{14,10},{16,20},{18,... | collective-permute-start | bytes 589832 | tf_op jit(solution)/shard_map/ppermute | solution.py:37
  101.6 5.2 %collective-permute-done.24.got = bf16[256,384]{1,0:T(8,128)(2,1)S(1)} collective-permute-done((bf16[256,384]{1,0:T(8,128)(2,1)S(1)}, bf16[256,384]{1,0:T(8,128)(2,1)S(1)}, u32[]{:S(2)}, u32[]{:S(2)}) %collective-permute-start.24) | collective-permute-done | bytes 196640 | tf_op jit(solution)/shard_map/ppermute | solution.py:37
  107.5 2.8 %collective-permute-start.31 = (bf16[64,640]{1,0:T(8,128)(2,1)S(1)}, bf16[64,640]{1,0:T(8,128)(2,1)S(1)}, u32[]{:S(2)}, u32[]{:S(2)}) collective-permute-start(bf16[64,640]{1,0:T(8,128)(2,1)S(1)} %get-tuple-element.93), channel_id=1, source_target_pairs={{0,16},{2,18},{4,20},{6,22},{8,24},{10,26},{12,28},{14,30},{16,0},... | collective-permute-start | bytes 245768 | tf_op jit(solution)/shard_map/ppermute | solution.py:37
  110.4 1.8 %collective-permute-done.25.got = bf16[128,384]{1,0:T(8,128)(2,1)S(1)} collective-permute-done((bf16[128,384]{1,0:T(8,128)(2,1)S(1)}, bf16[128,384]{1,0:T(8,128)(2,1)S(1)}, u32[]{:S(2)}, u32[]{:S(2)}) %collective-permute-start.25) | collective-permute-done | bytes 98336 | tf_op jit(solution)/shard_map/ppermute | solution.py:37
  112.2 1.4 %collective-permute-start.26 = (bf16[64,384]{1,0:T(8,128)(2,1)S(1)}, bf16[64,384]{1,0:T(8,128)(2,1)S(1)}, u32[]{:S(2)}, u32[]{:S(2)}) collective-permute-start(bf16[64,384]{1,0:T(8,128)(2,1)S(1)} %get-tuple-element.82), channel_id=1, source_target_pairs={{0,16},{2,18},{4,20},{6,22},{8,24},{10,26},{12,28},{14,30},{16,0},... | collective-permute-start | bytes 147464 | tf_op jit(solution)/shard_map/ppermute | solution.py:37
  113.8 3.7 %collective-permute-done.26.got = bf16[64,384]{1,0:T(8,128)(2,1)S(1)} collective-permute-done((bf16[64,384]{1,0:T(8,128)(2,1)S(1)}, bf16[64,384]{1,0:T(8,128)(2,1)S(1)}, u32[]{:S(2)}, u32[]{:S(2)}) %collective-permute-start.26) | collective-permute-done | bytes 49184 | tf_op jit(solution)/shard_map/ppermute | solution.py:37
  117.7 11.8 %all_to_all.5.refs_0_ = f32[32,1,128]{2,1,0:T(1,128)S(1)} all-to-all(f32[32,1,128]{2,1,0:T(1,128)S(1)} %get-tuple-element.95), channel_id=1, replica_groups=mesh['hi'=8,'core'=2,'feat'=2] {'hi','core','feat'}, dimensions={0} | all-to-all | bytes 32768 | tf_op jit(solution)/shard_map/all_to_all | solution.py:448
  129.5 1.2 update.1
  (84 shorter events, 11.3 us)
Async XLA Ops:
  0.6 15.9 %copy-start.2 = (bf16[256,1024]{1,0:T(8,128)(2,1)S(1)}, bf16[256,1024]{1,0:T(8,128)(2,1)}, u32[]{:S(2)}) copy-start(bf16[256,1024]{1,0:T(8,128)(2,1)} %inputs.1) | copy-start | bytes 1572868
  0.7 15.9 %copy-start.11 = (s32[256]{0:T(256)S(1)}, s32[256]{0:T(256)}, u32[]{:S(2)}) copy-start(s32[256]{0:T(256)} %param.17) | copy-start | bytes 3076
  0.7 15.9 %copy-start.9 = (s32[2,1024]{1,0:T(2,128)S(1)}, s32[2,1024]{1,0:T(2,128)}, u32[]{:S(2)}) copy-start(s32[2,1024]{1,0:T(2,128)} %col_mask.1) | copy-start | bytes 24580
  1.7 6.7 %collective-permute-start = (bf16[64,384]{1,0:T(8,128)(2,1)S(1)}, bf16[64,384]{1,0:T(8,128)(2,1)S(1)}, u32[]{:S(2)}, u32[]{:S(2)}) collective-permute-start(bf16[64,384]{1,0:T(8,128)(2,1)S(1)} %slice.8), channel_id=1, source_target_pairs={{0,16},{2,18},{4,20},{6,22},{8,24},{10,26},{12,28},{14,30},{16,0},... | collective-permute-start | bytes 147464 | tf_op jit(solution)/shard_map/ppermute | solution.py:37
  5.9 7.0 %collective-permute-start.4 = (bf16[64,640]{1,0:T(8,128)(2,1)S(1)}, bf16[64,640]{1,0:T(8,128)(2,1)S(1)}, u32[]{:S(2)}, u32[]{:S(2)}) collective-permute-start(bf16[64,640]{1,0:T(8,128)(2,1)S(1)} %slice.9), channel_id=1, source_target_pairs={{0,16},{2,18},{4,20},{6,22},{8,24},{10,26},{12,28},{14,30},{16,0},... | collective-permute-start | bytes 245768 | tf_op jit(solution)/shard_map/ppermute | solution.py:37
  8.5 6.5 %collective-permute-start.1 = (bf16[128,384]{1,0:T(8,128)(2,1)S(1)}, bf16[128,384]{1,0:T(8,128)(2,1)S(1)}, u32[]{:S(2)}, u32[]{:S(2)}) collective-permute-start(bf16[128,384]{1,0:T(8,128)(2,1)S(1)} %pad_maximum_fusion.5), channel_id=1, source_target_pairs={{0,8},{2,10},{4,12},{6,14},{8,0},{10,2},{12,4},{14,6},{16,24},{18,... | collective-permute-start | bytes 294920 | tf_op jit(solution)/shard_map/ppermute | solution.py:37
  12.9 5.4 %collective-permute-start.5 = (bf16[128,640]{1,0:T(8,128)(2,1)S(1)}, bf16[128,640]{1,0:T(8,128)(2,1)S(1)}, u32[]{:S(2)}, u32[]{:S(2)}) collective-permute-start(bf16[128,640]{1,0:T(8,128)(2,1)S(1)} %pad_maximum_fusion.4), channel_id=1, source_target_pairs={{0,8},{2,10},{4,12},{6,14},{8,0},{10,2},{12,4},{14,6},{16,24},{18,... | collective-permute-start | bytes 491528 | tf_op jit(solution)/shard_map/ppermute | solution.py:37
  15.0 7.8 %collective-permute-start.2 = (bf16[256,384]{1,0:T(8,128)(2,1)S(1)}, bf16[256,384]{1,0:T(8,128)(2,1)S(1)}, u32[]{:S(2)}, u32[]{:S(2)}) collective-permute-start(bf16[256,384]{1,0:T(8,128)(2,1)S(1)} %pad_maximum_fusion.3), channel_id=1, source_target_pairs={{0,4},{2,6},{4,0},{6,2},{8,12},{10,14},{12,8},{14,10},{16,20},{18,... | collective-permute-start | bytes 589832 | tf_op jit(solution)/shard_map/ppermute | solution.py:37
  18.3 10.1 %collective-permute-start.6 = (bf16[256,640]{1,0:T(8,128)(2,1)S(1)}, bf16[256,640]{1,0:T(8,128)(2,1)S(1)}, u32[]{:S(2)}, u32[]{:S(2)}) collective-permute-start(bf16[256,640]{1,0:T(8,128)(2,1)S(1)} %pad_maximum_fusion.2), channel_id=1, source_target_pairs={{0,4},{2,6},{4,0},{6,2},{8,12},{10,14},{12,8},{14,10},{16,20},{18,... | collective-permute-start | bytes 983048 | tf_op jit(solution)/shard_map/ppermute | solution.py:37
  22.8 10.0 %copy-start = (bf16[2048,1024]{1,0:T(8,128)(2,1)S(1)}, bf16[2048,1024]{1,0:T(8,128)(2,1)}, u32[]{:S(2)}) copy-start(bf16[2048,1024]{1,0:T(8,128)(2,1)} %freq.11) | copy-start | bytes 12582916
  25.4 7.5 %copy-start.13 = (f32[1024]{0:T(1024)S(1)}, f32[1024]{0:T(1024)}, u32[]{:S(2)}) copy-start(f32[1024]{0:T(1024)} %param.19) | copy-start | bytes 12292
  25.8 7.0 %collective-permute-start.3 = (bf16[256,384]{1,0:T(8,128)(2,1)S(1)}, bf16[256,384]{1,0:T(8,128)(2,1)S(1)}, u32[]{:S(2)}, u32[]{:S(2)}) collective-permute-start(bf16[256,384]{1,0:T(8,128)(2,1)S(1)} %get-tuple-element.59.hidden), channel_id=1, source_target_pairs={{0,1},{1,0},{2,3},{3,2},{4,5},{5,4},{6,7},{7,6},{8,9},{9,8},{10,11... | collective-permute-start | bytes 589832 | tf_op jit(solution)/shard_map/ppermute | solution.py:37
  28.4 5.1 %collective-permute-start.7 = (bf16[512,640]{1,0:T(8,128)(2,1)S(1)}, bf16[512,640]{1,0:T(8,128)(2,1)S(1)}, u32[]{:S(2)}, u32[]{:S(2)}) collective-permute-start(bf16[512,640]{1,0:T(8,128)(2,1)S(1)} %pad_maximum_fusion.refs_0_), channel_id=1, source_target_pairs={{0,2},{2,0},{4,6},{6,4},{8,10},{10,8},{12,14},{14,12},{16,18},{18,... | collective-permute-start | bytes 1966088 | tf_op jit(solution)/shard_map/ppermute | solution.py:37
  34.2 9.0 %copy-start.3 = (f32[256,16]{0,1:T(8,128)S(1)}, f32[256,16]{0,1:T(8,128)}, u32[]{:S(2)}) copy-start(f32[256,16]{0,1:T(8,128)} %param.25) | copy-start | bytes 49156
  34.2 9.0 %copy-start.10 = (s32[256]{0:T(256)S(1)}, s32[256]{0:T(256)}, u32[]{:S(2)}) copy-start(s32[256]{0:T(256)} %param.16) | copy-start | bytes 3076
  34.2 9.0 %collective-permute-start.8 = (bf16[256,640]{1,0:T(8,128)(2,1)S(1)}, bf16[256,640]{1,0:T(8,128)(2,1)S(1)}, u32[]{:S(2)}, u32[]{:S(2)}) collective-permute-start(bf16[256,640]{1,0:T(8,128)(2,1)S(1)} %get-tuple-element.60.hidden), channel_id=1, source_target_pairs={{0,1},{1,0},{2,3},{3,2},{4,5},{5,4},{6,7},{7,6},{8,9},{9,8},{10,11... | collective-permute-start | bytes 983048 | tf_op jit(solution)/shard_map/ppermute | solution.py:37
  43.2 19.1 %copy-start.8 = (f32[256,16]{0,1:T(8,128)S(1)}, f32[256,16]{0,1:T(8,128)}, u32[]{:S(2)}) copy-start(f32[256,16]{0,1:T(8,128)} %param.21) | copy-start | bytes 49156
  43.2 19.1 %copy-start.12 = (f32[256]{0:T(256)S(1)}, f32[256]{0:T(256)}, u32[]{:S(2)}) copy-start(f32[256]{0:T(256)} %param.20) | copy-start | bytes 3076
  45.3 1.3 collective-permute-start.9
  46.5 4.9 %collective-permute-start.12 = (f32[8,1152]{1,0:T(8,128)S(1)}, f32[8,1152]{1,0:T(8,128)S(1)}, u32[]{:S(2)}, u32[]{:S(2)}) collective-permute-start(f32[8,1152]{1,0:T(8,128)S(1)} %add.30), channel_id=1, source_target_pairs={{0,12},{2,14},{4,8},{6,10},{8,4},{10,6},{12,0},{14,2},{16,28},{18,... | collective-permute-start | bytes 110600 | tf_op jit(solution)/shard_map/ppermute | solution.py:37
  47.1 4.4 %collective-permute-start.10 = (f32[8,1152]{1,0:T(8,128)S(1)}, f32[8,1152]{1,0:T(8,128)S(1)}, u32[]{:S(2)}, u32[]{:S(2)}) collective-permute-start(f32[8,1152]{1,0:T(8,128)S(1)} %add.30), channel_id=1, source_target_pairs={{0,4},{2,6},{4,0},{6,2},{8,12},{10,14},{12,8},{14,10},{16,20},{18,... | collective-permute-start | bytes 110600 | tf_op jit(solution)/shard_map/ppermute | solution.py:37
  48.1 4.0 %collective-permute-start.11 = (f32[8,1152]{1,0:T(8,128)S(1)}, f32[8,1152]{1,0:T(8,128)S(1)}, u32[]{:S(2)}, u32[]{:S(2)}) collective-permute-start(f32[8,1152]{1,0:T(8,128)S(1)} %add.30), channel_id=1, source_target_pairs={{0,8},{2,10},{4,12},{6,14},{8,0},{10,2},{12,4},{14,6},{16,24},{18,... | collective-permute-start | bytes 110600 | tf_op jit(solution)/shard_map/ppermute | solution.py:37
  52.1 4.9 %collective-permute-start.13 = (f32[8,1152]{1,0:T(8,128)S(1)}, f32[8,1152]{1,0:T(8,128)S(1)}, u32[]{:S(2)}, u32[]{:S(2)}) collective-permute-start(f32[8,1152]{1,0:T(8,128)S(1)} %add_add_fusion.1), channel_id=1, source_target_pairs={{0,16},{2,18},{4,20},{6,22},{8,24},{10,26},{12,28},{14,30},{16,0},... | collective-permute-start | bytes 110600 | tf_op jit(solution)/shard_map/ppermute | solution.py:37
  57.0 1.2 collective-permute-start.14
  58.5 3.8 %collective-permute-start.15 = (f32[16,256]{1,0:T(8,128)S(1)}, f32[16,256]{1,0:T(8,128)S(1)}, u32[]{:S(2)}, u32[]{:S(2)}) collective-permute-start(f32[16,256]{1,0:T(8,128)S(1)} %get-tuple-element.64.near), channel_id=1, source_target_pairs={{0,1},{1,0},{2,3},{3,2},{4,5},{5,4},{6,7},{7,6},{8,9},{9,8},{10,11... | collective-permute-start | bytes 49160 | tf_op jit(solution)/shard_map/ppermute | solution.py:37
  62.5 1.2 collective-permute-start.16
  63.7 4.9 %collective-permute-start.19 = (f32[8,1152]{1,0:T(8,128)S(1)}, f32[8,1152]{1,0:T(8,128)S(1)}, u32[]{:S(2)}, u32[]{:S(2)}) collective-permute-start(f32[8,1152]{1,0:T(8,128)S(1)} %add.35), channel_id=1, source_target_pairs={{0,12},{2,14},{4,8},{6,10},{8,4},{10,6},{12,0},{14,2},{16,28},{18,... | collective-permute-start | bytes 110600 | tf_op jit(solution)/shard_map/ppermute | solution.py:37
  66.6 4.0 %collective-permute-start.17 = (f32[8,1152]{1,0:T(8,128)S(1)}, f32[8,1152]{1,0:T(8,128)S(1)}, u32[]{:S(2)}, u32[]{:S(2)}) collective-permute-start(f32[8,1152]{1,0:T(8,128)S(1)} %add.35), channel_id=1, source_target_pairs={{0,4},{2,6},{4,0},{6,2},{8,12},{10,14},{12,8},{14,10},{16,20},{18,... | collective-permute-start | bytes 110600 | tf_op jit(solution)/shard_map/ppermute | solution.py:37
  67.1 4.0 %collective-permute-start.18 = (f32[8,1152]{1,0:T(8,128)S(1)}, f32[8,1152]{1,0:T(8,128)S(1)}, u32[]{:S(2)}, u32[]{:S(2)}) collective-permute-start(f32[8,1152]{1,0:T(8,128)S(1)} %add.35), channel_id=1, source_target_pairs={{0,8},{2,10},{4,12},{6,14},{8,0},{10,2},{12,4},{14,6},{16,24},{18,... | collective-permute-start | bytes 110600 | tf_op jit(solution)/shard_map/ppermute | solution.py:37
  71.1 4.9 %collective-permute-start.20 = (f32[8,1152]{1,0:T(8,128)S(1)}, f32[8,1152]{1,0:T(8,128)S(1)}, u32[]{:S(2)}, u32[]{:S(2)}) collective-permute-start(f32[8,1152]{1,0:T(8,128)S(1)} %add_add_fusion), channel_id=1, source_target_pairs={{0,16},{2,18},{4,20},{6,22},{8,24},{10,26},{12,28},{14,30},{16,0},... | collective-permute-start | bytes 110600 | tf_op jit(solution)/shard_map/ppermute | solution.py:37
  76.0 1.2 collective-permute-start.21
  78.1 9.8 %collective-permute-start.27 = (bf16[256,640]{1,0:T(8,128)(2,1)S(1)}, bf16[256,640]{1,0:T(8,128)(2,1)S(1)}, u32[]{:S(2)}, u32[]{:S(2)}) collective-permute-start(bf16[256,640]{1,0:T(8,128)(2,1)S(1)} %get-tuple-element.84), channel_id=1, source_target_pairs={{0,1},{1,0},{2,3},{3,2},{4,5},{5,4},{6,7},{7,6},{8,9},{9,8},{10,11... | collective-permute-start | bytes 983048 | tf_op jit(solution)/shard_map/ppermute | solution.py:37
  88.5 2.2 %collective-permute-start.28 = (bf16[512,640]{1,0:T(8,128)(2,1)S(1)}, bf16[512,640]{1,0:T(8,128)(2,1)S(1)}, u32[]{:S(2)}, u32[]{:S(2)}) collective-permute-start(bf16[512,640]{1,0:T(8,128)(2,1)S(1)} %get-tuple-element.87), channel_id=1, source_target_pairs={{0,2},{2,0},{4,6},{6,4},{8,10},{10,8},{12,14},{14,12},{16,18},{18,... | collective-permute-start | bytes 1966088 | tf_op jit(solution)/shard_map/ppermute | solution.py:37
  89.1 7.7 %collective-permute-start.22 = (bf16[256,384]{1,0:T(8,128)(2,1)S(1)}, bf16[256,384]{1,0:T(8,128)(2,1)S(1)}, u32[]{:S(2)}, u32[]{:S(2)}) collective-permute-start(bf16[256,384]{1,0:T(8,128)(2,1)S(1)} %second_away.1), channel_id=1, source_target_pairs={{0,1},{1,0},{2,3},{3,2},{4,5},{5,4},{6,7},{7,6},{8,9},{9,8},{10,11... | collective-permute-start | bytes 589832 | tf_op jit(solution)/shard_map/ppermute | solution.py:37
  90.8 10.5 %collective-permute-start.29 = (bf16[256,640]{1,0:T(8,128)(2,1)S(1)}, bf16[256,640]{1,0:T(8,128)(2,1)S(1)}, u32[]{:S(2)}, u32[]{:S(2)}) collective-permute-start(bf16[256,640]{1,0:T(8,128)(2,1)S(1)} %get-tuple-element.89), channel_id=1, source_target_pairs={{0,4},{2,6},{4,0},{6,2},{8,12},{10,14},{12,8},{14,10},{16,20},{18,... | collective-permute-start | bytes 983048 | tf_op jit(solution)/shard_map/ppermute | solution.py:37
  92.4 4.4 %collective-permute-start.23 = (f32[16,256]{1,0:T(8,128)S(1)}, f32[16,256]{1,0:T(8,128)S(1)}, u32[]{:S(2)}, u32[]{:S(2)}) collective-permute-start(f32[16,256]{1,0:T(8,128)S(1)} %get-tuple-element.74.refs_0_), channel_id=1, source_target_pairs={{0,1},{1,0},{2,3},{3,2},{4,5},{5,4},{6,7},{7,6},{8,9},{9,8},{10,11... | collective-permute-start | bytes 49160 | tf_op jit(solution)/shard_map/ppermute | solution.py:37
  99.8 7.0 %collective-permute-start.24 = (bf16[256,384]{1,0:T(8,128)(2,1)S(1)}, bf16[256,384]{1,0:T(8,128)(2,1)S(1)}, u32[]{:S(2)}, u32[]{:S(2)}) collective-permute-start(bf16[256,384]{1,0:T(8,128)(2,1)S(1)} %get-tuple-element.78), channel_id=1, source_target_pairs={{0,4},{2,6},{4,0},{6,2},{8,12},{10,14},{12,8},{14,10},{16,20},{18,... | collective-permute-start | bytes 589832 | tf_op jit(solution)/shard_map/ppermute | solution.py:37
  101.4 28.1 %copy-start.1 = (f32[64,1024]{1,0:T(8,128)S(1)}, f32[64,1024]{1,0:T(8,128)}, u32[]{:S(2)}) copy-start(f32[64,1024]{1,0:T(8,128)} %refs_5_.1) | copy-start | bytes 786436
  101.4 28.1 %copy-start.4 = (f32[64,1024]{1,0:T(8,128)S(1)}, f32[64,1024]{1,0:T(8,128)}, u32[]{:S(2)}) copy-start(f32[64,1024]{1,0:T(8,128)} %refs_6_.1) | copy-start | bytes 786436
  101.4 28.1 %copy-start.5 = (f32[64,1024]{1,0:T(8,128)S(1)}, f32[64,1024]{1,0:T(8,128)}, u32[]{:S(2)}) copy-start(f32[64,1024]{1,0:T(8,128)} %refs_7_.1) | copy-start | bytes 786436
  101.4 28.1 %copy-start.6 = (f32[256,16]{0,1:T(8,128)S(1)}, f32[256,16]{0,1:T(8,128)}, u32[]{:S(2)}) copy-start(f32[256,16]{0,1:T(8,128)} %param.26) | copy-start | bytes 49156
  101.4 28.1 %copy-start.7 = (f32[256,16]{0,1:T(8,128)S(1)}, f32[256,16]{0,1:T(8,128)}, u32[]{:S(2)}) copy-start(f32[256,16]{0,1:T(8,128)} %param.27) | copy-start | bytes 49156
  101.5 6.0 %collective-permute-start.30 = (bf16[128,640]{1,0:T(8,128)(2,1)S(1)}, bf16[128,640]{1,0:T(8,128)(2,1)S(1)}, u32[]{:S(2)}, u32[]{:S(2)}) collective-permute-start(bf16[128,640]{1,0:T(8,128)(2,1)S(1)} %get-tuple-element.91), channel_id=1, source_target_pairs={{0,8},{2,10},{4,12},{6,14},{8,0},{10,2},{12,4},{14,6},{16,24},{18,... | collective-permute-start | bytes 491528 | tf_op jit(solution)/shard_map/ppermute | solution.py:37
  106.9 5.4 %collective-permute-start.25 = (bf16[128,384]{1,0:T(8,128)(2,1)S(1)}, bf16[128,384]{1,0:T(8,128)(2,1)S(1)}, u32[]{:S(2)}, u32[]{:S(2)}) collective-permute-start(bf16[128,384]{1,0:T(8,128)(2,1)S(1)} %get-tuple-element.80), channel_id=1, source_target_pairs={{0,8},{2,10},{4,12},{6,14},{8,0},{10,2},{12,4},{14,6},{16,24},{18,... | collective-permute-start | bytes 294920 | tf_op jit(solution)/shard_map/ppermute | solution.py:37
  107.5 6.1 %collective-permute-start.31 = (bf16[64,640]{1,0:T(8,128)(2,1)S(1)}, bf16[64,640]{1,0:T(8,128)(2,1)S(1)}, u32[]{:S(2)}, u32[]{:S(2)}) collective-permute-start(bf16[64,640]{1,0:T(8,128)(2,1)S(1)} %get-tuple-element.93), channel_id=1, source_target_pairs={{0,16},{2,18},{4,20},{6,22},{8,24},{10,26},{12,28},{14,30},{16,0},... | collective-permute-start | bytes 245768 | tf_op jit(solution)/shard_map/ppermute | solution.py:37
  112.2 5.3 %collective-permute-start.26 = (bf16[64,384]{1,0:T(8,128)(2,1)S(1)}, bf16[64,384]{1,0:T(8,128)(2,1)S(1)}, u32[]{:S(2)}, u32[]{:S(2)}) collective-permute-start(bf16[64,384]{1,0:T(8,128)(2,1)S(1)} %get-tuple-element.82), channel_id=1, source_target_pairs={{0,16},{2,18},{4,20},{6,22},{8,24},{10,26},{12,28},{14,30},{16,0},... | collective-permute-start | bytes 147464 | tf_op jit(solution)/shard_map/ppermute | solution.py:37
